TPU v7x, 256 devices: a whole 4x4x8 slice. The times are simulated.
256 devices in a mesh: row: 16 (over z, core), col: 16 (over x, y).
Axes of the slice: x: 4, y: 4, z: 8, core: 2. Of those that a mesh axis runs over, the one named last changes fastest.
Arguments:
- targets: float32 [3, 131072], P(None, 'row'), may hold values from 0 to 1, as said below
- sources: float32 [3, 32768], P(None, 'col'), may hold values from 0 to 1, as said below
- samples: bfloat16 [32768, 128], P('col', 'row'), may hold values from -0.03125 to 0.03125
- near: int32 [256, 8], P('row'), may hold values from -1 to 63, as said below
Outputs:
- leaf_bases: float32 [131072, 128], P(('row', 'col'))
- nested: float32 [131072, 128], P(('row', 'col'))
Inputs may be any that keep to these rules, and one draw needn't show every extreme that they name: `near`: in each row, entries after the first -1 are -1 and the first entry is a source leaf; a row may name a source leaf twice. `targets`: the points of one leaf lie about a common centre. `sources`: the points of one leaf lie about a common centre.
All inputs are finite; a program needn't handle non-finite values.
Results may differ from a plain program's by a relative error of at most 0.0071.
Values may be sent and summed in bfloat16 or wider, within the bound.
No kernel may reach another device: no remote copies, remote signals or barrier semaphores. Data moves between devices by JAX's collectives and lax.ppermute only.
A program may use at most 64 MiB of HBM per device.

v0:
```python
import jax
import jax.numpy as jnp
from jax import lax
from jax.sharding import Mesh
from jax.sharding import PartitionSpec as P

LEAF = 512
ROW = ("row_0", "row_1")
ROW_COL = ("row_0", "row_1", "col")


corr_length = 0.1
ridge = 0.1


def gathered_by_axis(x, axes, dim):
    if not axes:
        return x
    nearer = lax.all_gather(x, axes[-1], axis=dim, tiled=True)
    return gathered_by_axis(nearer, axes[:-1], dim)


def split_up(x, dim, size):
    before, after = (x.shape[:dim], x.shape[dim + 1 :])
    return jnp.moveaxis(x.reshape(*before, size, -1, *after), dim, 0)


def sent_and_summed(x, axis, dim):
    size = lax.axis_size(axis)
    parts = lax.all_to_all(split_up(x, dim, size), axis, 0, 0, tiled=True)
    return jnp.sum(parts, axis=0)


def partner(x, axis, apart):
    return lax.ppermute(x, axis, [(i, i ^ 1 << apart) for i in range(lax.axis_size(axis))])


def kernel_block(points, others):
    dist_sq = (points[0][:, None] - others[0][None, :]) ** 2
    dist_sq = dist_sq + (points[1][:, None] - others[1][None, :]) ** 2
    dist_sq = dist_sq + (points[2][:, None] - others[2][None, :]) ** 2
    return jnp.exp(-jnp.sqrt(dist_sq) / corr_length)


def basis(stacked):
    row_count = stacked.shape[0]
    rank_width = stacked.shape[1]
    gram_matrix = jnp.matmul(stacked.T, stacked, precision=lax.Precision.HIGHEST) / row_count
    ridge_term = ridge * jnp.trace(gram_matrix) / rank_width
    factor = jnp.linalg.cholesky(
        gram_matrix + ridge_term * jnp.eye(rank_width, dtype=gram_matrix.dtype)
    )
    bases = lax.linalg.triangular_solve(
        factor, stacked, left_side=False, lower=True, transpose_a=True
    )
    projected = jnp.matmul(bases.T, stacked, precision=lax.Precision.HIGHEST) / row_count
    return (bases, projected)


def ordered_pair(mine, other, side_bit):
    lower_part = jnp.where(side_bit == 0, mine, other)
    upper_part = jnp.where(side_bit == 0, other, mine)
    return jnp.concatenate([lower_part, upper_part], axis=0)


def per_device(targets, sources, samples, near):
    sample_cols = gathered_by_axis(samples, ROW, 1)
    rank_width = sample_cols.shape[1]
    col_width = sources.shape[1]
    row_width = targets.shape[1]
    col_index = lax.axis_index("col")
    col_leaves = col_width // LEAF
    local_ids = col_index * col_leaves + jnp.arange(col_leaves)
    near_hits = jnp.any(near[:, :, None] == local_ids[None, None, :], axis=1)
    keep_mask = jnp.where(near_hits, 0.0, 1.0).astype(jnp.float32)
    col_mask = jnp.broadcast_to(
        keep_mask[:, :, None], (keep_mask.shape[0], col_leaves, LEAF)
    ).reshape(keep_mask.shape[0], col_width)

    def leaf_term(inputs):
        points, mask_row = inputs
        kernel_tile = (kernel_block(points, sources) * mask_row[None, :]).astype(jnp.bfloat16)
        return jnp.dot(kernel_tile, sample_cols, preferred_element_type=jnp.float32)

    leaf_count = row_width // LEAF
    points = targets
    points = points.reshape(3, leaf_count, LEAF).transpose(1, 0, 2)
    products = lax.map(leaf_term, (points, col_mask))
    far_sample = sent_and_summed(products.reshape(row_width, rank_width), "col", 0)
    leaf_basis, proj_zero = basis(far_sample)
    first_bit = col_index % 2
    second_bit = col_index // 2 % 2
    sibling = partner(proj_zero, "col", 0)
    upper_one, proj_one = basis(ordered_pair(proj_zero, sibling, first_bit))
    cousin = partner(proj_one, "col", 1)
    upper_two, unused = basis(ordered_pair(proj_one, cousin, second_bit))
    own_one = lax.dynamic_slice_in_dim(upper_one, first_bit * rank_width, rank_width, 0)
    own_two = lax.dynamic_slice_in_dim(upper_two, second_bit * rank_width, rank_width, 0)
    first_product = jnp.matmul(leaf_basis, own_one, precision=lax.Precision.HIGHEST)
    nested = jnp.matmul(first_product, own_two, precision=lax.Precision.HIGHEST) / rank_width
    return (leaf_basis, nested)


def solution(mesh):
    torus = Mesh(mesh.devices.reshape(8, 2, mesh.shape["col"]), ("row_0", "row_1", "col"))
    placed = (P(None, ROW), P(None, "col"), P("col", ROW), P(ROW, None))
    return jax.shard_map(
        per_device,
        mesh=torus,
        in_specs=placed,
        out_specs=(P(ROW_COL, None), P(ROW_COL, None)),
        check_vma=False,
    )
```

profile of v0, /device:TPU:8, one launch (start us, length us, event | category | flops | bytes accessed | tf_op | source)
XLA Modules:
  0.0 263.3 jit_solution(10834530927861442496)
XLA Ops:
  1.7 2.1 all_gather.6
  3.7 28.9 %all_gather.7 = bf16[2048,128]{0,1:T(8,128)(2,1)S(1)} all-gather(bf16[2048,16]{0,1:T(8,128)(2,1)S(1)} %all_gather.6), channel_id=1, replica_groups=mesh['row_0'=8,'row_1'=2,'col'=16] {'row_0'}, dimensions={1}, use_global_device_ids=true | all-gather | bytes 589824 | tf_op jit(solution)/shard_map/all_gather | solution.py:19
  32.9 88.3 %while.10 = (s32[]{:T(128)}, f32[16,512,128]{2,1,0:T(8,128)}, f32[16,3,512]{2,1,0:T(4,128)}, f32[3,2048]{1,0:T(4,128)}, f32[16,2048]{1,0:T(8,128)S(1)}, /*index=...) while((s32[]{:T(128)}, f32[16,512,128]{2,1,0:T(8,128)}, f32[16,3,512]{2,1,0:T(4,128)}, ...), condition=%wide.region_2.3_spmd, body=%wide.region_1.2_spmd.sunk | while | flops 281018368 | bytes 903321 | solution.py:88
  34.6 3.8 %fusion.51 = f32[16,512,128]{2,1,0:T(8,128)} fusion(f32[16,512,128]{2,1,0:T(8,128)} %get-tuple-element.140, s32[]{:T(128)S(6)} %copy.54, bf16[2048,128]{1,0:T(8,128)(2,1)S(1)} %get-tuple-element.154, f32[2048]{0:T(1024)S(1)} %bitcast.79, f32[2048]{0:T(1024)S(1)} %bitcast.77, f32[512]{0:T(512)S(1)} %bitcast.82, f32[2048]{0:T(1024)S(1)} %bitcast.78, ...), kind=kOutput, calls=%fused_computation.3.clone.1 | convolution fusion | flops 281018368 | bytes 825348 | tf_op jit(solution)/shard_map/while/body/eval_jaxpr/dot_general | solution.py:83
  40.2 3.8 %fusion.51 = f32[16,512,128]{2,1,0:T(8,128)} fusion(f32[16,512,128]{2,1,0:T(8,128)} %get-tuple-element.140, s32[]{:T(128)S(6)} %copy.54, bf16[2048,128]{1,0:T(8,128)(2,1)S(1)} %get-tuple-element.154, f32[2048]{0:T(1024)S(1)} %bitcast.79, f32[2048]{0:T(1024)S(1)} %bitcast.77, f32[512]{0:T(512)S(1)} %bitcast.82, f32[2048]{0:T(1024)S(1)} %bitcast.78, ...), kind=kOutput, calls=%fused_computation.3.clone.1 | convolution fusion | flops 281018368 | bytes 825348 | tf_op jit(solution)/shard_map/while/body/eval_jaxpr/dot_general | solution.py:83
  45.7 3.8 %fusion.51 = f32[16,512,128]{2,1,0:T(8,128)} fusion(f32[16,512,128]{2,1,0:T(8,128)} %get-tuple-element.140, s32[]{:T(128)S(6)} %copy.54, bf16[2048,128]{1,0:T(8,128)(2,1)S(1)} %get-tuple-element.154, f32[2048]{0:T(1024)S(1)} %bitcast.79, f32[2048]{0:T(1024)S(1)} %bitcast.77, f32[512]{0:T(512)S(1)} %bitcast.82, f32[2048]{0:T(1024)S(1)} %bitcast.78, ...), kind=kOutput, calls=%fused_computation.3.clone.1 | convolution fusion | flops 281018368 | bytes 825348 | tf_op jit(solution)/shard_map/while/body/eval_jaxpr/dot_general | solution.py:83
  51.2 3.8 %fusion.51 = f32[16,512,128]{2,1,0:T(8,128)} fusion(f32[16,512,128]{2,1,0:T(8,128)} %get-tuple-element.140, s32[]{:T(128)S(6)} %copy.54, bf16[2048,128]{1,0:T(8,128)(2,1)S(1)} %get-tuple-element.154, f32[2048]{0:T(1024)S(1)} %bitcast.79, f32[2048]{0:T(1024)S(1)} %bitcast.77, f32[512]{0:T(512)S(1)} %bitcast.82, f32[2048]{0:T(1024)S(1)} %bitcast.78, ...), kind=kOutput, calls=%fused_computation.3.clone.1 | convolution fusion | flops 281018368 | bytes 825348 | tf_op jit(solution)/shard_map/while/body/eval_jaxpr/dot_general | solution.py:83
  56.7 3.8 %fusion.51 = f32[16,512,128]{2,1,0:T(8,128)} fusion(f32[16,512,128]{2,1,0:T(8,128)} %get-tuple-element.140, s32[]{:T(128)S(6)} %copy.54, bf16[2048,128]{1,0:T(8,128)(2,1)S(1)} %get-tuple-element.154, f32[2048]{0:T(1024)S(1)} %bitcast.79, f32[2048]{0:T(1024)S(1)} %bitcast.77, f32[512]{0:T(512)S(1)} %bitcast.82, f32[2048]{0:T(1024)S(1)} %bitcast.78, ...), kind=kOutput, calls=%fused_computation.3.clone.1 | convolution fusion | flops 281018368 | bytes 825348 | tf_op jit(solution)/shard_map/while/body/eval_jaxpr/dot_general | solution.py:83
  62.2 3.8 %fusion.51 = f32[16,512,128]{2,1,0:T(8,128)} fusion(f32[16,512,128]{2,1,0:T(8,128)} %get-tuple-element.140, s32[]{:T(128)S(6)} %copy.54, bf16[2048,128]{1,0:T(8,128)(2,1)S(1)} %get-tuple-element.154, f32[2048]{0:T(1024)S(1)} %bitcast.79, f32[2048]{0:T(1024)S(1)} %bitcast.77, f32[512]{0:T(512)S(1)} %bitcast.82, f32[2048]{0:T(1024)S(1)} %bitcast.78, ...), kind=kOutput, calls=%fused_computation.3.clone.1 | convolution fusion | flops 281018368 | bytes 825348 | tf_op jit(solution)/shard_map/while/body/eval_jaxpr/dot_general | solution.py:83
  67.7 3.8 %fusion.51 = f32[16,512,128]{2,1,0:T(8,128)} fusion(f32[16,512,128]{2,1,0:T(8,128)} %get-tuple-element.140, s32[]{:T(128)S(6)} %copy.54, bf16[2048,128]{1,0:T(8,128)(2,1)S(1)} %get-tuple-element.154, f32[2048]{0:T(1024)S(1)} %bitcast.79, f32[2048]{0:T(1024)S(1)} %bitcast.77, f32[512]{0:T(512)S(1)} %bitcast.82, f32[2048]{0:T(1024)S(1)} %bitcast.78, ...), kind=kOutput, calls=%fused_computation.3.clone.1 | convolution fusion | flops 281018368 | bytes 825348 | tf_op jit(solution)/shard_map/while/body/eval_jaxpr/dot_general | solution.py:83
  73.3 3.8 %fusion.51 = f32[16,512,128]{2,1,0:T(8,128)} fusion(f32[16,512,128]{2,1,0:T(8,128)} %get-tuple-element.140, s32[]{:T(128)S(6)} %copy.54, bf16[2048,128]{1,0:T(8,128)(2,1)S(1)} %get-tuple-element.154, f32[2048]{0:T(1024)S(1)} %bitcast.79, f32[2048]{0:T(1024)S(1)} %bitcast.77, f32[512]{0:T(512)S(1)} %bitcast.82, f32[2048]{0:T(1024)S(1)} %bitcast.78, ...), kind=kOutput, calls=%fused_computation.3.clone.1 | convolution fusion | flops 281018368 | bytes 825348 | tf_op jit(solution)/shard_map/while/body/eval_jaxpr/dot_general | solution.py:83
  78.8 3.8 %fusion.51 = f32[16,512,128]{2,1,0:T(8,128)} fusion(f32[16,512,128]{2,1,0:T(8,128)} %get-tuple-element.140, s32[]{:T(128)S(6)} %copy.54, bf16[2048,128]{1,0:T(8,128)(2,1)S(1)} %get-tuple-element.154, f32[2048]{0:T(1024)S(1)} %bitcast.79, f32[2048]{0:T(1024)S(1)} %bitcast.77, f32[512]{0:T(512)S(1)} %bitcast.82, f32[2048]{0:T(1024)S(1)} %bitcast.78, ...), kind=kOutput, calls=%fused_computation.3.clone.1 | convolution fusion | flops 281018368 | bytes 825348 | tf_op jit(solution)/shard_map/while/body/eval_jaxpr/dot_general | solution.py:83
  84.3 3.8 %fusion.51 = f32[16,512,128]{2,1,0:T(8,128)} fusion(f32[16,512,128]{2,1,0:T(8,128)} %get-tuple-element.140, s32[]{:T(128)S(6)} %copy.54, bf16[2048,128]{1,0:T(8,128)(2,1)S(1)} %get-tuple-element.154, f32[2048]{0:T(1024)S(1)} %bitcast.79, f32[2048]{0:T(1024)S(1)} %bitcast.77, f32[512]{0:T(512)S(1)} %bitcast.82, f32[2048]{0:T(1024)S(1)} %bitcast.78, ...), kind=kOutput, calls=%fused_computation.3.clone.1 | convolution fusion | flops 281018368 | bytes 825348 | tf_op jit(solution)/shard_map/while/body/eval_jaxpr/dot_general | solution.py:83
  89.8 3.8 %fusion.51 = f32[16,512,128]{2,1,0:T(8,128)} fusion(f32[16,512,128]{2,1,0:T(8,128)} %get-tuple-element.140, s32[]{:T(128)S(6)} %copy.54, bf16[2048,128]{1,0:T(8,128)(2,1)S(1)} %get-tuple-element.154, f32[2048]{0:T(1024)S(1)} %bitcast.79, f32[2048]{0:T(1024)S(1)} %bitcast.77, f32[512]{0:T(512)S(1)} %bitcast.82, f32[2048]{0:T(1024)S(1)} %bitcast.78, ...), kind=kOutput, calls=%fused_computation.3.clone.1 | convolution fusion | flops 281018368 | bytes 825348 | tf_op jit(solution)/shard_map/while/body/eval_jaxpr/dot_general | solution.py:83
  95.3 3.8 %fusion.51 = f32[16,512,128]{2,1,0:T(8,128)} fusion(f32[16,512,128]{2,1,0:T(8,128)} %get-tuple-element.140, s32[]{:T(128)S(6)} %copy.54, bf16[2048,128]{1,0:T(8,128)(2,1)S(1)} %get-tuple-element.154, f32[2048]{0:T(1024)S(1)} %bitcast.79, f32[2048]{0:T(1024)S(1)} %bitcast.77, f32[512]{0:T(512)S(1)} %bitcast.82, f32[2048]{0:T(1024)S(1)} %bitcast.78, ...), kind=kOutput, calls=%fused_computation.3.clone.1 | convolution fusion | flops 281018368 | bytes 825348 | tf_op jit(solution)/shard_map/while/body/eval_jaxpr/dot_general | solution.py:83
  100.8 3.8 %fusion.51 = f32[16,512,128]{2,1,0:T(8,128)} fusion(f32[16,512,128]{2,1,0:T(8,128)} %get-tuple-element.140, s32[]{:T(128)S(6)} %copy.54, bf16[2048,128]{1,0:T(8,128)(2,1)S(1)} %get-tuple-element.154, f32[2048]{0:T(1024)S(1)} %bitcast.79, f32[2048]{0:T(1024)S(1)} %bitcast.77, f32[512]{0:T(512)S(1)} %bitcast.82, f32[2048]{0:T(1024)S(1)} %bitcast.78, ...), kind=kOutput, calls=%fused_computation.3.clone.1 | convolution fusion | flops 281018368 | bytes 825348 | tf_op jit(solution)/shard_map/while/body/eval_jaxpr/dot_general | solution.py:83
  106.3 3.8 %fusion.51 = f32[16,512,128]{2,1,0:T(8,128)} fusion(f32[16,512,128]{2,1,0:T(8,128)} %get-tuple-element.140, s32[]{:T(128)S(6)} %copy.54, bf16[2048,128]{1,0:T(8,128)(2,1)S(1)} %get-tuple-element.154, f32[2048]{0:T(1024)S(1)} %bitcast.79, f32[2048]{0:T(1024)S(1)} %bitcast.77, f32[512]{0:T(512)S(1)} %bitcast.82, f32[2048]{0:T(1024)S(1)} %bitcast.78, ...), kind=kOutput, calls=%fused_computation.3.clone.1 | convolution fusion | flops 281018368 | bytes 825348 | tf_op jit(solution)/shard_map/while/body/eval_jaxpr/dot_general | solution.py:83
  111.9 3.8 %fusion.51 = f32[16,512,128]{2,1,0:T(8,128)} fusion(f32[16,512,128]{2,1,0:T(8,128)} %get-tuple-element.140, s32[]{:T(128)S(6)} %copy.54, bf16[2048,128]{1,0:T(8,128)(2,1)S(1)} %get-tuple-element.154, f32[2048]{0:T(1024)S(1)} %bitcast.79, f32[2048]{0:T(1024)S(1)} %bitcast.77, f32[512]{0:T(512)S(1)} %bitcast.82, f32[2048]{0:T(1024)S(1)} %bitcast.78, ...), kind=kOutput, calls=%fused_computation.3.clone.1 | convolution fusion | flops 281018368 | bytes 825348 | tf_op jit(solution)/shard_map/while/body/eval_jaxpr/dot_general | solution.py:83
  117.4 3.8 %fusion.51 = f32[16,512,128]{2,1,0:T(8,128)} fusion(f32[16,512,128]{2,1,0:T(8,128)} %get-tuple-element.140, s32[]{:T(128)S(6)} %copy.54, bf16[2048,128]{1,0:T(8,128)(2,1)S(1)} %get-tuple-element.154, f32[2048]{0:T(1024)S(1)} %bitcast.79, f32[2048]{0:T(1024)S(1)} %bitcast.77, f32[512]{0:T(512)S(1)} %bitcast.82, f32[2048]{0:T(1024)S(1)} %bitcast.78, ...), kind=kOutput, calls=%fused_computation.3.clone.1 | convolution fusion | flops 281018368 | bytes 825348 | tf_op jit(solution)/shard_map/while/body/eval_jaxpr/dot_general | solution.py:83
  121.2 51.8 %all_to_all.5 = f32[16,512,128]{2,1,0:T(8,128)} all-to-all(f32[16,512,128]{2,1,0:T(8,128)} %get-tuple-element.36), channel_id=1, replica_groups=mesh['row_0'=8,'row_1'=2,'col'=16] {'col'}, dimensions={0} | all-to-all | bytes 8388608 | tf_op jit(solution)/shard_map/all_to_all | solution.py:30
  173.0 2.4 reduce_sum.27
  175.4 1.2 fusion.20
  177.4 11.7 %cholesky.59 = f32[128,128]{1,0:T(8,128)S(1)} custom-call(f32[128,128]{1,0:T(8,128)S(1)} %fusion.13), custom_call_target="Cholesky" | custom-call | tf_op jit(solution)/shard_map/jit(cholesky)/cholesky | solution.py:50
  190.7 9.8 %custom-call.8 = f32[1,128,128]{1,2,0:T(8,128)S(1)} custom-call(f32[1,128,128]{2,1,0:T(8,128)S(1)} %copy.38), custom_call_target="InvertDiagBlocksLowerTriangular" | custom-call | tf_op jit(solution)/shard_map/triangular_solve | solution.py:53
  201.5 1.7 collective-permute-start
  203.3 2.8 %collective-permute-done = f32[128,128]{0,1:T(8,128)S(1)} collective-permute-done((f32[128,128]{0,1:T(8,128)S(1)}, f32[128,128]{0,1:T(8,128)S(1)}, u32[]{:S(2)}, u32[]{:S(2)}) %collective-permute-start) | collective-permute-done | bytes 65568 | tf_op jit(solution)/shard_map/ppermute | solution.py:35
  207.8 11.7 %cholesky.70 = f32[128,128]{1,0:T(8,128)S(1)} custom-call(f32[128,128]{1,0:T(8,128)S(1)} %fusion.10), custom_call_target="Cholesky" | custom-call | tf_op jit(solution)/shard_map/jit(cholesky)/cholesky | solution.py:50
  220.8 9.8 %custom-call.10 = f32[1,128,128]{1,2,0:T(8,128)S(1)} custom-call(f32[1,128,128]{2,1,0:T(8,128)S(1)} %fusion.5), custom_call_target="InvertDiagBlocksLowerTriangular" | custom-call | tf_op jit(solution)/shard_map/triangular_solve/custom-call.2 | solution.py:53
  231.2 1.2 collective-permute-start.1
  232.8 4.5 %collective-permute-done.1 = f32[128,128]{0,1:T(8,128)S(1)} collective-permute-done((f32[128,128]{0,1:T(8,128)S(1)}, f32[128,128]{0,1:T(8,128)S(1)}, u32[]{:S(2)}, u32[]{:S(2)}) %collective-permute-start.1) | collective-permute-done | bytes 65568 | tf_op jit(solution)/shard_map/ppermute | solution.py:35
  239.0 11.7 %cholesky.81 = f32[128,128]{1,0:T(8,128)S(1)} custom-call(f32[128,128]{1,0:T(8,128)S(1)} %fusion.8), custom_call_target="Cholesky" | custom-call | tf_op jit(solution)/shard_map/jit(cholesky)/cholesky | solution.py:50
  252.1 9.8 %custom-call.11 = f32[1,128,128]{1,2,0:T(8,128)S(1)} custom-call(f32[1,128,128]{2,1,0:T(8,128)S(1)} %fusion.6), custom_call_target="InvertDiagBlocksLowerTriangular" | custom-call | tf_op jit(solution)/shard_map/triangular_solve/custom-call.2 | solution.py:53
  (73 shorter events, 38.6 us)
Async XLA Ops:
  200.9 62.4 %copy-start = (f32[512,128]{1,0:T(8,128)}, f32[512,128]{1,0:T(8,128)S(1)}, u32[]{:S(2)}) copy-start(f32[512,128]{1,0:T(8,128)S(1)} %fusion.11) | copy-start | bytes 786436
  201.5 4.5 %collective-permute-start = (f32[128,128]{0,1:T(8,128)S(1)}, f32[128,128]{0,1:T(8,128)S(1)}, u32[]{:S(2)}, u32[]{:S(2)}) collective-permute-start(f32[128,128]{0,1:T(8,128)S(1)} %convolution_multiply_fusion.4), channel_id=1, source_target_pairs={{0,1},{1,0},{2,3},{3,2},{4,5},{5,4},{6,7},{7,6},{8,9},{9,8},{10,11... | collective-permute-start | bytes 196616 | tf_op jit(solution)/shard_map/ppermute | solution.py:35
  231.2 6.1 %collective-permute-start.1 = (f32[128,128]{0,1:T(8,128)S(1)}, f32[128,128]{0,1:T(8,128)S(1)}, u32[]{:S(2)}, u32[]{:S(2)}) collective-permute-start(f32[128,128]{0,1:T(8,128)S(1)} %convolution_multiply_fusion.2), channel_id=1, source_target_pairs={{0,2},{1,3},{2,0},{3,1},{4,6},{5,7},{6,4},{7,5},{8,10},{9,11},{10,... | collective-permute-start | bytes 196616 | tf_op jit(solution)/shard_map/ppermute | solution.py:35
where the time goes:
time: 266 us; the launch traced here: 263 us
  blocking collectives  82.8 us (31%)
  other arithmetic  72 us (27%)
  matrix products  66.9 us (25%)
  local copies, waits for them, and re-layouts  28.5 us (11%)
  waiting for transfers between devices  7.33 us (3%)
  starting transfers between devices  2.89 us (1%)
  between operations  2.83 us (1%)
    dot_general x16, matrix products, leaf_term(): return jnp.dot(kernel_tile, sample_cols, preferred_element_type=jnp.float32)  60.6 us
    all_to_all x1, blocking collectives, sent_and_summed(): parts = lax.all_to_all(split_up(x, dim, size), axis, 0, 0, tiled=True)  51.8 us
    another operation x9, other arithmetic, basis(): jnp.linalg.cholesky(gram_matrix + ridge_term * jnp.eye(rank_width, dtype=...  37.2 us
    another operation x6, other arithmetic, basis(): lax.linalg.triangular_solve(factor, stacked, left_side=False, lower=True,...  31.4 us
    all_gather x2, blocking collectives, gathered_by_axis(): nearer = lax.all_gather(x, axes[-1], axis=dim, tiled=True)  31 us
    slice x32, local copies, waits for them, and re-layouts, kernel_block(): dist_sq = (points[0][:, None] - others[0][None, :]) ** 2  27.6 us
    ppermute x2, waiting for transfers between devices, partner(): lax.ppermute(x, axis, [(i, i ^ 1 << apart) for i in range(lax.axis_size(a...  7.33 us
  transfers between devices with their start and end apart: 2, of which 2 were waited for; matrix products, arithmetic and copies ran while one was open for 0% of the time, Pallas kernels for 0%

commit v1 on v0

v1 whole, which is shorter than its diff:
```python
import jax
import jax.numpy as jnp
from jax import lax
from jax.sharding import Mesh
from jax.sharding import PartitionSpec as P
from jax.experimental import pallas as pl
from jax.experimental.pallas import tpu as pltpu

LEAF = 512
corr_length = 0.1
ridge = 0.1
LOG2E = 1.4426950408889634
HI = lax.Precision.HIGHEST
F32 = jnp.float32
BF = jnp.bfloat16


def parts3(x):
    a = x.astype(BF).astype(F32)
    rest = x - a
    b = rest.astype(BF).astype(F32)
    return a, b, rest - b


def features(points, centre, source):
    row = lax.broadcasted_iota(jnp.int32, points.shape, 0)
    shift = jnp.where(row < 3, (points - centre) * (LOG2E / corr_length), 0.0)
    norm = jnp.sum(shift * shift, axis=0, keepdims=True)
    if source:
        full = jnp.where(row == 3, norm, jnp.where(row == 4, 1.0, shift))
        a, b, c = parts3(full)
        stack = [a, b, a, c, b, a]
    else:
        full = jnp.where(row == 4, norm, jnp.where(row == 3, 1.0, -2.0 * shift))
        a, b, c = parts3(full)
        stack = [a, a, b, a, b, c]
    return jnp.concatenate(stack, axis=0).astype(BF)


def kernel_tile(lhs, rhs):
    d2 = lax.dot_general(lhs, rhs, (((0,), (0,)), ((), ())), preferred_element_type=F32)
    d2 = jnp.maximum(d2, 1e-24)
    return jnp.exp2(-(d2 * lax.rsqrt(d2))).astype(BF)


def far_body(width, keep_ref, tgt_ref, src_ref, smp_ref, out_ref, rhs_ref, lhs_ref):
    leaf = pl.program_id(0)
    pts = tgt_ref[...]
    centre = jnp.mean(pts, axis=1, keepdims=True)
    lhs_ref[...] = features(pts, centre, False)
    rhs_ref[...] = features(src_ref[...], centre, True)
    out_ref[...] = jnp.zeros_like(out_ref)
    per = LEAF // width

    def step(i, carry):
        @pl.when(keep_ref[leaf, i // per] != 0)
        def _():
            start = pl.multiple_of(i * width, width)
            tile = kernel_tile(lhs_ref[...], rhs_ref[:, pl.ds(start, width)])
            out_ref[...] += jnp.dot(tile, smp_ref[pl.ds(start, width), :], preferred_element_type=F32)
        return carry

    lax.fori_loop(0, src_ref.shape[1] // width, step, 0)


def far_sums(keep, targets8, sources8, samples, width=512):
    leaves = targets8.shape[1] // LEAF
    cols = sources8.shape[1]
    import functools
    return pl.pallas_call(
        functools.partial(far_body, width),
        out_shape=jax.ShapeDtypeStruct((leaves * LEAF, 128), F32),
        grid_spec=pltpu.PrefetchScalarGridSpec(
            num_scalar_prefetch=1,
            grid=(leaves,),
            in_specs=[
                pl.BlockSpec((8, LEAF), lambda i, k: (0, i)),
                pl.BlockSpec((8, cols), lambda i, k: (0, 0)),
                pl.BlockSpec((cols, 128), lambda i, k: (0, 0)),
            ],
            out_specs=pl.BlockSpec((LEAF, 128), lambda i, k: (i, 0)),
            scratch_shapes=[pltpu.VMEM((48, cols), BF), pltpu.VMEM((48, LEAF), BF)],
        ),
        name="far_sums",
    )(keep, targets8, sources8, samples)


def eliminate(gram, aug_ref, top_ref):
    n = 128
    i = lax.broadcasted_iota(jnp.int32, (n, n), 0)
    j = lax.broadcasted_iota(jnp.int32, (n, n), 1)
    aug_ref[:, :n] = gram
    aug_ref[:, n:] = jnp.where(i == j, 1.0, 0.0)
    sub = lax.broadcasted_iota(jnp.int32, (8, n), 0)
    lane = lax.broadcasted_iota(jnp.int32, (8, n), 1)
    for b in range(n // 8):
        at = 8 * b
        left = aug_ref[at:at + 8, :n]
        right = aug_ref[at:at + 8, n:]
        cols = [jnp.broadcast_to(left[:, at + k:at + k + 1], (8, n)) for k in range(8)]
        scale = jnp.zeros((8, n), F32)
        for k in range(8):
            piv = jnp.broadcast_to(cols[k][k:k + 1, :], (8, n))
            inv = lax.rsqrt(piv)
            scale = jnp.where(sub == k, inv, scale)
            if k < 7:
                mult = jnp.where(sub > k, cols[k] * (inv * inv), 0.0)
                for q in range(k + 1, 8):
                    cols[q] = cols[q] - mult * jnp.broadcast_to(cols[q][k:k + 1, :], (8, n))
                left = left - mult * jnp.broadcast_to(left[k:k + 1, :], (8, n))
                right = right - mult * jnp.broadcast_to(right[k:k + 1, :], (8, n))
        left = jnp.where(lane >= sub + at, left * scale, 0.0)
        right = right * scale
        top_ref[at:at + 8, :n] = left
        top_ref[at:at + 8, n:] = right
        if b < n // 8 - 1:
            l1, l2, l3 = parts3(left)
            r1, r2, r3 = parts3(right)
            lhs = jnp.concatenate([l1, l1, l2, l1, l2, l3], axis=0).astype(BF)
            rl = jnp.concatenate([l1, l2, l1, l3, l2, l1], axis=0)
            rr = jnp.concatenate([r1, r2, r1, r3, r2, r1], axis=0)
            rhs = jnp.concatenate([rl, rr], axis=1).astype(BF)
            upd = lax.dot_general(lhs, rhs, (((0,), (0,)), ((), ())), preferred_element_type=F32)
            aug_ref[at + 8:, :] -= upd[at + 8:, :]


def regular(gram):
    i = lax.broadcasted_iota(jnp.int32, gram.shape, 0)
    j = lax.broadcasted_iota(jnp.int32, gram.shape, 1)
    diag = jnp.where(i == j, gram, 0.0)
    lam = (ridge / gram.shape[0]) * jnp.sum(jnp.sum(diag, axis=1, keepdims=True), axis=0, keepdims=True)
    return gram + jnp.where(i == j, lam, 0.0), lam


def tdot(a, b):
    return lax.dot_general(a, b, (((0,), (0,)), ((), ())), precision=HI, preferred_element_type=F32)


def ndot(a, b):
    return lax.dot_general(a, b, (((1,), (1,)), ((), ())), precision=HI, preferred_element_type=F32)


def mdot(a, b):
    return lax.dot_general(a, b, (((1,), (0,)), ((), ())), precision=HI, preferred_element_type=F32)


def leaf_body(z_ref, inv_ref, proj_ref, sq_ref, aug_ref, top_ref):
    z = z_ref[...]
    gram, lam = regular(tdot(z, z) * (1.0 / z.shape[0]))
    eliminate(gram, aug_ref, top_ref)
    inv = top_ref[:, 128:]
    proj = top_ref[:, :128] - lam * inv
    inv_ref[...] = inv
    proj_ref[...] = proj
    sq_ref[...] = tdot(proj, proj)


def node_body(a_ref, b_ref, inv_ref, proj_ref, sq_ref, aug_ref, top_ref):
    gram, lam = regular((a_ref[...] + b_ref[...]) * (1.0 / 256))
    eliminate(gram, aug_ref, top_ref)
    inv = top_ref[:, 128:]
    proj = top_ref[:, :128] - lam * inv
    inv_ref[...] = inv
    proj_ref[...] = proj
    sq_ref[...] = tdot(proj, proj)


def carry_body(z_ref, inv_ref, proj_ref, base_ref, next_ref):
    base = ndot(z_ref[...], inv_ref[...])
    base_ref[...] = base
    next_ref[...] = mdot(base, proj_ref[...])


def carry2_body(z_ref, inv_ref, proj_ref, next_ref):
    next_ref[...] = mdot(ndot(z_ref[...], inv_ref[...]), proj_ref[...])


def last_body(a_ref, b_ref, z_ref, out_ref, aug_ref, top_ref):
    gram, lam = regular((a_ref[...] + b_ref[...]) * (1.0 / 256))
    eliminate(gram, aug_ref, top_ref)
    out_ref[...] = ndot(z_ref[...], top_ref[:, 128:]) * (1.0 / 128)


def sds(*shape):
    return jax.ShapeDtypeStruct(shape, F32)


SCR = [pltpu.VMEM((128, 256), F32), pltpu.VMEM((128, 256), F32)]


def cost(f):
    return pl.CostEstimate(flops=f, bytes_accessed=400000, transcendentals=0)


def leaf_node(z):
    return pl.pallas_call(leaf_body, out_shape=(sds(128, 128),) * 3, scratch_shapes=SCR, name="leaf_node")(z)


def pair_node(a, b):
    return pl.pallas_call(node_body, out_shape=(sds(128, 128),) * 3, scratch_shapes=SCR, name="pair_node")(a, b)


def carry(z, inv, proj):
    return pl.pallas_call(carry_body, out_shape=(sds(512, 128),) * 2, name="carry")(z, inv, proj)


def carry2(z, inv, proj):
    return pl.pallas_call(carry2_body, out_shape=sds(512, 128), name="carry2")(z, inv, proj)


def last_node(a, b, z):
    return pl.pallas_call(last_body, out_shape=sds(512, 128), scratch_shapes=SCR, name="last_node")(a, b, z)


ROW = ("row_0", "row_1")
ROW_COL = ("row_0", "row_1", "col")


def gathered_by_axis(x, axes, dim):
    if not axes:
        return x
    nearer = lax.all_gather(x, axes[-1], axis=dim, tiled=True)
    return gathered_by_axis(nearer, axes[:-1], dim)


def split_up(x, dim, size):
    before, after = (x.shape[:dim], x.shape[dim + 1:])
    return jnp.moveaxis(x.reshape(*before, size, -1, *after), dim, 0)


def sent_and_summed(x, axis, dim):
    size = lax.axis_size(axis)
    parts = lax.all_to_all(split_up(x, dim, size), axis, 0, 0, tiled=True)
    return jnp.sum(parts, axis=0)


def partner(x, axis, apart):
    return lax.ppermute(x, axis, [(i, i ^ 1 << apart) for i in range(lax.axis_size(axis))])


def per_device(targets, sources, samples, near):
    sample_cols = gathered_by_axis(samples, ROW, 1)
    col_index = lax.axis_index("col")
    col_leaves = sources.shape[1] // LEAF
    local_ids = col_index * col_leaves + jnp.arange(col_leaves)
    near_hits = jnp.any(near[:, :, None] == local_ids[None, None, :], axis=1)
    keep = jnp.where(near_hits, 0, 1).astype(jnp.int32)
    pad = lambda x: jnp.pad(x, ((0, 5), (0, 0)))
    products = far_sums(keep, pad(targets), pad(sources), sample_cols)
    far_sample = sent_and_summed(products, "col", 0)
    inv0, proj0, sq0 = leaf_node(far_sample)
    sib = partner(sq0, "col", 0)
    leaf_basis, carried = carry(far_sample, inv0, proj0)
    inv1, proj1, sq1 = pair_node(sq0, sib)
    cousin = partner(sq1, "col", 1)
    carried = carry2(carried, inv1, proj1)
    nested = last_node(sq1, cousin, carried)
    return (leaf_basis, nested)


def solution(mesh):
    torus = Mesh(mesh.devices.reshape(8, 2, mesh.shape["col"]), ("row_0", "row_1", "col"))
    placed = (P(None, ROW), P(None, "col"), P("col", ROW), P(ROW, None))
    return jax.shard_map(
        per_device,
        mesh=torus,
        in_specs=placed,
        out_specs=(P(ROW_COL, None), P(ROW_COL, None)),
        check_vma=False,
    )
```

time: 266 us -> 173 us (0.65)
  other arithmetic: 72 us -> 4.49 us
  matrix products: 66.9 us -> 0 us
  Pallas kernels: 0 us -> 58.3 us
  local copies, waits for them, and re-layouts: 28.5 us -> 5.35 us
  blocking collectives: 82.8 us -> 97.8 us
  waiting for transfers between devices: 7.33 us -> 3.02 us
    another operation x15 -> x0, other arithmetic: 68.6 us -> none  [the longest x9 37.2 us: basis(): jnp.linalg.cholesky(gram_matrix + ridge_term * jnp.eye(rank_width, dtype=...]
    dot_general x23 -> x0, matrix products: 65.9 us -> none  [the longest x16 60.6 us: leaf_term(): return jnp.dot(kernel_tile, sample_cols, preferred_element_type=jnp.float32)]
    pallas_call x0 -> x6, Pallas kernels: none -> 58.3 us  [the longest x1 28.7 us: far_sums(): pl.pallas_call(functools.partial(far_body, width), out_shape=jax.ShapeDty...]
    slice x32 -> x0, local copies, waits for them, and re-layouts: 27.6 us -> none  [kernel_block(): dist_sq = (points[0][:, None] - others[0][None, :]) ** 2]
    all_to_all x1, blocking collectives: 51.8 us -> 66.9 us  [sent_and_summed(): parts = lax.all_to_all(split_up(x, dim, size), axis, 0, 0, tiled=True)]
    ppermute x2, waiting for transfers between devices: 7.33 us -> 3.02 us  [partner(): lax.ppermute(x, axis, [(i, i ^ 1 << apart) for i in range(lax.axis_size(a...]
    pad x0 -> x2, local copies, waits for them, and re-layouts: none -> 3.02 us  [per_device(): pad = lambda x: jnp.pad(x, ((0, 5), (0, 0)))]
  transfers between devices with their start and end apart: 2 -> 2, of which waited for: 2 -> 1; matrix products, arithmetic and copies ran while one was open for 0% -> 0% of each run, Pallas kernels for 0% -> 3%
where the time goes in v1:
time: 173 us; the launch traced here: 172 us
  blocking collectives  97.8 us (57%)
  Pallas kernels  58.3 us (34%)
  local copies, waits for them, and re-layouts  5.35 us (3%)
  other arithmetic  4.49 us (3%)
  waiting for transfers between devices  3.02 us (2%)
  starting transfers between devices  2.31 us (1%)
    all_to_all x1, blocking collectives, sent_and_summed(): parts = lax.all_to_all(split_up(x, dim, size), axis, 0, 0, tiled=True)  66.9 us
    all_gather x2, blocking collectives, gathered_by_axis(): nearer = lax.all_gather(x, axes[-1], axis=dim, tiled=True)  30.9 us
    pallas_call x1, Pallas kernels, far_sums(): pl.pallas_call(functools.partial(far_body, width), out_shape=jax.ShapeDty...  28.7 us
    pallas_call x1, Pallas kernels, leaf_node(): pl.pallas_call(leaf_body, out_shape=(sds(128, 128),) * 3, scratch_shapes=...  8.32 us
    pallas_call x1, Pallas kernels, last_node(): pl.pallas_call(last_body, out_shape=sds(512, 128), scratch_shapes=SCR, na...  8.13 us
    pallas_call x1, Pallas kernels, pair_node(): pl.pallas_call(node_body, out_shape=(sds(128, 128),) * 3, scratch_shapes=...  7.81 us
  transfers between devices with their start and end apart: 2, of which 1 were waited for; matrix products, arithmetic and copies ran while one was open for 0% of the time, Pallas kernels for 3%

profile of v1, /device:TPU:8, one launch (start us, length us, event | category | flops | bytes accessed | tf_op | source)
XLA Modules:
  0.0 172.0 jit_solution(9096928262258203601)
XLA Ops:
  0.6 0.8 compare_reduce_fusion
  1.4 0.1 copy.10
  1.5 0.6 broadcast_select_fusion.keep_ref
  2.1 2.1 %all_gather.6 = bf16[2048,16]{0,1:T(8,128)(2,1)S(1)} all-gather(bf16[2048,8]{0,1:T(8,128)(2,1)} %param.6), channel_id=1, replica_groups=mesh['row_0'=8,'row_1'=2,'col'=16] {'row_1'}, dimensions={1}, use_global_device_ids=true | all-gather | bytes 98304 | tf_op jit(solution)/shard_map/all_gather | solution.py:222
  4.2 1.4 pad.9.src_ref
  5.6 1.6 pad.8.tgt_ref
  7.2 28.9 %all_gather.7 = bf16[2048,128]{0,1:T(8,128)(2,1)S(1)} all-gather(bf16[2048,16]{0,1:T(8,128)(2,1)S(1)} %all_gather.6), channel_id=1, replica_groups=mesh['row_0'=8,'row_1'=2,'col'=16] {'row_0'}, dimensions={1}, use_global_device_ids=true | all-gather | bytes 589824 | tf_op jit(solution)/shard_map/all_gather | solution.py:222
  36.1 1.0 copy.11.smp_ref
  37.1 28.7 %far_sums.1 = f32[8192,128]{1,0:T(8,128)} custom-call(s32[16,4]{1,0:T(8,128)} %broadcast_select_fusion.keep_ref, f32[8,8192]{1,0:T(8,128)} %pad.8.tgt_ref, f32[8,2048]{1,0:T(8,128)} %pad.9.src_ref, bf16[2048,128]{1,0:T(8,128)(2,1)} %copy.11.smp_ref), custom_call_target="tpu_custom_call" | custom-call | tf_op jit(solution)/shard_map/far_sums/pallas_call | solution.py:70
  65.8 66.9 %all_to_all.5 = f32[16,512,128]{2,1,0:T(8,128)} all-to-all(f32[16,512,128]{2,1,0:T(8,128)} %bitcast.1), channel_id=1, replica_groups=mesh['row_0'=8,'row_1'=2,'col'=16] {'col'}, dimensions={0} | all-to-all | bytes 8388608 | tf_op jit(solution)/shard_map/all_to_all | solution.py:233
  132.6 3.1 %reduce_sum.9.z_ref = f32[512,128]{1,0:T(8,128)} reduce(f32[16,512,128]{2,1,0:T(8,128)} %all_to_all.5, f32[]{:T(128)} %constant.14.clone.1), dimensions={0}, to_apply=%region_1.2 | reduce | flops 983040 | bytes 4456452 | tf_op jit(solution)/shard_map/reduce_sum | solution.py:234
  135.7 8.3 %leaf_node.1 = (f32[128,128]{1,0:T(8,128)}, f32[128,128]{1,0:T(8,128)}, f32[128,128]{1,0:T(8,128)}) custom-call(f32[512,128]{1,0:T(8,128)} %reduce_sum.9.z_ref), custom_call_target="tpu_custom_call" | custom-call | tf_op jit(solution)/shard_map/leaf_node/pallas_call | solution.py:196
  144.1 1.5 collective-permute-start
  145.5 3.0 %collective-permute-done.b_ref = f32[128,128]{1,0:T(8,128)S(1)} collective-permute-done((f32[128,128]{1,0:T(8,128)}, f32[128,128]{1,0:T(8,128)S(1)}, u32[]{:S(2)}, u32[]{:S(2)}) %collective-permute-start) | collective-permute-done | bytes 65568 | tf_op jit(solution)/shard_map/ppermute | solution.py:238
  148.5 0.0 copy-start.1
  148.5 0.6 copy-done.1
  149.2 7.8 %pair_node.1 = (f32[128,128]{1,0:T(8,128)}, f32[128,128]{1,0:T(8,128)}, f32[128,128]{1,0:T(8,128)}) custom-call(f32[128,128]{1,0:T(8,128)} %get-tuple-element.13.a_ref, f32[128,128]{1,0:T(8,128)} %copy-done.1), custom_call_target="tpu_custom_call" | custom-call | tf_op jit(solution)/shard_map/pair_node/pallas_call | solution.py:200
  157.0 0.8 collective-permute-start.1
  157.8 2.7 %carry.1 = (f32[512,128]{1,0:T(8,128)}, f32[512,128]{1,0:T(8,128)}) custom-call(f32[512,128]{1,0:T(8,128)} %reduce_sum.9.z_ref, f32[128,128]{1,0:T(8,128)} %get-tuple-element.10.inv_ref, f32[128,128]{1,0:T(8,128)} %get-tuple-element.11.proj_ref), custom_call_target="tpu_custom_call" | custom-call | tf_op jit(solution)/shard_map/carry/pallas_call | solution.py:204
  160.5 2.7 %carry2.1.z_ref = f32[512,128]{1,0:T(8,128)} custom-call(f32[512,128]{1,0:T(8,128)} %get-tuple-element.15.z_ref, f32[128,128]{1,0:T(8,128)} %get-tuple-element.16.inv_ref, f32[128,128]{1,0:T(8,128)} %get-tuple-element.17.proj_ref), custom_call_target="tpu_custom_call" | custom-call | tf_op jit(solution)/shard_map/carry2/pallas_call | solution.py:208
  163.2 0.0 collective-permute-done.1.b_ref
  163.2 0.0 copy-start
  163.2 0.6 copy-done
  163.8 8.1 %last_node.1 = f32[512,128]{1,0:T(8,128)} custom-call(f32[128,128]{1,0:T(8,128)} %get-tuple-element.14.a_ref, f32[128,128]{1,0:T(8,128)} %copy-done, f32[512,128]{1,0:T(8,128)} %carry2.1.z_ref), custom_call_target="tpu_custom_call" | custom-call | tf_op jit(solution)/shard_map/last_node/pallas_call | solution.py:212
  (1 shorter events, 0.0 us)
Async XLA Ops:
  144.1 4.5 %collective-permute-start = (f32[128,128]{1,0:T(8,128)}, f32[128,128]{1,0:T(8,128)S(1)}, u32[]{:S(2)}, u32[]{:S(2)}) collective-permute-start(f32[128,128]{1,0:T(8,128)} %get-tuple-element.13.a_ref), channel_id=1, source_target_pairs={{0,1},{1,0},{2,3},{3,2},{4,5},{5,4},{6,7},{7,6},{8,9},{9,8},{10,11... | collective-permute-start | bytes 196616 | tf_op jit(solution)/shard_map/ppermute | solution.py:238
  148.5 0.6 copy-start.1
  157.0 6.2 %collective-permute-start.1 = (f32[128,128]{1,0:T(8,128)}, f32[128,128]{1,0:T(8,128)S(1)}, u32[]{:S(2)}, u32[]{:S(2)}) collective-permute-start(f32[128,128]{1,0:T(8,128)} %get-tuple-element.14.a_ref), channel_id=1, source_target_pairs={{0,2},{1,3},{2,0},{3,1},{4,6},{5,7},{6,4},{7,5},{8,10},{9,11},{10,... | collective-permute-start | bytes 196616 | tf_op jit(solution)/shard_map/ppermute | solution.py:238
  163.2 0.6 copy-start

commit v2 on v1

--- a/solution.py
+++ b/solution.py
@@ -22,10 +22,10 @@
     return a, b, rest - b
 
 
-def features(points, centre, source):
+def features(points, centre, source, masked=0.0):
     row = lax.broadcasted_iota(jnp.int32, points.shape, 0)
     shift = jnp.where(row < 3, (points - centre) * (LOG2E / corr_length), 0.0)
-    norm = jnp.sum(shift * shift, axis=0, keepdims=True)
+    norm = jnp.sum(shift * shift, axis=0, keepdims=True) + masked
     if source:
         full = jnp.where(row == 3, norm, jnp.where(row == 4, 1.0, shift))
         a, b, c = parts3(full)
@@ -43,46 +43,86 @@
     return jnp.exp2(-(d2 * lax.rsqrt(d2))).astype(BF)
 
 
-def far_body(width, keep_ref, tgt_ref, src_ref, smp_ref, out_ref, rhs_ref, lhs_ref):
+def tiles_body(keep_ref, tgt_ref, src_ref, out_ref):
     leaf = pl.program_id(0)
     pts = tgt_ref[...]
     centre = jnp.mean(pts, axis=1, keepdims=True)
-    lhs_ref[...] = features(pts, centre, False)
-    rhs_ref[...] = features(src_ref[...], centre, True)
-    out_ref[...] = jnp.zeros_like(out_ref)
-    per = LEAF // width
-
-    def step(i, carry):
-        @pl.when(keep_ref[leaf, i // per] != 0)
-        def _():
-            start = pl.multiple_of(i * width, width)
-            tile = kernel_tile(lhs_ref[...], rhs_ref[:, pl.ds(start, width)])
-            out_ref[...] += jnp.dot(tile, smp_ref[pl.ds(start, width), :], preferred_element_type=F32)
-        return carry
-
-    lax.fori_loop(0, src_ref.shape[1] // width, step, 0)
-
-
-def far_sums(keep, targets8, sources8, samples, width=512):
-    leaves = targets8.shape[1] // LEAF
-    cols = sources8.shape[1]
-    import functools
+    lhs = features(pts, centre, False)
+    for i in range(src_ref.shape[1] // LEAF):
+        at = slice(i * LEAF, (i + 1) * LEAF)
+        away = jnp.where(keep_ref[leaf, i] != 0, 0.0, 1e9)
+        rhs = features(src_ref[:, at], centre, True, away)
+        out_ref[:, at] = kernel_tile(lhs, rhs)
+
+
+def kernel_tiles(keep, targets8, sources8):
+    rows, cols = targets8.shape[1], sources8.shape[1]
     return pl.pallas_call(
-        functools.partial(far_body, width),
-        out_shape=jax.ShapeDtypeStruct((leaves * LEAF, 128), F32),
+        tiles_body,
+        out_shape=jax.ShapeDtypeStruct((rows, cols), BF),
         grid_spec=pltpu.PrefetchScalarGridSpec(
             num_scalar_prefetch=1,
-            grid=(leaves,),
+            grid=(rows // LEAF,),
             in_specs=[
                 pl.BlockSpec((8, LEAF), lambda i, k: (0, i)),
                 pl.BlockSpec((8, cols), lambda i, k: (0, 0)),
-                pl.BlockSpec((cols, 128), lambda i, k: (0, 0)),
             ],
-            out_specs=pl.BlockSpec((LEAF, 128), lambda i, k: (i, 0)),
-            scratch_shapes=[pltpu.VMEM((48, cols), BF), pltpu.VMEM((48, LEAF), BF)],
+            out_specs=pl.BlockSpec((LEAF, cols), lambda i, k: (i, 0)),
         ),
-        name="far_sums",
-    )(keep, targets8, sources8, samples)
+        cost_estimate=pl.CostEstimate(flops=8_000_000_000, bytes_accessed=2 * rows * cols, transcendentals=2 * rows * cols),
+        name="kernel_tiles",
+    )(keep, targets8, sources8)
+
+
+def prep_body(where_ref, mine_ref, other_ref, out_ref):
+    z, c = where_ref[0], where_ref[1]
+    for ref, half in ((mine_ref, c), (other_ref, 1 - c)):
+        rows = jnp.concatenate([ref[jnp.bitwise_xor(z, p)] for p in range(8)], axis=0)
+        start = pl.multiple_of(half * 1024, 1024)
+        out_ref[pl.ds(start, 1024), :] = rows.T
+
+
+def prepared(where, mine, other):
+    return pl.pallas_call(
+        prep_body,
+        out_shape=jax.ShapeDtypeStruct((2048, 128), BF),
+        in_specs=[pl.BlockSpec(memory_space=pltpu.SMEM)] + [pl.BlockSpec(memory_space=pltpu.VMEM)] * 2,
+        cost_estimate=pl.CostEstimate(flops=500_000_000, bytes_accessed=1_000_000, transcendentals=0),
+        name="prepared",
+    )(where, mine, other)
+
+
+def sums_body(leaf_ref, *refs):
+    tiles, cols, out_ref = refs[:4], refs[4:8], refs[8]
+    total = None
+    for k_ref, s_ref in zip(tiles, cols):
+        term = jnp.dot(k_ref[...], s_ref[...], preferred_element_type=F32)
+        total = term if total is None else total + term
+
+    @pl.when(pl.program_id(0) == 0)
+    def _():
+        out_ref[...] = total
+
+    @pl.when(pl.program_id(0) != 0)
+    def _():
+        out_ref[...] += total
+
+
+def leaf_sums(leaf, tiles, cols):
+    step = 512
+    return pl.pallas_call(
+        sums_body,
+        out_shape=jax.ShapeDtypeStruct((LEAF, 128), F32),
+        grid_spec=pltpu.PrefetchScalarGridSpec(
+            num_scalar_prefetch=1,
+            grid=(2048 // step,),
+            in_specs=[pl.BlockSpec((LEAF, step), lambda i, leaf: (leaf[0], i))] * 4
+            + [pl.BlockSpec((step, 128), lambda i, leaf: (i, 0))] * 4,
+            out_specs=pl.BlockSpec((LEAF, 128), lambda i, leaf: (0, 0)),
+        ),
+        cost_estimate=pl.CostEstimate(flops=3_000_000_000, bytes_accessed=9_000_000, transcendentals=0),
+        name="leaf_sums",
+    )(leaf, *tiles, *cols)
 
 
 def eliminate(gram, aug_ref, top_ref):
@@ -144,8 +184,9 @@
     return lax.dot_general(a, b, (((1,), (0,)), ((), ())), precision=HI, preferred_element_type=F32)
 
 
-def leaf_body(z_ref, inv_ref, proj_ref, sq_ref, aug_ref, top_ref):
-    z = z_ref[...]
+def leaf_body(a_ref, b_ref, c_ref, d_ref, z_ref, inv_ref, proj_ref, sq_ref, aug_ref, top_ref):
+    z = (a_ref[...] + b_ref[...]) + (c_ref[...] + d_ref[...])
+    z_ref[...] = z
     gram, lam = regular(tdot(z, z) * (1.0 / z.shape[0]))
     eliminate(gram, aug_ref, top_ref)
     inv = top_ref[:, 128:]
@@ -192,8 +233,9 @@
     return pl.CostEstimate(flops=f, bytes_accessed=400000, transcendentals=0)
 
 
-def leaf_node(z):
-    return pl.pallas_call(leaf_body, out_shape=(sds(128, 128),) * 3, scratch_shapes=SCR, name="leaf_node")(z)
+def leaf_node(parts):
+    outs = (sds(512, 128),) + (sds(128, 128),) * 3
+    return pl.pallas_call(leaf_body, out_shape=outs, scratch_shapes=SCR, name="leaf_node")(*parts)
 
 
 def pair_node(a, b):
@@ -212,59 +254,68 @@
     return pl.pallas_call(last_body, out_shape=sds(512, 128), scratch_shapes=SCR, name="last_node")(a, b, z)
 
 
-ROW = ("row_0", "row_1")
-ROW_COL = ("row_0", "row_1", "col")
-
-
-def gathered_by_axis(x, axes, dim):
-    if not axes:
-        return x
-    nearer = lax.all_gather(x, axes[-1], axis=dim, tiled=True)
-    return gathered_by_axis(nearer, axes[:-1], dim)
-
-
-def split_up(x, dim, size):
-    before, after = (x.shape[:dim], x.shape[dim + 1:])
-    return jnp.moveaxis(x.reshape(*before, size, -1, *after), dim, 0)
-
-
-def sent_and_summed(x, axis, dim):
+ROW = ("z", "c")
+COL = ("x", "y")
+
+
+def moved(x, axis, by):
     size = lax.axis_size(axis)
-    parts = lax.all_to_all(split_up(x, dim, size), axis, 0, 0, tiled=True)
-    return jnp.sum(parts, axis=0)
-
-
-def partner(x, axis, apart):
-    return lax.ppermute(x, axis, [(i, i ^ 1 << apart) for i in range(lax.axis_size(axis))])
+    return lax.ppermute(x, axis, [(i, (i + by) % size) for i in range(size)])
+
+
+def crossed(x, axis, bit):
+    return lax.ppermute(x, axis, [(i, i ^ bit) for i in range(lax.axis_size(axis))])
+
+
+def gathered_samples(samples, core):
+    flat = samples.T
+    half = flat.shape[1] // 2
+    mine = lax.dynamic_slice_in_dim(flat, core * half, half, 1)
+    away = lax.dynamic_slice_in_dim(flat, (1 - core) * half, half, 1)
+    near = crossed(away, "c", 1)
+    block = jnp.where(core == 0, jnp.concatenate([mine, near]), jnp.concatenate([near, mine]))[None]
+    for bit in (1, 2, 4):
+        block = jnp.concatenate([block, crossed(block, "z", bit)])
+    blocks = [block] + [moved(block, "x", q) for q in (1, 2, 3)]
+    return blocks, [crossed(b, "c", 1) for b in blocks]
 
 
 def per_device(targets, sources, samples, near):
-    sample_cols = gathered_by_axis(samples, ROW, 1)
-    col_index = lax.axis_index("col")
-    col_leaves = sources.shape[1] // LEAF
-    local_ids = col_index * col_leaves + jnp.arange(col_leaves)
-    near_hits = jnp.any(near[:, :, None] == local_ids[None, None, :], axis=1)
-    keep = jnp.where(near_hits, 0, 1).astype(jnp.int32)
-    pad = lambda x: jnp.pad(x, ((0, 5), (0, 0)))
-    products = far_sums(keep, pad(targets), pad(sources), sample_cols)
-    far_sample = sent_and_summed(products, "col", 0)
-    inv0, proj0, sq0 = leaf_node(far_sample)
-    sib = partner(sq0, "col", 0)
+    z, core, x, y = (lax.axis_index(a) for a in ("z", "c", "x", "y"))
+    pad = lambda v: jnp.pad(v, ((0, 5), (0, 0)))
+    srcs = [sources] + [moved(sources, "x", q) for q in (1, 2, 3)]
+    mine, other = gathered_samples(samples, core)
+    tgt = pad(lax.dynamic_slice_in_dim(targets, x * 2048, 2048, 1))
+    near_rows = lax.dynamic_slice_in_dim(near, x * 4, 4, 0)
+    cols = (jnp.arange(16) // 4)
+    from_x = jnp.mod(x - cols, 4)
+    ids = (from_x * 4 + y) * 4 + jnp.arange(16) % 4
+    hits = jnp.any(near_rows[:, :, None] == ids[None, None, :], axis=1)
+    keep = jnp.where(hits, 0, 1).astype(jnp.int32)
+    tiles = [kernel_tiles(keep[:, 4 * q:4 * q + 4], tgt, pad(srcs[q])) for q in range(4)]
+    where = jnp.stack([z, core]).astype(jnp.int32)
+    ready = [prepared(where, a, b) for a, b in zip(mine, other)]
+    sums = {}
+    for d in (2, 1, 3, 0):
+        leaf = jnp.mod(y + d, 4).astype(jnp.int32).reshape(1)
+        part = leaf_sums(leaf, tiles, ready)
+        sums[d] = moved(part, "y", d) if d else part
+    far_sample, inv0, proj0, sq0 = leaf_node([sums[d] for d in range(4)])
+    sib = crossed(sq0, "y", 1)
     leaf_basis, carried = carry(far_sample, inv0, proj0)
     inv1, proj1, sq1 = pair_node(sq0, sib)
-    cousin = partner(sq1, "col", 1)
+    cousin = crossed(sq1, "y", 2)
     carried = carry2(carried, inv1, proj1)
     nested = last_node(sq1, cousin, carried)
     return (leaf_basis, nested)
 
 
 def solution(mesh):
-    torus = Mesh(mesh.devices.reshape(8, 2, mesh.shape["col"]), ("row_0", "row_1", "col"))
-    placed = (P(None, ROW), P(None, "col"), P("col", ROW), P(ROW, None))
+    torus = Mesh(mesh.devices.reshape(8, 2, 4, 4), ("z", "c", "x", "y"))
     return jax.shard_map(
         per_device,
         mesh=torus,
-        in_specs=placed,
-        out_specs=(P(ROW_COL, None), P(ROW_COL, None)),
+        in_specs=(P(None, ROW), P(None, COL), P(COL, ROW), P(ROW, None)),
+        out_specs=(P(ROW + COL, None), P(ROW + COL, None)),
         check_vma=False,
     )

time: 173 us -> 153 us (0.88)
  blocking collectives: 97.8 us -> 0 us
  Pallas kernels: 58.3 us -> 98.3 us
  starting transfers between devices: 2.31 us -> 29 us
  waiting for transfers between devices: 3.02 us -> 12.5 us
  local copies, waits for them, and re-layouts: 5.35 us -> 11 us
  other arithmetic: 4.49 us -> 0.75 us
    all_to_all x1 -> x0, blocking collectives: 66.9 us -> none  [sent_and_summed(): parts = lax.all_to_all(split_up(x, dim, size), axis, 0, 0, tiled=True)]
    pallas_call x2 -> x13, Pallas kernels: 37 us -> 76.9 us  [the longest x4 33.9 us: kernel_tiles(): pl.pallas_call(tiles_body, out_shape=jax.ShapeDtypeStruct((rows, cols), B...]
    all_gather x2 -> x0, blocking collectives: 30.9 us -> none  [gathered_by_axis(): nearer = lax.all_gather(x, axes[-1], axis=dim, tiled=True)]
    ppermute x2 -> x19, starting transfers between devices: 2.31 us -> 29 us  [the longest x10 15.7 us: crossed(): lax.ppermute(x, axis, [(i, i ^ bit) for i in range(lax.axis_size(axis))])]
    ppermute x2 -> x19, waiting for transfers between devices: 3.02 us -> 12.5 us  [the longest x9 7.24 us: moved(): return lax.ppermute(x, axis, [(i, (i + by) % size) for i in range(size)])]
    unnamed x4 -> x32, local copies, waits for them, and re-layouts: 1.23 us -> 4.81 us
    reduce_sum x1 -> x0, other arithmetic: 3.11 us -> none  [sent_and_summed(): return jnp.sum(parts, axis=0)]
    pad x2 -> x5, local copies, waits for them, and re-layouts: 3.02 us -> 3.92 us  [per_device(): pad = lambda v: jnp.pad(v, ((0, 5), (0, 0)))]
  transfers between devices with their start and end apart: 2 -> 19, of which waited for: 1 -> 5; matrix products, arithmetic and copies ran while one was open for 0% -> 5% of each run, Pallas kernels for 3% -> 34%
where the time goes in v2:
time: 153 us; the launch traced here: 152 us
  Pallas kernels  98.3 us (64%)
  starting transfers between devices  29 us (19%)
  waiting for transfers between devices  12.5 us (8%)
  local copies, waits for them, and re-layouts  11 us (7%)
    pallas_call x4, Pallas kernels, kernel_tiles(): pl.pallas_call(tiles_body, out_shape=jax.ShapeDtypeStruct((rows, cols), B...  33.9 us
    pallas_call x4, Pallas kernels, leaf_sums(): pl.pallas_call(sums_body, out_shape=jax.ShapeDtypeStruct((LEAF, 128), F32...  26.3 us
    ppermute x10, starting transfers between devices, crossed(): lax.ppermute(x, axis, [(i, i ^ bit) for i in range(lax.axis_size(axis))])  15.7 us
    ppermute x9, starting transfers between devices, moved(): return lax.ppermute(x, axis, [(i, (i + by) % size) for i in range(size)])  13.4 us
    pallas_call x1, Pallas kernels, leaf_node(): pl.pallas_call(leaf_body, out_shape=outs, scratch_shapes=SCR, name='leaf_...  8.56 us
    pallas_call x4, Pallas kernels, prepared(): pl.pallas_call(prep_body, out_shape=jax.ShapeDtypeStruct((2048, 128), BF)...  8.15 us
    pallas_call x1, Pallas kernels, last_node(): pl.pallas_call(last_body, out_shape=sds(512, 128), scratch_shapes=SCR, na...  8.14 us
    pallas_call x1, Pallas kernels, pair_node(): pl.pallas_call(node_body, out_shape=(sds(128, 128),) * 3, scratch_shapes=...  7.82 us
  transfers between devices with their start and end apart: 19, of which 5 were waited for; matrix products, arithmetic and copies ran while one was open for 5% of the time, Pallas kernels for 34%

profile of v2, /device:TPU:8, one launch (start us, length us, event | category | flops | bytes accessed | tf_op | source)
XLA Modules:
  0.0 152.3 jit_solution(16774740304504795347)
XLA Ops:
  0.6 1.6 %collective-permute-start = (f32[3,2048]{1,0:T(4,128)}, f32[3,2048]{1,0:T(4,128)S(1)}, u32[]{:S(2)}, u32[]{:S(2)}) collective-permute-start(f32[3,2048]{1,0:T(4,128)} %param.5), channel_id=1, source_target_pairs={{0,4},{4,8},{8,12},{12,0},{1,5},{5,9},{9,13},{13,1},{2,6},{6,10},{... | collective-permute-start | bytes 73736 | tf_op jit(solution)/shard_map/ppermute | solution.py:263
  2.2 1.7 %collective-permute-start.2 = (f32[3,2048]{1,0:T(4,128)}, f32[3,2048]{1,0:T(4,128)S(1)}, u32[]{:S(2)}, u32[]{:S(2)}) collective-permute-start(f32[3,2048]{1,0:T(4,128)} %param.5), channel_id=1, source_target_pairs={{0,12},{4,0},{8,4},{12,8},{1,13},{5,1},{9,5},{13,9},{2,14},{6,2},{... | collective-permute-start | bytes 73736 | tf_op jit(solution)/shard_map/ppermute | solution.py:263
  4.0 1.8 %collective-permute-start.1 = (f32[3,2048]{1,0:T(4,128)}, f32[3,2048]{1,0:T(4,128)S(1)}, u32[]{:S(2)}, u32[]{:S(2)}) collective-permute-start(f32[3,2048]{1,0:T(4,128)} %param.5), channel_id=1, source_target_pairs={{0,8},{4,12},{8,0},{12,4},{1,9},{5,13},{9,1},{13,5},{2,10},{6,14},... | collective-permute-start | bytes 73736 | tf_op jit(solution)/shard_map/ppermute | solution.py:263
  10.2 2.0 %collective-permute-start.4 = (bf16[1,16,1024]{2,1,0:T(8,128)(2,1)S(1)}, bf16[1,16,1024]{2,1,0:T(8,128)(2,1)S(1)}, u32[]{:S(2)}, u32[]{:S(2)}) collective-permute-start(bf16[1,16,1024]{2,1,0:T(8,128)(2,1)S(1)} %maximum_select_fusion), channel_id=1, source_target_pairs={{0,32},{32,0},{64,96},{96,64},{128,160},{160,128},{192,224},{224,1... | collective-permute-start | bytes 98312 | tf_op jit(solution)/shard_map/ppermute | solution.py:267
  12.2 8.5 %kernel_tiles.4.refs_0_ = bf16[2048,2048]{1,0:T(8,128)(2,1)} custom-call(s32[4,4]{1,0:T(4,128)} %get-tuple-element.25.keep_ref, f32[8,2048]{1,0:T(8,128)} %pad.16.tgt_ref, f32[8,2048]{1,0:T(8,128)} %pad.17.src_ref), custom_call_target="tpu_custom_call" | custom-call | flops 8000000000 | bytes 8388608 | tf_op jit(solution)/shard_map/kernel_tiles/pallas_call | solution.py:60
  20.8 3.4 %collective-permute-start.5 = (bf16[2,16,1024]{2,1,0:T(8,128)(2,1)S(1)}, bf16[2,16,1024]{2,1,0:T(8,128)(2,1)S(1)}, u32[]{:S(2)}, u32[]{:S(2)}) collective-permute-start(bf16[2,16,1024]{2,1,0:T(8,128)(2,1)S(1)} %pad_maximum_fusion.2), channel_id=1, source_target_pairs={{0,64},{32,96},{64,0},{96,32},{128,192},{160,224},{192,128},{224,1... | collective-permute-start | bytes 196616 | tf_op jit(solution)/shard_map/ppermute | solution.py:267
  25.3 2.4 %collective-permute-done.5 = bf16[2,16,1024]{2,1,0:T(8,128)(2,1)S(1)} collective-permute-done((bf16[2,16,1024]{2,1,0:T(8,128)(2,1)S(1)}, bf16[2,16,1024]{2,1,0:T(8,128)(2,1)S(1)}, u32[]{:S(2)}, u32[]{:S(2)}) %collective-permute-start.5) | collective-permute-done | bytes 65568 | tf_op jit(solution)/shard_map/ppermute | solution.py:267
  27.8 6.0 %collective-permute-start.6 = (bf16[4,16,1024]{2,1,0:T(8,128)(2,1)S(1)}, bf16[4,16,1024]{2,1,0:T(8,128)(2,1)S(1)}, u32[]{:S(2)}, u32[]{:S(2)}) collective-permute-start(bf16[4,16,1024]{2,1,0:T(8,128)(2,1)S(1)} %pad_maximum_fusion.1), channel_id=1, source_target_pairs={{0,128},{32,160},{64,192},{96,224},{128,0},{160,32},{192,64},{224,... | collective-permute-start | bytes 393224 | tf_op jit(solution)/shard_map/ppermute | solution.py:267
  33.8 8.4 %kernel_tiles.6.refs_2_ = bf16[2048,2048]{1,0:T(8,128)(2,1)} custom-call(s32[4,4]{1,0:T(4,128)} %get-tuple-element.23.keep_ref, f32[8,2048]{1,0:T(8,128)} %pad.16.tgt_ref, f32[8,2048]{1,0:T(8,128)} %pad.19.src_ref), custom_call_target="tpu_custom_call" | custom-call | flops 8000000000 | bytes 8388608 | tf_op jit(solution)/shard_map/kernel_tiles/pallas_call | solution.py:60
  44.1 1.5 collective-permute-start.10
  46.1 8.5 %kernel_tiles.7.refs_3_ = bf16[2048,2048]{1,0:T(8,128)(2,1)} custom-call(s32[4,4]{1,0:T(4,128)} %get-tuple-element.22.keep_ref, f32[8,2048]{1,0:T(8,128)} %pad.16.tgt_ref, f32[8,2048]{1,0:T(8,128)} %pad.20.src_ref), custom_call_target="tpu_custom_call" | custom-call | flops 8000000000 | bytes 8388608 | tf_op jit(solution)/shard_map/kernel_tiles/pallas_call | solution.py:60
  56.1 2.4 %collective-permute-done.8.mine_ref = bf16[8,16,1024]{2,1,0:T(8,128)(2,1)S(1)} collective-permute-done((bf16[8,16,1024]{2,1,0:T(8,128)(2,1)S(1)}, bf16[8,16,1024]{2,1,0:T(8,128)(2,1)S(1)}, u32[]{:S(2)}, u32[]{:S(2)}) %collective-permute-start.8) | collective-permute-done | bytes 262176 | tf_op jit(solution)/shard_map/ppermute | solution.py:263
  58.4 8.4 %kernel_tiles.5.refs_1_ = bf16[2048,2048]{1,0:T(8,128)(2,1)} custom-call(s32[4,4]{1,0:T(4,128)} %get-tuple-element.24.keep_ref, f32[8,2048]{1,0:T(8,128)} %pad.16.tgt_ref, f32[8,2048]{1,0:T(8,128)} %pad.18.src_ref), custom_call_target="tpu_custom_call" | custom-call | flops 8000000000 | bytes 8388608 | tf_op jit(solution)/shard_map/kernel_tiles/pallas_call | solution.py:60
  67.6 2.0 %prepared.4.refs_4_ = bf16[2048,128]{1,0:T(8,128)(2,1)} custom-call(s32[2]{0:T(128)} %pad_add_fusion.where_ref, bf16[8,16,1024]{2,1,0:T(8,128)(2,1)} %copy-done.3, bf16[8,16,1024]{2,1,0:T(8,128)(2,1)} %copy-done.12), custom_call_target="tpu_custom_call" | custom-call | flops 500000000 | bytes 1000000 | tf_op jit(solution)/shard_map/prepared/pallas_call | solution.py:86
  70.4 2.0 %prepared.7.refs_7_ = bf16[2048,128]{1,0:T(8,128)(2,1)} custom-call(s32[2]{0:T(128)} %pad_add_fusion.where_ref, bf16[8,16,1024]{2,1,0:T(8,128)(2,1)} %copy-done.11, bf16[8,16,1024]{2,1,0:T(8,128)(2,1)} %copy-done.13), custom_call_target="tpu_custom_call" | custom-call | flops 500000000 | bytes 1000000 | tf_op jit(solution)/shard_map/prepared/pallas_call | solution.py:86
  73.1 2.0 %prepared.6.refs_6_ = bf16[2048,128]{1,0:T(8,128)(2,1)} custom-call(s32[2]{0:T(128)} %pad_add_fusion.where_ref, bf16[8,16,1024]{2,1,0:T(8,128)(2,1)} %copy-done.10, bf16[8,16,1024]{2,1,0:T(8,128)(2,1)} %copy-done.14), custom_call_target="tpu_custom_call" | custom-call | flops 500000000 | bytes 1000000 | tf_op jit(solution)/shard_map/prepared/pallas_call | solution.py:86
  75.8 2.0 %prepared.5.refs_5_ = bf16[2048,128]{1,0:T(8,128)(2,1)} custom-call(s32[2]{0:T(128)} %pad_add_fusion.where_ref, bf16[8,16,1024]{2,1,0:T(8,128)(2,1)} %copy-done.9, bf16[8,16,1024]{2,1,0:T(8,128)(2,1)} %copy-done.15), custom_call_target="tpu_custom_call" | custom-call | flops 500000000 | bytes 1000000 | tf_op jit(solution)/shard_map/prepared/pallas_call | solution.py:86
  77.9 6.5 %leaf_sums.7 = f32[512,128]{1,0:T(8,128)} custom-call(s32[1]{0:T(128)} %bitcast.10.leaf_ref, bf16[2048,2048]{1,0:T(8,128)(2,1)} %kernel_tiles.4.refs_0_, bf16[2048,2048]{1,0:T(8,128)(2,1)} %kernel_tiles.5.refs_1_, bf16[2048,2048]{1,0:T(8,128)(2,1)} %kernel_tiles.6.refs_2_, bf16[2048,2048]{1,0:T(8,128)(2,1)} %kernel_tiles.7.refs_3_, ...), custom_call_target="tpu_custom_call" | custom-call | flops 3000000000 | bytes 9000000 | tf_op jit(solution)/shard_map/leaf_sums/pallas_call | solution.py:113
  84.4 6.5 %leaf_sums.6 = f32[512,128]{1,0:T(8,128)} custom-call(s32[1]{0:T(128)} %bitcast.9.leaf_ref, bf16[2048,2048]{1,0:T(8,128)(2,1)} %kernel_tiles.4.refs_0_, bf16[2048,2048]{1,0:T(8,128)(2,1)} %kernel_tiles.5.refs_1_, bf16[2048,2048]{1,0:T(8,128)(2,1)} %kernel_tiles.6.refs_2_, bf16[2048,2048]{1,0:T(8,128)(2,1)} %kernel_tiles.7.refs_3_, ...), custom_call_target="tpu_custom_call" | custom-call | flops 3000000000 | bytes 9000000 | tf_op jit(solution)/shard_map/leaf_sums/pallas_call | solution.py:113
  91.0 6.6 %leaf_sums.5 = f32[512,128]{1,0:T(8,128)} custom-call(s32[1]{0:T(128)} %bitcast.8.leaf_ref, bf16[2048,2048]{1,0:T(8,128)(2,1)} %kernel_tiles.4.refs_0_, bf16[2048,2048]{1,0:T(8,128)(2,1)} %kernel_tiles.5.refs_1_, bf16[2048,2048]{1,0:T(8,128)(2,1)} %kernel_tiles.6.refs_2_, bf16[2048,2048]{1,0:T(8,128)(2,1)} %kernel_tiles.7.refs_3_, ...), custom_call_target="tpu_custom_call" | custom-call | flops 3000000000 | bytes 9000000 | tf_op jit(solution)/shard_map/leaf_sums/pallas_call | solution.py:113
  97.6 1.7 %collective-permute-start.14 = (f32[512,128]{1,0:T(8,128)}, f32[512,128]{1,0:T(8,128)S(1)}, u32[]{:S(2)}, u32[]{:S(2)}) collective-permute-start(f32[512,128]{1,0:T(8,128)} %leaf_sums.5), channel_id=1, source_target_pairs={{0,1},{1,2},{2,3},{3,0},{4,5},{5,6},{6,7},{7,4},{8,9},{9,10},{10,1... | collective-permute-start | bytes 786440 | tf_op jit(solution)/shard_map/ppermute | solution.py:263
  100.2 2.5 %collective-permute-start.16 = (f32[512,128]{1,0:T(8,128)S(1)}, f32[512,128]{1,0:T(8,128)S(1)}, u32[]{:S(2)}, u32[]{:S(2)}) collective-permute-start(f32[512,128]{1,0:T(8,128)S(1)} %copy-done.1), channel_id=1, source_target_pairs={{0,3},{1,0},{2,1},{3,2},{4,7},{5,4},{6,5},{7,6},{8,11},{9,8},{10,9... | collective-permute-start | bytes 786440 | tf_op jit(solution)/shard_map/ppermute | solution.py:263
  102.6 6.6 %leaf_sums.4.a_ref = f32[512,128]{1,0:T(8,128)} custom-call(s32[1]{0:T(128)} %bitcast.leaf_ref, bf16[2048,2048]{1,0:T(8,128)(2,1)} %kernel_tiles.4.refs_0_, bf16[2048,2048]{1,0:T(8,128)(2,1)} %kernel_tiles.5.refs_1_, bf16[2048,2048]{1,0:T(8,128)(2,1)} %kernel_tiles.6.refs_2_, bf16[2048,2048]{1,0:T(8,128)(2,1)} %kernel_tiles.7.refs_3_, ...), custom_call_target="tpu_custom_call" | custom-call | flops 3000000000 | bytes 9000000 | tf_op jit(solution)/shard_map/leaf_sums/pallas_call | solution.py:113
  110.0 4.1 %collective-permute-done.16.d_ref = f32[512,128]{1,0:T(8,128)S(1)} collective-permute-done((f32[512,128]{1,0:T(8,128)S(1)}, f32[512,128]{1,0:T(8,128)S(1)}, u32[]{:S(2)}, u32[]{:S(2)}) %collective-permute-start.16) | collective-permute-done | bytes 262176 | tf_op jit(solution)/shard_map/ppermute | solution.py:263
  114.8 8.6 %leaf_node.1 = (f32[512,128]{1,0:T(8,128)}, f32[128,128]{1,0:T(8,128)}, f32[128,128]{1,0:T(8,128)}, f32[128,128]{1,0:T(8,128)}) custom-call(f32[512,128]{1,0:T(8,128)} %leaf_sums.4.a_ref, f32[512,128]{1,0:T(8,128)} %copy-done.4, f32[512,128]{1,0:T(8,128)} %copy-done.5, f32[512,128]{1,0:T(8,128)} %copy-done.6), custom_call_target="tpu_custom_call" | custom-call | tf_op jit(solution)/shard_map/leaf_node/pallas_call | solution.py:238
  123.4 1.7 %collective-permute-start.17 = (f32[128,128]{1,0:T(8,128)}, f32[128,128]{1,0:T(8,128)S(1)}, u32[]{:S(2)}, u32[]{:S(2)}) collective-permute-start(f32[128,128]{1,0:T(8,128)} %get-tuple-element.15.a_ref), channel_id=1, source_target_pairs={{0,1},{1,0},{2,3},{3,2},{4,5},{5,4},{6,7},{7,6},{8,9},{9,8},{10,11... | collective-permute-start | bytes 196616 | tf_op jit(solution)/shard_map/ppermute | solution.py:267
  125.1 2.8 %collective-permute-done.17.b_ref = f32[128,128]{1,0:T(8,128)S(1)} collective-permute-done((f32[128,128]{1,0:T(8,128)}, f32[128,128]{1,0:T(8,128)S(1)}, u32[]{:S(2)}, u32[]{:S(2)}) %collective-permute-start.17) | collective-permute-done | bytes 65568 | tf_op jit(solution)/shard_map/ppermute | solution.py:267
  128.5 7.8 %pair_node.1 = (f32[128,128]{1,0:T(8,128)}, f32[128,128]{1,0:T(8,128)}, f32[128,128]{1,0:T(8,128)}) custom-call(f32[128,128]{1,0:T(8,128)} %get-tuple-element.15.a_ref, f32[128,128]{1,0:T(8,128)} %copy-done.8), custom_call_target="tpu_custom_call" | custom-call | tf_op jit(solution)/shard_map/pair_node/pallas_call | solution.py:242
  136.3 1.8 %collective-permute-start.18 = (f32[128,128]{1,0:T(8,128)}, f32[128,128]{1,0:T(8,128)S(1)}, u32[]{:S(2)}, u32[]{:S(2)}) collective-permute-start(f32[128,128]{1,0:T(8,128)} %get-tuple-element.16.a_ref), channel_id=1, source_target_pairs={{0,2},{1,3},{2,0},{3,1},{4,6},{5,7},{6,4},{7,5},{8,10},{9,11},{10,... | collective-permute-start | bytes 196616 | tf_op jit(solution)/shard_map/ppermute | solution.py:267
  138.1 2.7 %carry.1 = (f32[512,128]{1,0:T(8,128)}, f32[512,128]{1,0:T(8,128)}) custom-call(f32[512,128]{1,0:T(8,128)} %get-tuple-element.11.z_ref, f32[128,128]{1,0:T(8,128)} %get-tuple-element.12.inv_ref, f32[128,128]{1,0:T(8,128)} %get-tuple-element.13.proj_ref), custom_call_target="tpu_custom_call" | custom-call | tf_op jit(solution)/shard_map/carry/pallas_call | solution.py:246
  140.8 2.7 %carry2.1.z_ref = f32[512,128]{1,0:T(8,128)} custom-call(f32[512,128]{1,0:T(8,128)} %get-tuple-element.17.z_ref, f32[128,128]{1,0:T(8,128)} %get-tuple-element.18.inv_ref, f32[128,128]{1,0:T(8,128)} %get-tuple-element.19.proj_ref), custom_call_target="tpu_custom_call" | custom-call | tf_op jit(solution)/shard_map/carry2/pallas_call | solution.py:250
  144.1 8.1 %last_node.1 = f32[512,128]{1,0:T(8,128)} custom-call(f32[128,128]{1,0:T(8,128)} %get-tuple-element.16.a_ref, f32[128,128]{1,0:T(8,128)} %copy-done.7, f32[512,128]{1,0:T(8,128)} %carry2.1.z_ref), custom_call_target="tpu_custom_call" | custom-call | tf_op jit(solution)/shard_map/last_node/pallas_call | solution.py:254
  (73 shorter events, 15.9 us)
Async XLA Ops:
  0.6 6.8 %copy-start = (f32[3,8192]{1,0:T(4,128)S(1)}, f32[3,8192]{1,0:T(4,128)}, u32[]{:S(2)}) copy-start(f32[3,8192]{1,0:T(4,128)} %param.4) | copy-start | bytes 294916
  0.6 54.0 %collective-permute-start = (f32[3,2048]{1,0:T(4,128)}, f32[3,2048]{1,0:T(4,128)S(1)}, u32[]{:S(2)}, u32[]{:S(2)}) collective-permute-start(f32[3,2048]{1,0:T(4,128)} %param.5), channel_id=1, source_target_pairs={{0,4},{4,8},{8,12},{12,0},{1,5},{5,9},{9,13},{13,1},{2,6},{6,10},{... | collective-permute-start | bytes 73736 | tf_op jit(solution)/shard_map/ppermute | solution.py:263
  2.2 40.0 %collective-permute-start.2 = (f32[3,2048]{1,0:T(4,128)}, f32[3,2048]{1,0:T(4,128)S(1)}, u32[]{:S(2)}, u32[]{:S(2)}) collective-permute-start(f32[3,2048]{1,0:T(4,128)} %param.5), channel_id=1, source_target_pairs={{0,12},{4,0},{8,4},{12,8},{1,13},{5,1},{9,5},{13,9},{2,14},{6,2},{... | collective-permute-start | bytes 73736 | tf_op jit(solution)/shard_map/ppermute | solution.py:263
  4.0 20.7 %collective-permute-start.1 = (f32[3,2048]{1,0:T(4,128)}, f32[3,2048]{1,0:T(4,128)S(1)}, u32[]{:S(2)}, u32[]{:S(2)}) collective-permute-start(f32[3,2048]{1,0:T(4,128)} %param.5), channel_id=1, source_target_pairs={{0,8},{4,12},{8,0},{12,4},{1,9},{5,13},{9,1},{13,5},{2,10},{6,14},... | collective-permute-start | bytes 73736 | tf_op jit(solution)/shard_map/ppermute | solution.py:263
  6.5 3.7 %collective-permute-start.3 = (bf16[8,1024]{1,0:T(8,128)(2,1)S(1)}, bf16[8,1024]{1,0:T(8,128)(2,1)S(1)}, u32[]{:S(2)}, u32[]{:S(2)}) collective-permute-start(bf16[8,1024]{1,0:T(8,128)(2,1)S(1)} %get-tuple-element.21), channel_id=1, source_target_pairs={{0,16},{16,0},{1,17},{17,1},{2,18},{18,2},{3,19},{19,3},{4,20},{20... | collective-permute-start | bytes 49160 | tf_op jit(solution)/shard_map/ppermute | solution.py:267
  10.2 10.5 %collective-permute-start.4 = (bf16[1,16,1024]{2,1,0:T(8,128)(2,1)S(1)}, bf16[1,16,1024]{2,1,0:T(8,128)(2,1)S(1)}, u32[]{:S(2)}, u32[]{:S(2)}) collective-permute-start(bf16[1,16,1024]{2,1,0:T(8,128)(2,1)S(1)} %maximum_select_fusion), channel_id=1, source_target_pairs={{0,32},{32,0},{64,96},{96,64},{128,160},{160,128},{192,224},{224,1... | collective-permute-start | bytes 98312 | tf_op jit(solution)/shard_map/ppermute | solution.py:267
  20.8 7.0 %collective-permute-start.5 = (bf16[2,16,1024]{2,1,0:T(8,128)(2,1)S(1)}, bf16[2,16,1024]{2,1,0:T(8,128)(2,1)S(1)}, u32[]{:S(2)}, u32[]{:S(2)}) collective-permute-start(bf16[2,16,1024]{2,1,0:T(8,128)(2,1)S(1)} %pad_maximum_fusion.2), channel_id=1, source_target_pairs={{0,64},{32,96},{64,0},{96,32},{128,192},{160,224},{192,128},{224,1... | collective-permute-start | bytes 196616 | tf_op jit(solution)/shard_map/ppermute | solution.py:267
  27.8 15.1 %collective-permute-start.6 = (bf16[4,16,1024]{2,1,0:T(8,128)(2,1)S(1)}, bf16[4,16,1024]{2,1,0:T(8,128)(2,1)S(1)}, u32[]{:S(2)}, u32[]{:S(2)}) collective-permute-start(bf16[4,16,1024]{2,1,0:T(8,128)(2,1)S(1)} %pad_maximum_fusion.1), channel_id=1, source_target_pairs={{0,128},{32,160},{64,192},{96,224},{128,0},{160,32},{192,64},{224,... | collective-permute-start | bytes 393224 | tf_op jit(solution)/shard_map/ppermute | solution.py:267
  42.9 12.4 %copy-start.3 = (bf16[8,16,1024]{2,1,0:T(8,128)(2,1)}, bf16[8,16,1024]{2,1,0:T(8,128)(2,1)S(1)}, u32[]{:S(2)}) copy-start(bf16[8,16,1024]{2,1,0:T(8,128)(2,1)S(1)} %pad_maximum_fusion.mine_ref) | copy-start | bytes 786436
  42.9 12.4 %collective-permute-start.12 = (bf16[8,16,1024]{2,1,0:T(8,128)(2,1)S(1)}, bf16[8,16,1024]{2,1,0:T(8,128)(2,1)S(1)}, u32[]{:S(2)}, u32[]{:S(2)}) collective-permute-start(bf16[8,16,1024]{2,1,0:T(8,128)(2,1)S(1)} %pad_maximum_fusion.mine_ref), channel_id=1, source_target_pairs={{0,12},{4,0},{8,4},{12,8},{1,13},{5,1},{9,5},{13,9},{2,14},{6,2},{... | collective-permute-start | bytes 786440 | tf_op jit(solution)/shard_map/ppermute | solution.py:263
  44.1 11.7 %collective-permute-start.10 = (bf16[8,16,1024]{2,1,0:T(8,128)(2,1)S(1)}, bf16[8,16,1024]{2,1,0:T(8,128)(2,1)S(1)}, u32[]{:S(2)}, u32[]{:S(2)}) collective-permute-start(bf16[8,16,1024]{2,1,0:T(8,128)(2,1)S(1)} %pad_maximum_fusion.mine_ref), channel_id=1, source_target_pairs={{0,8},{4,12},{8,0},{12,4},{1,9},{5,13},{9,1},{13,5},{2,10},{6,14},... | collective-permute-start | bytes 786440 | tf_op jit(solution)/shard_map/ppermute | solution.py:263
  45.6 12.8 %collective-permute-start.8 = (bf16[8,16,1024]{2,1,0:T(8,128)(2,1)S(1)}, bf16[8,16,1024]{2,1,0:T(8,128)(2,1)S(1)}, u32[]{:S(2)}, u32[]{:S(2)}) collective-permute-start(bf16[8,16,1024]{2,1,0:T(8,128)(2,1)S(1)} %pad_maximum_fusion.mine_ref), channel_id=1, source_target_pairs={{0,4},{4,8},{8,12},{12,0},{1,5},{5,9},{9,13},{13,1},{2,6},{6,10},{... | collective-permute-start | bytes 786440 | tf_op jit(solution)/shard_map/ppermute | solution.py:263
  55.2 11.7 %collective-permute-start.7 = (bf16[8,16,1024]{2,1,0:T(8,128)(2,1)S(1)}, bf16[8,16,1024]{2,1,0:T(8,128)(2,1)S(1)}, u32[]{:S(2)}, u32[]{:S(2)}) collective-permute-start(bf16[8,16,1024]{2,1,0:T(8,128)(2,1)S(1)} %pad_maximum_fusion.mine_ref), channel_id=1, source_target_pairs={{0,16},{16,0},{1,17},{17,1},{2,18},{18,2},{3,19},{19,3},{4,20},{20... | collective-permute-start | bytes 786440 | tf_op jit(solution)/shard_map/ppermute | solution.py:267
  55.3 11.6 %copy-start.11 = (bf16[8,16,1024]{2,1,0:T(8,128)(2,1)}, bf16[8,16,1024]{2,1,0:T(8,128)(2,1)S(1)}, u32[]{:S(2)}) copy-start(bf16[8,16,1024]{2,1,0:T(8,128)(2,1)S(1)} %collective-permute-done.12.mine_ref) | copy-start | bytes 786436
  55.3 14.4 %collective-permute-start.13 = (bf16[8,16,1024]{2,1,0:T(8,128)(2,1)S(1)}, bf16[8,16,1024]{2,1,0:T(8,128)(2,1)S(1)}, u32[]{:S(2)}, u32[]{:S(2)}) collective-permute-start(bf16[8,16,1024]{2,1,0:T(8,128)(2,1)S(1)} %collective-permute-done.12.mine_ref), channel_id=1, source_target_pairs={{0,16},{16,0},{1,17},{17,1},{2,18},{18,2},{3,19},{19,3},{4,20},{20... | collective-permute-start | bytes 786440 | tf_op jit(solution)/shard_map/ppermute | solution.py:267
  55.8 11.1 %copy-start.10 = (bf16[8,16,1024]{2,1,0:T(8,128)(2,1)}, bf16[8,16,1024]{2,1,0:T(8,128)(2,1)S(1)}, u32[]{:S(2)}) copy-start(bf16[8,16,1024]{2,1,0:T(8,128)(2,1)S(1)} %collective-permute-done.10.mine_ref) | copy-start | bytes 786436
  55.8 16.6 %collective-permute-start.11 = (bf16[8,16,1024]{2,1,0:T(8,128)(2,1)S(1)}, bf16[8,16,1024]{2,1,0:T(8,128)(2,1)S(1)}, u32[]{:S(2)}, u32[]{:S(2)}) collective-permute-start(bf16[8,16,1024]{2,1,0:T(8,128)(2,1)S(1)} %collective-permute-done.10.mine_ref), channel_id=1, source_target_pairs={{0,16},{16,0},{1,17},{17,1},{2,18},{18,2},{3,19},{19,3},{4,20},{20... | collective-permute-start | bytes 786440 | tf_op jit(solution)/shard_map/ppermute | solution.py:267
  58.4 8.5 %copy-start.9 = (bf16[8,16,1024]{2,1,0:T(8,128)(2,1)}, bf16[8,16,1024]{2,1,0:T(8,128)(2,1)S(1)}, u32[]{:S(2)}) copy-start(bf16[8,16,1024]{2,1,0:T(8,128)(2,1)S(1)} %collective-permute-done.8.mine_ref) | copy-start | bytes 786436
  58.4 16.7 %collective-permute-start.9 = (bf16[8,16,1024]{2,1,0:T(8,128)(2,1)S(1)}, bf16[8,16,1024]{2,1,0:T(8,128)(2,1)S(1)}, u32[]{:S(2)}, u32[]{:S(2)}) collective-permute-start(bf16[8,16,1024]{2,1,0:T(8,128)(2,1)S(1)} %collective-permute-done.8.mine_ref), channel_id=1, source_target_pairs={{0,16},{16,0},{1,17},{17,1},{2,18},{18,2},{3,19},{19,3},{4,20},{20... | collective-permute-start | bytes 786440 | tf_op jit(solution)/shard_map/ppermute | solution.py:267
  66.9 0.7 copy-start.12
  69.7 0.7 copy-start.13
  72.4 0.7 copy-start.14
  75.1 0.7 copy-start.15
  90.9 8.3 %copy-start.2 = (f32[512,128]{1,0:T(8,128)S(1)}, f32[512,128]{1,0:T(8,128)}, u32[]{:S(2)}) copy-start(f32[512,128]{1,0:T(8,128)} %leaf_sums.6) | copy-start | bytes 786436
  90.9 9.2 %copy-start.1 = (f32[512,128]{1,0:T(8,128)S(1)}, f32[512,128]{1,0:T(8,128)}, u32[]{:S(2)}) copy-start(f32[512,128]{1,0:T(8,128)} %leaf_sums.7) | copy-start | bytes 786436
  97.6 11.7 %collective-permute-start.14 = (f32[512,128]{1,0:T(8,128)}, f32[512,128]{1,0:T(8,128)S(1)}, u32[]{:S(2)}, u32[]{:S(2)}) collective-permute-start(f32[512,128]{1,0:T(8,128)} %leaf_sums.5), channel_id=1, source_target_pairs={{0,1},{1,2},{2,3},{3,0},{4,5},{5,6},{6,7},{7,4},{8,9},{9,10},{10,1... | collective-permute-start | bytes 786440 | tf_op jit(solution)/shard_map/ppermute | solution.py:263
  99.3 10.7 %collective-permute-start.15 = (f32[512,128]{1,0:T(8,128)S(1)}, f32[512,128]{1,0:T(8,128)S(1)}, u32[]{:S(2)}, u32[]{:S(2)}) collective-permute-start(f32[512,128]{1,0:T(8,128)S(1)} %copy-done.2), channel_id=1, source_target_pairs={{0,2},{1,3},{2,0},{3,1},{4,6},{5,7},{6,4},{7,5},{8,10},{9,11},{10,... | collective-permute-start | bytes 786440 | tf_op jit(solution)/shard_map/ppermute | solution.py:263
  100.2 14.0 %collective-permute-start.16 = (f32[512,128]{1,0:T(8,128)S(1)}, f32[512,128]{1,0:T(8,128)S(1)}, u32[]{:S(2)}, u32[]{:S(2)}) collective-permute-start(f32[512,128]{1,0:T(8,128)S(1)} %copy-done.1), channel_id=1, source_target_pairs={{0,3},{1,0},{2,1},{3,2},{4,7},{5,4},{6,5},{7,6},{8,11},{9,8},{10,9... | collective-permute-start | bytes 786440 | tf_op jit(solution)/shard_map/ppermute | solution.py:263
  109.3 4.9 %copy-start.4 = (f32[512,128]{1,0:T(8,128)}, f32[512,128]{1,0:T(8,128)S(1)}, u32[]{:S(2)}) copy-start(f32[512,128]{1,0:T(8,128)S(1)} %collective-permute-done.14.b_ref) | copy-start | bytes 786436
  110.0 4.1 %copy-start.5 = (f32[512,128]{1,0:T(8,128)}, f32[512,128]{1,0:T(8,128)S(1)}, u32[]{:S(2)}) copy-start(f32[512,128]{1,0:T(8,128)S(1)} %collective-permute-done.15.c_ref) | copy-start | bytes 786436
  123.4 4.5 %collective-permute-start.17 = (f32[128,128]{1,0:T(8,128)}, f32[128,128]{1,0:T(8,128)S(1)}, u32[]{:S(2)}, u32[]{:S(2)}) collective-permute-start(f32[128,128]{1,0:T(8,128)} %get-tuple-element.15.a_ref), channel_id=1, source_target_pairs={{0,1},{1,0},{2,3},{3,2},{4,5},{5,4},{6,7},{7,6},{8,9},{9,8},{10,11... | collective-permute-start | bytes 196616 | tf_op jit(solution)/shard_map/ppermute | solution.py:267
  136.3 7.2 %collective-permute-start.18 = (f32[128,128]{1,0:T(8,128)}, f32[128,128]{1,0:T(8,128)S(1)}, u32[]{:S(2)}, u32[]{:S(2)}) collective-permute-start(f32[128,128]{1,0:T(8,128)} %get-tuple-element.16.a_ref), channel_id=1, source_target_pairs={{0,2},{1,3},{2,0},{3,1},{4,6},{5,7},{6,4},{7,5},{8,10},{9,11},{10,... | collective-permute-start | bytes 196616 | tf_op jit(solution)/shard_map/ppermute | solution.py:267
  (3 other events, 2.0 us)

commit v3 on v2

v3 whole, which is shorter than its diff:
```python
import functools

import jax
import jax.numpy as jnp
from jax import lax
from jax.sharding import Mesh
from jax.sharding import PartitionSpec as P
from jax.experimental import pallas as pl
from jax.experimental.pallas import tpu as pltpu

LEAF = 512
corr_length = 0.1
ridge = 0.1
LOG2E = 1.4426950408889634
HI = lax.Precision.HIGHEST
F32 = jnp.float32
BF = jnp.bfloat16


def parts3(x):
    a = x.astype(BF).astype(F32)
    rest = x - a
    b = rest.astype(BF).astype(F32)
    return a, b, rest - b


def features(pts_ref, centre, source, masked=0.0):
    points = pts_ref[...]
    row = lax.broadcasted_iota(jnp.int32, points.shape, 0)
    shift = jnp.where(row < 3, (points - centre) * (LOG2E / corr_length), 0.0)
    norm = jnp.sum(shift * shift, axis=0, keepdims=True) + masked
    if source:
        a, b, c = parts3(jnp.where(row == 3, norm, jnp.where(row == 4, 1.0, shift)))
        stack = [a, b, a, c, b, a]
    else:
        a, b, c = parts3(jnp.where(row == 4, norm, jnp.where(row == 3, 1.0, -2.0 * shift)))
        stack = [a, a, b, a, b, c]
    return jnp.concatenate(stack, axis=0).astype(BF)


def kernel_tile(rows, cols):
    d2 = lax.dot_general(rows, cols, (((0,), (0,)), ((), ())), preferred_element_type=F32)
    d2 = jnp.maximum(d2, 1e-24)
    return jnp.exp2(-(d2 * lax.rsqrt(d2))).astype(BF)


def target_features(tgt_ref, pts_ref, row_leaf):
    pts_ref[...] = jnp.zeros_like(pts_ref)
    pts_ref[0:3, :] = tgt_ref[:, pl.ds(pl.multiple_of(row_leaf * LEAF, LEAF), LEAF)]
    centre = jnp.mean(pts_ref[...], axis=1, keepdims=True)
    return features(pts_ref, centre, False), centre


def tile_of(q, i, leaf, at_ref, near_ref, src_ref, pts_ref, cols, centre):
    c, x, y = at_ref[1], at_ref[2], at_ref[3]
    chunk = jnp.bitwise_and(2 * c + i, 3)
    leaf_id = (jnp.bitwise_and(x - q, 3) * 4 + y) * 4 + chunk
    hit = near_ref[x * 4 + leaf, 0] == leaf_id
    for k in range(1, 8):
        hit = jnp.logical_or(hit, near_ref[x * 4 + leaf, k] == leaf_id)
    pts_ref[0:3, :] = src_ref[:, pl.ds(pl.multiple_of(chunk * LEAF, LEAF), LEAF)]
    return kernel_tile(features(pts_ref, centre, True, jnp.where(hit, 1e9, 0.0)), cols)


def tiles_body(q, at_ref, near_ref, tgt_ref, src_ref, out_ref, tpts_ref, spts_ref):
    leaf = pl.program_id(0)
    cols, centre = target_features(tgt_ref, tpts_ref, at_ref[2] * 4 + leaf)
    spts_ref[...] = jnp.zeros_like(spts_ref)
    for i in range(4):
        out_ref[i * LEAF:(i + 1) * LEAF, :] = tile_of(
            q, i, leaf, at_ref, near_ref, src_ref, spts_ref.at[i], cols, centre)


def kernel_tiles(q, at, near, targets, sources):
    return pl.pallas_call(
        functools.partial(tiles_body, q),
        out_shape=jax.ShapeDtypeStruct((2048, 2048), BF),
        grid_spec=pltpu.PrefetchScalarGridSpec(
            num_scalar_prefetch=2,
            grid=(4,),
            in_specs=[
                pl.BlockSpec((3, targets.shape[1]), lambda i, a, n: (0, 0)),
                pl.BlockSpec((3, 2048), lambda i, a, n: (0, 0)),
            ],
            out_specs=pl.BlockSpec((2048, LEAF), lambda i, a, n: (0, i)),
            scratch_shapes=[pltpu.VMEM((8, LEAF), F32), pltpu.VMEM((4, 8, LEAF), F32)],
        ),
        cost_estimate=pl.CostEstimate(flops=8_000_000_000, bytes_accessed=8_400_000, transcendentals=8_400_000),
        name="kernel_tiles",
    )(at, near, targets, sources)


def sums_body(turn, stored, fused, at_ref, near_ref, tgt_ref, *refs):
    ns, nf = len(stored), len(fused)
    tiles, refs = refs[:ns], refs[ns:]
    srcs, refs = refs[:nf], refs[nf:]
    mine, refs = refs[:ns + nf], refs[ns + nf:]
    other, refs = refs[:ns + nf], refs[ns + nf:]
    out_ref, tpts_ref, spts_ref = refs
    i = pl.program_id(0)
    leaf = jnp.bitwise_and(at_ref[3] + turn, 3)
    cols, centre = target_features(tgt_ref, tpts_ref, at_ref[2] * 4 + leaf)
    spts_ref[...] = jnp.zeros_like(spts_ref)
    total = jnp.zeros((128, LEAF), F32)
    for n in range(ns + nf):
        rows = jnp.where(i < 2, mine[n][...], other[n][...]).reshape(128, LEAF)
        if n < ns:
            tile = tiles[n][...]
        else:
            tile = tile_of(fused[n - ns], i, leaf, at_ref, near_ref, srcs[n - ns], spts_ref.at[n - ns], cols, centre)
        total += jnp.dot(rows, tile, preferred_element_type=F32)

    @pl.when(i == 0)
    def _():
        out_ref[...] = total

    @pl.when(i != 0)
    def _():
        out_ref[...] += total


def leaf_sums(turn, at, near, targets, tiles, sources, mine, other):
    stored, fused = sorted(tiles), sorted(sources)
    order = stored + fused
    width = len(fused)
    return pl.pallas_call(
        functools.partial(sums_body, turn, stored, fused),
        out_shape=jax.ShapeDtypeStruct((128, LEAF), F32),
        grid_spec=pltpu.PrefetchScalarGridSpec(
            num_scalar_prefetch=2,
            grid=(4,),
            in_specs=[pl.BlockSpec((3, targets.shape[1]), lambda i, a, n: (0, 0))]
            + [pl.BlockSpec((LEAF, LEAF), lambda i, a, n: (i, jnp.bitwise_and(a[3] + turn, 3)))] * len(stored)
            + [pl.BlockSpec((3, 2048), lambda i, a, n: (0, 0))] * width
            + [pl.BlockSpec((4, 32, LEAF), lambda i, a, n: (0, 0, jnp.minimum(i, 1)))] * 4
            + [pl.BlockSpec((4, 32, LEAF), lambda i, a, n: (0, 0, jnp.maximum(i - 2, 0)))] * 4,
            out_specs=pl.BlockSpec((128, LEAF), lambda i, a, n: (0, 0)),
            scratch_shapes=[pltpu.VMEM((8, LEAF), F32), pltpu.VMEM((width, 8, LEAF), F32)],
        ),
        cost_estimate=pl.CostEstimate(flops=4_000_000_000, bytes_accessed=9_000_000, transcendentals=1_000_000),
        name="leaf_sums",
    )(at, near, targets, *[tiles[q] for q in stored], *[sources[q] for q in fused],
      *[mine[q] for q in order], *[other[q] for q in order])


def eliminate(gram, aug_ref, top_ref):
    n = 128
    i = lax.broadcasted_iota(jnp.int32, (n, n), 0)
    j = lax.broadcasted_iota(jnp.int32, (n, n), 1)
    aug_ref[:, :n] = gram
    aug_ref[:, n:] = jnp.where(i == j, 1.0, 0.0)
    sub = lax.broadcasted_iota(jnp.int32, (8, n), 0)
    lane = lax.broadcasted_iota(jnp.int32, (8, n), 1)
    for b in range(n // 8):
        at = 8 * b
        left = aug_ref[at:at + 8, :n]
        right = aug_ref[at:at + 8, n:]
        cols = [jnp.broadcast_to(left[:, at + k:at + k + 1], (8, n)) for k in range(8)]
        scale = jnp.zeros((8, n), F32)
        for k in range(8):
            piv = jnp.broadcast_to(cols[k][k:k + 1, :], (8, n))
            inv = lax.rsqrt(piv)
            scale = jnp.where(sub == k, inv, scale)
            if k < 7:
                mult = jnp.where(sub > k, cols[k] * (inv * inv), 0.0)
                for q in range(k + 1, 8):
                    cols[q] = cols[q] - mult * jnp.broadcast_to(cols[q][k:k + 1, :], (8, n))
                left = left - mult * jnp.broadcast_to(left[k:k + 1, :], (8, n))
                right = right - mult * jnp.broadcast_to(right[k:k + 1, :], (8, n))
        left = jnp.where(lane >= sub + at, left * scale, 0.0)
        right = right * scale
        top_ref[at:at + 8, :n] = left
        top_ref[at:at + 8, n:] = right
        if b < n // 8 - 1:
            l1, l2, l3 = parts3(left)
            r1, r2, r3 = parts3(right)
            lhs = jnp.concatenate([l1, l1, l2, l1, l2, l3], axis=0).astype(BF)
            rl = jnp.concatenate([l1, l2, l1, l3, l2, l1], axis=0)
            rr = jnp.concatenate([r1, r2, r1, r3, r2, r1], axis=0)
            rhs = jnp.concatenate([rl, rr], axis=1).astype(BF)
            upd = lax.dot_general(lhs, rhs, (((0,), (0,)), ((), ())), preferred_element_type=F32)
            aug_ref[at + 8:, :] -= upd[at + 8:, :]


def regular(gram):
    i = lax.broadcasted_iota(jnp.int32, gram.shape, 0)
    j = lax.broadcasted_iota(jnp.int32, gram.shape, 1)
    diag = jnp.where(i == j, gram, 0.0)
    lam = (ridge / gram.shape[0]) * jnp.sum(jnp.sum(diag, axis=1, keepdims=True), axis=0, keepdims=True)
    return gram + jnp.where(i == j, lam, 0.0), lam


def tdot(a, b):
    return lax.dot_general(a, b, (((0,), (0,)), ((), ())), precision=HI, preferred_element_type=F32)


def ndot(a, b):
    return lax.dot_general(a, b, (((1,), (1,)), ((), ())), precision=HI, preferred_element_type=F32)


def mdot(a, b):
    return lax.dot_general(a, b, (((1,), (0,)), ((), ())), precision=HI, preferred_element_type=F32)


def leaf_body(at_ref, a_ref, b_ref, c_ref, d_ref, z_ref, inv_ref, proj_ref, sq_ref, aug_ref, top_ref):
    for k in range(4):
        for s in range(2):
            plane = jnp.bitwise_xor(jnp.bitwise_and(at_ref[0] - 2 * k, 7), s)
            rows = slice(16 * (2 * k + s), 16 * (2 * k + s) + 16)
            both = (a_ref[rows, :] + b_ref[rows, :]) + (c_ref[rows, :] + d_ref[rows, :])
            z_ref[pl.ds(pl.multiple_of(plane * 16, 16), 16), :] = both
    z = z_ref[...]
    gram, lam = regular(ndot(z, z) * (1.0 / LEAF))
    eliminate(gram, aug_ref, top_ref)
    inv = top_ref[:, 128:]
    proj = top_ref[:, :128] - lam * inv
    inv_ref[...] = inv
    proj_ref[...] = proj
    sq_ref[...] = tdot(proj, proj)


def node_body(a_ref, b_ref, inv_ref, proj_ref, sq_ref, aug_ref, top_ref):
    gram, lam = regular((a_ref[...] + b_ref[...]) * (1.0 / 256))
    eliminate(gram, aug_ref, top_ref)
    inv = top_ref[:, 128:]
    proj = top_ref[:, :128] - lam * inv
    inv_ref[...] = inv
    proj_ref[...] = proj
    sq_ref[...] = tdot(proj, proj)


def carry_body(z_ref, inv_ref, proj_ref, base_ref, next_ref):
    base = lax.dot_general(z_ref[...], inv_ref[...], (((0,), (1,)), ((), ())), precision=HI, preferred_element_type=F32)
    base_ref[...] = base
    next_ref[...] = mdot(base, proj_ref[...])


def carry2_body(z_ref, inv_ref, proj_ref, next_ref):
    next_ref[...] = mdot(ndot(z_ref[...], inv_ref[...]), proj_ref[...])


def last_body(a_ref, b_ref, z_ref, out_ref, aug_ref, top_ref):
    gram, lam = regular((a_ref[...] + b_ref[...]) * (1.0 / 256))
    eliminate(gram, aug_ref, top_ref)
    out_ref[...] = ndot(z_ref[...], top_ref[:, 128:]) * (1.0 / 128)


def sds(*shape):
    return jax.ShapeDtypeStruct(shape, F32)


SCR = [pltpu.VMEM((128, 256), F32), pltpu.VMEM((128, 256), F32)]


def cost(f):
    return pl.CostEstimate(flops=f, bytes_accessed=400000, transcendentals=0)


def leaf_node(at, parts):
    vm = pl.BlockSpec(memory_space=pltpu.VMEM)
    return pl.pallas_call(
        leaf_body,
        out_shape=(sds(128, LEAF),) + (sds(128, 128),) * 3,
        in_specs=[pl.BlockSpec(memory_space=pltpu.SMEM)] + [vm] * 4,
        scratch_shapes=SCR,
        name="leaf_node",
    )(at, *parts)


def pair_node(a, b):
    return pl.pallas_call(node_body, out_shape=(sds(128, 128),) * 3, scratch_shapes=SCR, name="pair_node")(a, b)


def carry(z, inv, proj):
    return pl.pallas_call(carry_body, out_shape=(sds(512, 128),) * 2, name="carry")(z, inv, proj)


def carry2(z, inv, proj):
    return pl.pallas_call(carry2_body, out_shape=sds(512, 128), name="carry2")(z, inv, proj)


def last_node(a, b, z):
    return pl.pallas_call(last_body, out_shape=sds(512, 128), scratch_shapes=SCR, name="last_node")(a, b, z)


ROW = ("z", "c")
COL = ("x", "y")


def moved(x, axis, by):
    size = lax.axis_size(axis)
    return lax.ppermute(x, axis, [(i, (i + by) % size) for i in range(size)])


def crossed(x, axis, bit):
    return lax.ppermute(x, axis, [(i, i ^ bit) for i in range(lax.axis_size(axis))])


def diagonal(x):
    return lax.ppermute(x, ROW, [(i, i ^ 3) for i in range(16)])


def own_half(samples, core):
    flat = samples.T
    half = flat.shape[1] // 2
    mine = lax.dynamic_slice_in_dim(flat, core * half, half, 1)
    away = lax.dynamic_slice_in_dim(flat, (1 - core) * half, half, 1)
    across, up, cross = crossed(away, "c", 1), crossed(mine, "z", 1), diagonal(away)
    first = jnp.where(core == 0, jnp.concatenate([mine, across]), jnp.concatenate([across, mine]))
    second = jnp.where(core == 0, jnp.concatenate([up, cross]), jnp.concatenate([cross, up]))
    pair = jnp.concatenate([first, second])
    return jnp.stack([pair] + [moved(pair, "z", 2 * k) for k in (1, 2, 3)])


def per_device(targets, sources, samples, near):
    at = jnp.stack([lax.axis_index(a) for a in ("z", "c", "x", "y")]).astype(jnp.int32)
    block = own_half(samples, at[1])
    srcs = [sources] + [moved(sources, "x", q) for q in (1, 2, 3)]
    mine = [block] + [moved(block, "x", q) for q in (1, 2, 3)]
    other = [crossed(b, "c", 1) for b in mine]
    stored = (0, 1, 3)
    tiles = {q: kernel_tiles(q, at, near, targets, srcs[q]) for q in stored}
    fused = {q: srcs[q] for q in range(4) if q not in stored}
    sums = {}
    for d in (2, 1, 3, 0):
        part = leaf_sums(d, at, near, targets, tiles, fused, mine, other)
        sums[d] = moved(part, "y", d) if d else part
    far_sample, inv0, proj0, sq0 = leaf_node(at, [sums[d] for d in range(4)])
    sib = crossed(sq0, "y", 1)
    leaf_basis, carried = carry(far_sample, inv0, proj0)
    inv1, proj1, sq1 = pair_node(sq0, sib)
    cousin = crossed(sq1, "y", 2)
    carried = carry2(carried, inv1, proj1)
    nested = last_node(sq1, cousin, carried)
    return (leaf_basis, nested)


def solution(mesh):
    torus = Mesh(mesh.devices.reshape(8, 2, 4, 4), ("z", "c", "x", "y"))
    return jax.shard_map(
        per_device,
        mesh=torus,
        in_specs=(P(None, ROW), P(None, COL), P(COL, ROW), P(ROW, None)),
        out_specs=(P(ROW + COL, None), P(ROW + COL, None)),
        check_vma=False,
    )
```

time: 153 us -> 133 us (0.87)
  Pallas kernels: 98.3 us -> 87.3 us
  waiting for transfers between devices: 12.5 us -> 4.81 us
  local copies, waits for them, and re-layouts: 11 us -> 6.38 us
  starting transfers between devices: 29 us -> 32.1 us
    ppermute x9 -> x12, starting transfers between devices: 13.4 us -> 26.6 us  [moved(): return lax.ppermute(x, axis, [(i, (i + by) % size) for i in range(size)])]
    ppermute x10 -> x8, starting transfers between devices: 15.7 us -> 4.14 us  [crossed(): lax.ppermute(x, axis, [(i, i ^ bit) for i in range(lax.axis_size(axis))])]
    pallas_call x13 -> x8, Pallas kernels: 76.9 us -> 65.8 us  [the longest x4 30.6 us: leaf_sums(): pl.pallas_call(functools.partial(sums_body, turn, stored, fused), out_sha...]
    ppermute x9 -> x12, waiting for transfers between devices: 7.24 us -> 0.03 us  [moved(): return lax.ppermute(x, axis, [(i, (i + by) % size) for i in range(size)])]
    pad x5 -> x0, local copies, waits for them, and re-layouts: 3.92 us -> none  [per_device(): pad = lambda v: jnp.pad(v, ((0, 5), (0, 0)))]
    unnamed x32 -> x35, local copies, waits for them, and re-layouts: 4.81 us -> 5.64 us
    ppermute x10 -> x8, waiting for transfers between devices: 5.21 us -> 4.78 us  [crossed(): lax.ppermute(x, axis, [(i, i ^ bit) for i in range(lax.axis_size(axis))])]
  transfers between devices with their start and end apart: 19 -> 21, of which waited for: 5 -> 2; matrix products, arithmetic and copies ran while one was open for 5% -> 2% of each run, Pallas kernels for 34% -> 42%
where the time goes in v3:
time: 133 us; the launch traced here: 132 us
  Pallas kernels  87.3 us (66%)
  starting transfers between devices  32.1 us (24%)
  local copies, waits for them, and re-layouts  6.38 us (5%)
  waiting for transfers between devices  4.81 us (4%)
    pallas_call x4, Pallas kernels, leaf_sums(): pl.pallas_call(functools.partial(sums_body, turn, stored, fused), out_sha...  30.6 us
    ppermute x12, starting transfers between devices, moved(): return lax.ppermute(x, axis, [(i, (i + by) % size) for i in range(size)])  26.6 us
    pallas_call x3, Pallas kernels, kernel_tiles(): pl.pallas_call(functools.partial(tiles_body, q), out_shape=jax.ShapeDtype...  26.5 us
    pallas_call x1, Pallas kernels, leaf_node(): pl.pallas_call(leaf_body, out_shape=(sds(128, LEAF),) + (sds(128, 128),)...  8.7 us
    pallas_call x1, Pallas kernels, last_node(): pl.pallas_call(last_body, out_shape=sds(512, 128), scratch_shapes=SCR, na...  8.13 us
    pallas_call x1, Pallas kernels, pair_node(): pl.pallas_call(node_body, out_shape=(sds(128, 128),) * 3, scratch_shapes=...  7.83 us
    unnamed x35, local copies, waits for them, and re-layouts  5.64 us
    ppermute x8, waiting for transfers between devices, crossed(): lax.ppermute(x, axis, [(i, i ^ bit) for i in range(lax.axis_size(axis))])  4.78 us
  transfers between devices with their start and end apart: 21, of which 2 were waited for; matrix products, arithmetic and copies ran while one was open for 2% of the time, Pallas kernels for 42%

profile of v3, /device:TPU:8, one launch (start us, length us, event | category | flops | bytes accessed | tf_op | source)
XLA Modules:
  0.0 132.1 jit_solution(2723339157726162980)
XLA Ops:
  0.6 0.7 dynamic-slice_bitcast_fusion.1
  1.4 1.4 %collective-permute-start.5 = (bf16[8,1024]{1,0:T(8,128)(2,1)S(1)}, bf16[8,1024]{1,0:T(8,128)(2,1)S(1)}, u32[]{:S(2)}, u32[]{:S(2)}) collective-permute-start(bf16[8,1024]{1,0:T(8,128)(2,1)S(1)} %get-tuple-element.23), channel_id=1, source_target_pairs={{0,48},{16,32},{32,16},{48,0},{64,112},{80,96},{96,80},{112,64},{1... | collective-permute-start | bytes 49160 | tf_op jit(solution)/shard_map/ppermute | solution.py:300
  3.4 1.5 %collective-permute-start = (f32[3,2048]{1,0:T(4,128)}, f32[3,2048]{1,0:T(4,128)S(1)}, u32[]{:S(2)}, u32[]{:S(2)}) collective-permute-start(f32[3,2048]{1,0:T(4,128)} %src_ref.1), channel_id=1, source_target_pairs={{0,4},{4,8},{8,12},{12,0},{1,5},{5,9},{9,13},{13,1},{2,6},{6,10},{... | collective-permute-start | bytes 73736 | tf_op jit(solution)/shard_map/ppermute | solution.py:292
  4.9 2.7 %collective-permute-start.2 = (f32[3,2048]{1,0:T(4,128)}, f32[3,2048]{1,0:T(4,128)S(1)}, u32[]{:S(2)}, u32[]{:S(2)}) collective-permute-start(f32[3,2048]{1,0:T(4,128)} %src_ref.1), channel_id=1, source_target_pairs={{0,8},{4,12},{8,0},{12,4},{1,9},{5,13},{9,1},{13,5},{2,10},{6,14},... | collective-permute-start | bytes 73736 | tf_op jit(solution)/shard_map/ppermute | solution.py:292
  8.4 1.4 %copy.9.near_ref = s32[16,8]{1,0:T(8,128)} copy(s32[16,8]{0,1:T(8,128)} %param.7) | data formatting | bytes 1024 | tf_op args[3]
  9.8 1.6 %collective-permute-done.4 = bf16[8,1024]{1,0:T(8,128)(2,1)S(1)} collective-permute-done((bf16[8,1024]{1,0:T(8,128)(2,1)S(1)}, bf16[8,1024]{1,0:T(8,128)(2,1)S(1)}, u32[]{:S(2)}, u32[]{:S(2)}) %collective-permute-start.4) | collective-permute-done | bytes 16416 | tf_op jit(solution)/shard_map/ppermute | solution.py:296
  11.4 6.4 %collective-permute-start.7 = (bf16[32,1024]{1,0:T(8,128)(2,1)S(1)}, bf16[32,1024]{1,0:T(8,128)(2,1)S(1)}, u32[]{:S(2)}, u32[]{:S(2)}) collective-permute-start(bf16[32,1024]{1,0:T(8,128)(2,1)S(1)} %get-tuple-element.21), channel_id=1, source_target_pairs={{0,128},{32,160},{64,192},{96,224},{128,0},{160,32},{192,64},{224,... | collective-permute-start | bytes 196616 | tf_op jit(solution)/shard_map/ppermute | solution.py:292
  17.8 1.5 %collective-permute-start.6 = (bf16[32,1024]{1,0:T(8,128)(2,1)S(1)}, bf16[32,1024]{1,0:T(8,128)(2,1)S(1)}, u32[]{:S(2)}, u32[]{:S(2)}) collective-permute-start(bf16[32,1024]{1,0:T(8,128)(2,1)S(1)} %get-tuple-element.21), channel_id=1, source_target_pairs={{0,64},{32,96},{64,128},{96,160},{128,192},{160,224},{192,0},{224,... | collective-permute-start | bytes 196616 | tf_op jit(solution)/shard_map/ppermute | solution.py:292
  19.3 2.7 %collective-permute-start.8 = (bf16[32,1024]{1,0:T(8,128)(2,1)S(1)}, bf16[32,1024]{1,0:T(8,128)(2,1)S(1)}, u32[]{:S(2)}, u32[]{:S(2)}) collective-permute-start(bf16[32,1024]{1,0:T(8,128)(2,1)S(1)} %get-tuple-element.21), channel_id=1, source_target_pairs={{0,192},{32,224},{64,0},{96,32},{128,64},{160,96},{192,128},{224,1... | collective-permute-start | bytes 196616 | tf_op jit(solution)/shard_map/ppermute | solution.py:292
  21.9 8.9 %kernel_tiles.3.refs_0_ = bf16[2048,2048]{1,0:T(8,128)(2,1)} custom-call(s32[4]{0:T(128)} %pad_add_fusion.at_ref, s32[16,8]{1,0:T(8,128)} %copy.9.near_ref, f32[3,8192]{1,0:T(4,128)} %tgt_ref.13, f32[3,2048]{1,0:T(4,128)} %src_ref.1), custom_call_target="tpu_custom_call" | custom-call | flops 8000000000 | bytes 8400000 | tf_op jit(solution)/shard_map/kernel_tiles/pallas_call | solution.py:75
  30.8 1.4 %collective-permute-start.1 = (f32[3,2048]{1,0:T(4,128)S(1)}, f32[3,2048]{1,0:T(4,128)S(1)}, u32[]{:S(2)}, u32[]{:S(2)}) collective-permute-start(f32[3,2048]{1,0:T(4,128)S(1)} %copy-done.14), channel_id=1, source_target_pairs={{0,12},{4,0},{8,4},{12,8},{1,13},{5,1},{9,5},{13,9},{2,14},{6,2},{... | collective-permute-start | bytes 73736 | tf_op jit(solution)/shard_map/ppermute | solution.py:292
  32.9 2.8 %collective-permute-start.10 = (bf16[4,32,1024]{2,1,0:T(8,128)(2,1)S(1)}, bf16[4,32,1024]{2,1,0:T(8,128)(2,1)S(1)}, u32[]{:S(2)}, u32[]{:S(2)}) collective-permute-start(bf16[4,32,1024]{2,1,0:T(8,128)(2,1)S(1)} %pad_maximum_fusion.refs_4_), channel_id=1, source_target_pairs={{0,12},{4,0},{8,4},{12,8},{1,13},{5,1},{9,5},{13,9},{2,14},{6,2},{... | collective-permute-start | bytes 786440 | tf_op jit(solution)/shard_map/ppermute | solution.py:292
  35.7 2.1 %collective-permute-start.9 = (bf16[4,32,1024]{2,1,0:T(8,128)(2,1)S(1)}, bf16[4,32,1024]{2,1,0:T(8,128)(2,1)S(1)}, u32[]{:S(2)}, u32[]{:S(2)}) collective-permute-start(bf16[4,32,1024]{2,1,0:T(8,128)(2,1)S(1)} %pad_maximum_fusion.refs_4_), channel_id=1, source_target_pairs={{0,4},{4,8},{8,12},{12,0},{1,5},{5,9},{9,13},{13,1},{2,6},{6,10},{... | collective-permute-start | bytes 786440 | tf_op jit(solution)/shard_map/ppermute | solution.py:292
  37.8 8.8 %kernel_tiles.5.refs_2_ = bf16[2048,2048]{1,0:T(8,128)(2,1)} custom-call(s32[4]{0:T(128)} %pad_add_fusion.at_ref, s32[16,8]{1,0:T(8,128)} %copy.9.near_ref, f32[3,8192]{1,0:T(4,128)} %tgt_ref.13, f32[3,2048]{1,0:T(4,128)} %copy-done.16), custom_call_target="tpu_custom_call" | custom-call | flops 8000000000 | bytes 8400000 | tf_op jit(solution)/shard_map/kernel_tiles/pallas_call | solution.py:75
  47.7 8.9 %kernel_tiles.4.refs_1_ = bf16[2048,2048]{1,0:T(8,128)(2,1)} custom-call(s32[4]{0:T(128)} %pad_add_fusion.at_ref, s32[16,8]{1,0:T(8,128)} %copy.9.near_ref, f32[3,8192]{1,0:T(4,128)} %tgt_ref.13, f32[3,2048]{1,0:T(4,128)} %copy-done.15), custom_call_target="tpu_custom_call" | custom-call | flops 8000000000 | bytes 8400000 | tf_op jit(solution)/shard_map/kernel_tiles/pallas_call | solution.py:75
  57.5 0.7 copy-done.7
  58.2 7.6 %leaf_sums.5 = f32[128,512]{1,0:T(8,128)} custom-call(s32[4]{0:T(128)} %pad_add_fusion.at_ref, s32[16,8]{1,0:T(8,128)} %copy.9.near_ref, f32[3,8192]{1,0:T(4,128)} %tgt_ref.13, bf16[2048,2048]{1,0:T(8,128)(2,1)} %kernel_tiles.3.refs_0_, bf16[2048,2048]{1,0:T(8,128)(2,1)} %kernel_tiles.4.refs_1_, bf16[2048,2048]{1,0:T(8,128)(2,1)} %kernel_tiles.5.refs_2_, ...), custom_call_target="tpu_custom_call" | custom-call | flops 4000000000 | bytes 9000000 | tf_op jit(solution)/shard_map/leaf_sums/pallas_call | solution.py:126
  65.9 1.6 %collective-permute-start.16 = (f32[128,512]{1,0:T(8,128)}, f32[128,512]{1,0:T(8,128)S(1)}, u32[]{:S(2)}, u32[]{:S(2)}) collective-permute-start(f32[128,512]{1,0:T(8,128)} %leaf_sums.5), channel_id=1, source_target_pairs={{0,1},{1,2},{2,3},{3,0},{4,5},{5,6},{6,7},{7,4},{8,9},{9,10},{10,1... | collective-permute-start | bytes 786440 | tf_op jit(solution)/shard_map/ppermute | solution.py:292
  67.4 7.6 %leaf_sums.6 = f32[128,512]{1,0:T(8,128)} custom-call(s32[4]{0:T(128)} %pad_add_fusion.at_ref, s32[16,8]{1,0:T(8,128)} %copy.9.near_ref, f32[3,8192]{1,0:T(4,128)} %tgt_ref.13, bf16[2048,2048]{1,0:T(8,128)(2,1)} %kernel_tiles.3.refs_0_, bf16[2048,2048]{1,0:T(8,128)(2,1)} %kernel_tiles.4.refs_1_, bf16[2048,2048]{1,0:T(8,128)(2,1)} %kernel_tiles.5.refs_2_, ...), custom_call_target="tpu_custom_call" | custom-call | flops 4000000000 | bytes 9000000 | tf_op jit(solution)/shard_map/leaf_sums/pallas_call | solution.py:126
  75.1 0.9 collective-permute-start.17
  76.0 7.6 %leaf_sums.7 = f32[128,512]{1,0:T(8,128)} custom-call(s32[4]{0:T(128)} %pad_add_fusion.at_ref, s32[16,8]{1,0:T(8,128)} %copy.9.near_ref, f32[3,8192]{1,0:T(4,128)} %tgt_ref.13, bf16[2048,2048]{1,0:T(8,128)(2,1)} %kernel_tiles.3.refs_0_, bf16[2048,2048]{1,0:T(8,128)(2,1)} %kernel_tiles.4.refs_1_, bf16[2048,2048]{1,0:T(8,128)(2,1)} %kernel_tiles.5.refs_2_, ...), custom_call_target="tpu_custom_call" | custom-call | flops 4000000000 | bytes 9000000 | tf_op jit(solution)/shard_map/leaf_sums/pallas_call | solution.py:126
  83.6 2.4 %collective-permute-start.18 = (f32[128,512]{1,0:T(8,128)}, f32[128,512]{1,0:T(8,128)S(1)}, u32[]{:S(2)}, u32[]{:S(2)}) collective-permute-start(f32[128,512]{1,0:T(8,128)} %leaf_sums.7), channel_id=1, source_target_pairs={{0,3},{1,0},{2,1},{3,2},{4,7},{5,4},{6,5},{7,6},{8,11},{9,8},{10,9... | collective-permute-start | bytes 786440 | tf_op jit(solution)/shard_map/ppermute | solution.py:292
  86.0 7.8 %leaf_sums.4.a_ref = f32[128,512]{1,0:T(8,128)} custom-call(s32[4]{0:T(128)} %pad_add_fusion.at_ref, s32[16,8]{1,0:T(8,128)} %copy.9.near_ref, f32[3,8192]{1,0:T(4,128)} %tgt_ref.13, bf16[2048,2048]{1,0:T(8,128)(2,1)} %kernel_tiles.3.refs_0_, bf16[2048,2048]{1,0:T(8,128)(2,1)} %kernel_tiles.4.refs_1_, bf16[2048,2048]{1,0:T(8,128)(2,1)} %kernel_tiles.5.refs_2_, ...), custom_call_target="tpu_custom_call" | custom-call | flops 4000000000 | bytes 9000000 | tf_op jit(solution)/shard_map/leaf_sums/pallas_call | solution.py:126
  94.6 0.7 copy-done.11
  95.3 8.7 %leaf_node.1 = (f32[128,512]{1,0:T(8,128)}, f32[128,128]{1,0:T(8,128)}, f32[128,128]{1,0:T(8,128)}, f32[128,128]{1,0:T(8,128)}) custom-call(s32[4]{0:T(128)} %pad_add_fusion.at_ref, f32[128,512]{1,0:T(8,128)} %leaf_sums.4.a_ref, f32[128,512]{1,0:T(8,128)} %copy-done.9, f32[128,512]{1,0:T(8,128)} %copy-done.10, f32[128,512]{1,0:T(8,128)} %copy-done.11), custom_call_target="tpu_custom_call" | custom-call | tf_op jit(solution)/shard_map/leaf_node/pallas_call | solution.py:261
  104.0 1.3 %collective-permute-start.19 = (f32[128,128]{1,0:T(8,128)}, f32[128,128]{1,0:T(8,128)S(1)}, u32[]{:S(2)}, u32[]{:S(2)}) collective-permute-start(f32[128,128]{1,0:T(8,128)} %get-tuple-element.15.a_ref), channel_id=1, source_target_pairs={{0,1},{1,0},{2,3},{3,2},{4,5},{5,4},{6,7},{7,6},{8,9},{9,8},{10,11... | collective-permute-start | bytes 196616 | tf_op jit(solution)/shard_map/ppermute | solution.py:296
  105.3 3.2 %collective-permute-done.19.b_ref = f32[128,128]{1,0:T(8,128)S(1)} collective-permute-done((f32[128,128]{1,0:T(8,128)}, f32[128,128]{1,0:T(8,128)S(1)}, u32[]{:S(2)}, u32[]{:S(2)}) %collective-permute-start.19) | collective-permute-done | bytes 65568 | tf_op jit(solution)/shard_map/ppermute | solution.py:296
  109.1 7.8 %pair_node.1 = (f32[128,128]{1,0:T(8,128)}, f32[128,128]{1,0:T(8,128)}, f32[128,128]{1,0:T(8,128)}) custom-call(f32[128,128]{1,0:T(8,128)} %get-tuple-element.15.a_ref, f32[128,128]{1,0:T(8,128)} %copy-done.13), custom_call_target="tpu_custom_call" | custom-call | tf_op jit(solution)/shard_map/pair_node/pallas_call | solution.py:271
  116.9 0.9 collective-permute-start.20
  117.9 2.8 %carry.1 = (f32[512,128]{1,0:T(8,128)}, f32[512,128]{1,0:T(8,128)}) custom-call(f32[128,512]{1,0:T(8,128)} %get-tuple-element.11.z_ref, f32[128,128]{1,0:T(8,128)} %get-tuple-element.12.inv_ref, f32[128,128]{1,0:T(8,128)} %get-tuple-element.13.proj_ref), custom_call_target="tpu_custom_call" | custom-call | tf_op jit(solution)/shard_map/carry/pallas_call | solution.py:275
  120.6 2.7 %carry2.1.z_ref = f32[512,128]{1,0:T(8,128)} custom-call(f32[512,128]{1,0:T(8,128)} %get-tuple-element.17.z_ref, f32[128,128]{1,0:T(8,128)} %get-tuple-element.18.inv_ref, f32[128,128]{1,0:T(8,128)} %get-tuple-element.19.proj_ref), custom_call_target="tpu_custom_call" | custom-call | tf_op jit(solution)/shard_map/carry2/pallas_call | solution.py:279
  123.9 8.1 %last_node.1 = f32[512,128]{1,0:T(8,128)} custom-call(f32[128,128]{1,0:T(8,128)} %get-tuple-element.16.a_ref, f32[128,128]{1,0:T(8,128)} %copy-done.12, f32[512,128]{1,0:T(8,128)} %carry2.1.z_ref), custom_call_target="tpu_custom_call" | custom-call | tf_op jit(solution)/shard_map/last_node/pallas_call | solution.py:283
  (63 shorter events, 6.1 us)
Async XLA Ops:
  1.4 10.0 %collective-permute-start.5 = (bf16[8,1024]{1,0:T(8,128)(2,1)S(1)}, bf16[8,1024]{1,0:T(8,128)(2,1)S(1)}, u32[]{:S(2)}, u32[]{:S(2)}) collective-permute-start(bf16[8,1024]{1,0:T(8,128)(2,1)S(1)} %get-tuple-element.23), channel_id=1, source_target_pairs={{0,48},{16,32},{32,16},{48,0},{64,112},{80,96},{96,80},{112,64},{1... | collective-permute-start | bytes 49160 | tf_op jit(solution)/shard_map/ppermute | solution.py:300
  2.7 7.0 %collective-permute-start.3 = (bf16[8,1024]{1,0:T(8,128)(2,1)S(1)}, bf16[8,1024]{1,0:T(8,128)(2,1)S(1)}, u32[]{:S(2)}, u32[]{:S(2)}) collective-permute-start(bf16[8,1024]{1,0:T(8,128)(2,1)S(1)} %get-tuple-element.23), channel_id=1, source_target_pairs={{0,16},{16,0},{1,17},{17,1},{2,18},{18,2},{3,19},{19,3},{4,20},{20... | collective-permute-start | bytes 49160 | tf_op jit(solution)/shard_map/ppermute | solution.py:296
  3.4 43.2 %collective-permute-start = (f32[3,2048]{1,0:T(4,128)}, f32[3,2048]{1,0:T(4,128)S(1)}, u32[]{:S(2)}, u32[]{:S(2)}) collective-permute-start(f32[3,2048]{1,0:T(4,128)} %src_ref.1), channel_id=1, source_target_pairs={{0,4},{4,8},{8,12},{12,0},{1,5},{5,9},{9,13},{13,1},{2,6},{6,10},{... | collective-permute-start | bytes 73736 | tf_op jit(solution)/shard_map/ppermute | solution.py:292
  4.9 51.7 %collective-permute-start.2 = (f32[3,2048]{1,0:T(4,128)}, f32[3,2048]{1,0:T(4,128)S(1)}, u32[]{:S(2)}, u32[]{:S(2)}) collective-permute-start(f32[3,2048]{1,0:T(4,128)} %src_ref.1), channel_id=1, source_target_pairs={{0,8},{4,12},{8,0},{12,4},{1,9},{5,13},{9,1},{13,5},{2,10},{6,14},... | collective-permute-start | bytes 73736 | tf_op jit(solution)/shard_map/ppermute | solution.py:292
  7.6 3.7 %collective-permute-start.4 = (bf16[8,1024]{1,0:T(8,128)(2,1)S(1)}, bf16[8,1024]{1,0:T(8,128)(2,1)S(1)}, u32[]{:S(2)}, u32[]{:S(2)}) collective-permute-start(bf16[8,1024]{1,0:T(8,128)(2,1)S(1)} %get-tuple-element.22), channel_id=1, source_target_pairs={{0,32},{32,0},{64,96},{96,64},{128,160},{160,128},{192,224},{224,1... | collective-permute-start | bytes 49160 | tf_op jit(solution)/shard_map/ppermute | solution.py:296
  11.4 19.4 %copy-start.14 = (f32[3,2048]{1,0:T(4,128)S(1)}, f32[3,2048]{1,0:T(4,128)}, u32[]{:S(2)}) copy-start(f32[3,2048]{1,0:T(4,128)} %src_ref.1) | copy-start | bytes 73732
  11.4 19.4 %collective-permute-start.7 = (bf16[32,1024]{1,0:T(8,128)(2,1)S(1)}, bf16[32,1024]{1,0:T(8,128)(2,1)S(1)}, u32[]{:S(2)}, u32[]{:S(2)}) collective-permute-start(bf16[32,1024]{1,0:T(8,128)(2,1)S(1)} %get-tuple-element.21), channel_id=1, source_target_pairs={{0,128},{32,160},{64,192},{96,224},{128,0},{160,32},{192,64},{224,... | collective-permute-start | bytes 196616 | tf_op jit(solution)/shard_map/ppermute | solution.py:292
  17.8 14.5 %collective-permute-start.6 = (bf16[32,1024]{1,0:T(8,128)(2,1)S(1)}, bf16[32,1024]{1,0:T(8,128)(2,1)S(1)}, u32[]{:S(2)}, u32[]{:S(2)}) collective-permute-start(bf16[32,1024]{1,0:T(8,128)(2,1)S(1)} %get-tuple-element.21), channel_id=1, source_target_pairs={{0,64},{32,96},{64,128},{96,160},{128,192},{160,224},{192,0},{224,... | collective-permute-start | bytes 196616 | tf_op jit(solution)/shard_map/ppermute | solution.py:292
  19.3 13.0 %collective-permute-start.8 = (bf16[32,1024]{1,0:T(8,128)(2,1)S(1)}, bf16[32,1024]{1,0:T(8,128)(2,1)S(1)}, u32[]{:S(2)}, u32[]{:S(2)}) collective-permute-start(bf16[32,1024]{1,0:T(8,128)(2,1)S(1)} %get-tuple-element.21), channel_id=1, source_target_pairs={{0,192},{32,224},{64,0},{96,32},{128,64},{160,96},{192,128},{224,1... | collective-permute-start | bytes 196616 | tf_op jit(solution)/shard_map/ppermute | solution.py:292
  30.8 4.8 %collective-permute-start.1 = (f32[3,2048]{1,0:T(4,128)S(1)}, f32[3,2048]{1,0:T(4,128)S(1)}, u32[]{:S(2)}, u32[]{:S(2)}) collective-permute-start(f32[3,2048]{1,0:T(4,128)S(1)} %copy-done.14), channel_id=1, source_target_pairs={{0,12},{4,0},{8,4},{12,8},{1,13},{5,1},{9,5},{13,9},{2,14},{6,2},{... | collective-permute-start | bytes 73736 | tf_op jit(solution)/shard_map/ppermute | solution.py:292
  32.3 14.3 %copy-start = (bf16[4,32,1024]{2,1,0:T(8,128)(2,1)}, bf16[4,32,1024]{2,1,0:T(8,128)(2,1)S(1)}, u32[]{:S(2)}) copy-start(bf16[4,32,1024]{2,1,0:T(8,128)(2,1)S(1)} %pad_maximum_fusion.refs_4_) | copy-start | bytes 786436
  32.3 14.4 %collective-permute-start.11 = (bf16[4,32,1024]{2,1,0:T(8,128)(2,1)S(1)}, bf16[4,32,1024]{2,1,0:T(8,128)(2,1)S(1)}, u32[]{:S(2)}, u32[]{:S(2)}) collective-permute-start(bf16[4,32,1024]{2,1,0:T(8,128)(2,1)S(1)} %pad_maximum_fusion.refs_4_), channel_id=1, source_target_pairs={{0,8},{4,12},{8,0},{12,4},{1,9},{5,13},{9,1},{13,5},{2,10},{6,14},... | collective-permute-start | bytes 786440 | tf_op jit(solution)/shard_map/ppermute | solution.py:292
  32.9 14.3 %collective-permute-start.10 = (bf16[4,32,1024]{2,1,0:T(8,128)(2,1)S(1)}, bf16[4,32,1024]{2,1,0:T(8,128)(2,1)S(1)}, u32[]{:S(2)}, u32[]{:S(2)}) collective-permute-start(bf16[4,32,1024]{2,1,0:T(8,128)(2,1)S(1)} %pad_maximum_fusion.refs_4_), channel_id=1, source_target_pairs={{0,12},{4,0},{8,4},{12,8},{1,13},{5,1},{9,5},{13,9},{2,14},{6,2},{... | collective-permute-start | bytes 786440 | tf_op jit(solution)/shard_map/ppermute | solution.py:292
  35.7 2.1 %copy-start.16 = (f32[3,2048]{1,0:T(4,128)}, f32[3,2048]{1,0:T(4,128)S(1)}, u32[]{:S(2)}) copy-start(f32[3,2048]{1,0:T(4,128)S(1)} %collective-permute-done.1.src_ref) | copy-start | bytes 73732
  35.7 11.8 %collective-permute-start.9 = (bf16[4,32,1024]{2,1,0:T(8,128)(2,1)S(1)}, bf16[4,32,1024]{2,1,0:T(8,128)(2,1)S(1)}, u32[]{:S(2)}, u32[]{:S(2)}) collective-permute-start(bf16[4,32,1024]{2,1,0:T(8,128)(2,1)S(1)} %pad_maximum_fusion.refs_4_), channel_id=1, source_target_pairs={{0,4},{4,8},{8,12},{12,0},{1,5},{5,9},{9,13},{13,1},{2,6},{6,10},{... | collective-permute-start | bytes 786440 | tf_op jit(solution)/shard_map/ppermute | solution.py:292
  46.6 1.1 copy-start.15
  46.6 10.0 %collective-permute-start.12 = (bf16[4,32,1024]{2,1,0:T(8,128)(2,1)S(1)}, bf16[4,32,1024]{2,1,0:T(8,128)(2,1)S(1)}, u32[]{:S(2)}, u32[]{:S(2)}) collective-permute-start(bf16[4,32,1024]{2,1,0:T(8,128)(2,1)S(1)} %pad_maximum_fusion.refs_4_), channel_id=1, source_target_pairs={{0,16},{16,0},{1,17},{17,1},{2,18},{18,2},{3,19},{19,3},{4,20},{20... | collective-permute-start | bytes 786440 | tf_op jit(solution)/shard_map/ppermute | solution.py:296
  46.7 9.9 %copy-start.1 = (bf16[4,32,1024]{2,1,0:T(8,128)(2,1)}, bf16[4,32,1024]{2,1,0:T(8,128)(2,1)S(1)}, u32[]{:S(2)}) copy-start(bf16[4,32,1024]{2,1,0:T(8,128)(2,1)S(1)} %collective-permute-done.11.refs_7_) | copy-start | bytes 786436
  46.7 9.9 %collective-permute-start.15 = (bf16[4,32,1024]{2,1,0:T(8,128)(2,1)S(1)}, bf16[4,32,1024]{2,1,0:T(8,128)(2,1)S(1)}, u32[]{:S(2)}, u32[]{:S(2)}) collective-permute-start(bf16[4,32,1024]{2,1,0:T(8,128)(2,1)S(1)} %collective-permute-done.11.refs_7_), channel_id=1, source_target_pairs={{0,16},{16,0},{1,17},{17,1},{2,18},{18,2},{3,19},{19,3},{4,20},{20... | collective-permute-start | bytes 786440 | tf_op jit(solution)/shard_map/ppermute | solution.py:296
  47.2 9.4 %copy-start.2 = (bf16[4,32,1024]{2,1,0:T(8,128)(2,1)}, bf16[4,32,1024]{2,1,0:T(8,128)(2,1)S(1)}, u32[]{:S(2)}) copy-start(bf16[4,32,1024]{2,1,0:T(8,128)(2,1)S(1)} %collective-permute-done.10.refs_6_) | copy-start | bytes 786436
  47.2 9.5 %collective-permute-start.14 = (bf16[4,32,1024]{2,1,0:T(8,128)(2,1)S(1)}, bf16[4,32,1024]{2,1,0:T(8,128)(2,1)S(1)}, u32[]{:S(2)}, u32[]{:S(2)}) collective-permute-start(bf16[4,32,1024]{2,1,0:T(8,128)(2,1)S(1)} %collective-permute-done.10.refs_6_), channel_id=1, source_target_pairs={{0,16},{16,0},{1,17},{17,1},{2,18},{18,2},{3,19},{19,3},{4,20},{20... | collective-permute-start | bytes 786440 | tf_op jit(solution)/shard_map/ppermute | solution.py:296
  47.5 9.1 %copy-start.3 = (bf16[4,32,1024]{2,1,0:T(8,128)(2,1)}, bf16[4,32,1024]{2,1,0:T(8,128)(2,1)S(1)}, u32[]{:S(2)}) copy-start(bf16[4,32,1024]{2,1,0:T(8,128)(2,1)S(1)} %collective-permute-done.9.refs_5_) | copy-start | bytes 786436
  47.5 9.2 %collective-permute-start.13 = (bf16[4,32,1024]{2,1,0:T(8,128)(2,1)S(1)}, bf16[4,32,1024]{2,1,0:T(8,128)(2,1)S(1)}, u32[]{:S(2)}, u32[]{:S(2)}) collective-permute-start(bf16[4,32,1024]{2,1,0:T(8,128)(2,1)S(1)} %collective-permute-done.9.refs_5_), channel_id=1, source_target_pairs={{0,16},{16,0},{1,17},{17,1},{2,18},{18,2},{3,19},{19,3},{4,20},{20... | collective-permute-start | bytes 786440 | tf_op jit(solution)/shard_map/ppermute | solution.py:296
  56.6 0.7 copy-start.4
  56.6 0.8 copy-start.5
  56.7 0.9 copy-start.6
  65.9 27.9 %collective-permute-start.16 = (f32[128,512]{1,0:T(8,128)}, f32[128,512]{1,0:T(8,128)S(1)}, u32[]{:S(2)}, u32[]{:S(2)}) collective-permute-start(f32[128,512]{1,0:T(8,128)} %leaf_sums.5), channel_id=1, source_target_pairs={{0,1},{1,2},{2,3},{3,0},{4,5},{5,6},{6,7},{7,4},{8,9},{9,10},{10,1... | collective-permute-start | bytes 786440 | tf_op jit(solution)/shard_map/ppermute | solution.py:292
  75.1 18.7 %collective-permute-start.17 = (f32[128,512]{1,0:T(8,128)}, f32[128,512]{1,0:T(8,128)S(1)}, u32[]{:S(2)}, u32[]{:S(2)}) collective-permute-start(f32[128,512]{1,0:T(8,128)} %leaf_sums.6), channel_id=1, source_target_pairs={{0,2},{1,3},{2,0},{3,1},{4,6},{5,7},{6,4},{7,5},{8,10},{9,11},{10,... | collective-permute-start | bytes 786440 | tf_op jit(solution)/shard_map/ppermute | solution.py:292
  83.6 10.2 %collective-permute-start.18 = (f32[128,512]{1,0:T(8,128)}, f32[128,512]{1,0:T(8,128)S(1)}, u32[]{:S(2)}, u32[]{:S(2)}) collective-permute-start(f32[128,512]{1,0:T(8,128)} %leaf_sums.7), channel_id=1, source_target_pairs={{0,3},{1,0},{2,1},{3,2},{4,7},{5,4},{6,5},{7,6},{8,11},{9,8},{10,9... | collective-permute-start | bytes 786440 | tf_op jit(solution)/shard_map/ppermute | solution.py:292
  93.8 0.8 copy-start.10
  104.0 4.5 %collective-permute-start.19 = (f32[128,128]{1,0:T(8,128)}, f32[128,128]{1,0:T(8,128)S(1)}, u32[]{:S(2)}, u32[]{:S(2)}) collective-permute-start(f32[128,128]{1,0:T(8,128)} %get-tuple-element.15.a_ref), channel_id=1, source_target_pairs={{0,1},{1,0},{2,3},{3,2},{4,5},{5,4},{6,7},{7,6},{8,9},{9,8},{10,11... | collective-permute-start | bytes 196616 | tf_op jit(solution)/shard_map/ppermute | solution.py:296
  116.9 6.4 %collective-permute-start.20 = (f32[128,128]{1,0:T(8,128)}, f32[128,128]{1,0:T(8,128)S(1)}, u32[]{:S(2)}, u32[]{:S(2)}) collective-permute-start(f32[128,128]{1,0:T(8,128)} %get-tuple-element.16.a_ref), channel_id=1, source_target_pairs={{0,2},{1,3},{2,0},{3,1},{4,6},{5,7},{6,4},{7,5},{8,10},{9,11},{10,... | collective-permute-start | bytes 196616 | tf_op jit(solution)/shard_map/ppermute | solution.py:296
  (6 other events, 4.0 us)

commit v4 on v3

--- a/solution.py
+++ b/solution.py
@@ -96,47 +96,43 @@
     srcs, refs = refs[:nf], refs[nf:]
     mine, refs = refs[:ns + nf], refs[ns + nf:]
     other, refs = refs[:ns + nf], refs[ns + nf:]
-    out_ref, tpts_ref, spts_ref = refs
-    i = pl.program_id(0)
+    out_ref, held_ref, tpts_ref, spts_ref, sems = refs
     leaf = jnp.bitwise_and(at_ref[3] + turn, 3)
+    lanes = pl.ds(pl.multiple_of(leaf * LEAF, LEAF), LEAF)
+    copies = [pltpu.make_async_copy(tiles[n].at[:, lanes], held_ref.at[n], sems.at[n]) for n in range(ns)]
+    for copy in copies:
+        copy.start()
     cols, centre = target_features(tgt_ref, tpts_ref, at_ref[2] * 4 + leaf)
     spts_ref[...] = jnp.zeros_like(spts_ref)
-    total = jnp.zeros((128, LEAF), F32)
+    for n in range(nf):
+        for i in range(4):
+            held_ref[ns + n, i * LEAF:(i + 1) * LEAF, :] = tile_of(
+                fused[n], i, leaf, at_ref, near_ref, srcs[n], spts_ref.at[4 * n + i], cols, centre)
+    for copy in copies:
+        copy.wait()
+    total = None
     for n in range(ns + nf):
-        rows = jnp.where(i < 2, mine[n][...], other[n][...]).reshape(128, LEAF)
-        if n < ns:
-            tile = tiles[n][...]
-        else:
-            tile = tile_of(fused[n - ns], i, leaf, at_ref, near_ref, srcs[n - ns], spts_ref.at[n - ns], cols, centre)
-        total += jnp.dot(rows, tile, preferred_element_type=F32)
-
-    @pl.when(i == 0)
-    def _():
-        out_ref[...] = total
-
-    @pl.when(i != 0)
-    def _():
-        out_ref[...] += total
+        rows = jnp.concatenate([mine[n][...].reshape(128, 1024), other[n][...].reshape(128, 1024)], axis=1)
+        term = jnp.dot(rows, held_ref[n], preferred_element_type=F32)
+        total = term if total is None else total + term
+    out_ref[...] = total
 
 
 def leaf_sums(turn, at, near, targets, tiles, sources, mine, other):
     stored, fused = sorted(tiles), sorted(sources)
     order = stored + fused
-    width = len(fused)
+    vm = pl.BlockSpec(memory_space=pltpu.VMEM)
+    sm = pl.BlockSpec(memory_space=pltpu.SMEM)
     return pl.pallas_call(
         functools.partial(sums_body, turn, stored, fused),
         out_shape=jax.ShapeDtypeStruct((128, LEAF), F32),
-        grid_spec=pltpu.PrefetchScalarGridSpec(
-            num_scalar_prefetch=2,
-            grid=(4,),
-            in_specs=[pl.BlockSpec((3, targets.shape[1]), lambda i, a, n: (0, 0))]
-            + [pl.BlockSpec((LEAF, LEAF), lambda i, a, n: (i, jnp.bitwise_and(a[3] + turn, 3)))] * len(stored)
-            + [pl.BlockSpec((3, 2048), lambda i, a, n: (0, 0))] * width
-            + [pl.BlockSpec((4, 32, LEAF), lambda i, a, n: (0, 0, jnp.minimum(i, 1)))] * 4
-            + [pl.BlockSpec((4, 32, LEAF), lambda i, a, n: (0, 0, jnp.maximum(i - 2, 0)))] * 4,
-            out_specs=pl.BlockSpec((128, LEAF), lambda i, a, n: (0, 0)),
-            scratch_shapes=[pltpu.VMEM((8, LEAF), F32), pltpu.VMEM((width, 8, LEAF), F32)],
-        ),
+        in_specs=[sm, sm, vm] + [pl.BlockSpec(memory_space=pl.ANY)] * len(stored) + [vm] * (len(fused) + 8),
+        scratch_shapes=[
+            pltpu.VMEM((4, 2048, LEAF), BF),
+            pltpu.VMEM((8, LEAF), F32),
+            pltpu.VMEM((4 * len(fused), 8, LEAF), F32),
+            pltpu.SemaphoreType.DMA((len(stored),)),
+        ],
         cost_estimate=pl.CostEstimate(flops=4_000_000_000, bytes_accessed=9_000_000, transcendentals=1_000_000),
         name="leaf_sums",
     )(at, near, targets, *[tiles[q] for q in stored], *[sources[q] for q in fused],
@@ -300,7 +296,7 @@
     return lax.ppermute(x, ROW, [(i, i ^ 3) for i in range(16)])
 
 
-def own_half(samples, core):
+def own_pair(samples, core):
     flat = samples.T
     half = flat.shape[1] // 2
     mine = lax.dynamic_slice_in_dim(flat, core * half, half, 1)
@@ -308,19 +304,27 @@
     across, up, cross = crossed(away, "c", 1), crossed(mine, "z", 1), diagonal(away)
     first = jnp.where(core == 0, jnp.concatenate([mine, across]), jnp.concatenate([across, mine]))
     second = jnp.where(core == 0, jnp.concatenate([up, cross]), jnp.concatenate([cross, up]))
-    pair = jnp.concatenate([first, second])
-    return jnp.stack([pair] + [moved(pair, "z", 2 * k) for k in (1, 2, 3)])
+    return jnp.concatenate([first, second])
+
+
+def after(x, *work):
+    return lax.optimization_barrier((x, *work))[0]
 
 
 def per_device(targets, sources, samples, near):
     at = jnp.stack([lax.axis_index(a) for a in ("z", "c", "x", "y")]).astype(jnp.int32)
-    block = own_half(samples, at[1])
     srcs = [sources] + [moved(sources, "x", q) for q in (1, 2, 3)]
+    pair = own_pair(samples, at[1])
+    tiles = {0: kernel_tiles(0, at, near, targets, sources)}
+    pair = after(pair, tiles[0])
+    block = jnp.stack([pair] + [moved(pair, "z", 2 * k) for k in (1, 2, 3)])
+    tiles[1] = kernel_tiles(1, at, near, targets, srcs[1])
+    block = after(block, tiles[1])
     mine = [block] + [moved(block, "x", q) for q in (1, 2, 3)]
+    tiles[3] = kernel_tiles(3, at, near, targets, srcs[3])
+    mine = [block] + [after(b, tiles[3]) for b in mine[1:]]
     other = [crossed(b, "c", 1) for b in mine]
-    stored = (0, 1, 3)
-    tiles = {q: kernel_tiles(q, at, near, targets, srcs[q]) for q in stored}
-    fused = {q: srcs[q] for q in range(4) if q not in stored}
+    fused = {2: srcs[2]}
     sums = {}
     for d in (2, 1, 3, 0):
         part = leaf_sums(d, at, near, targets, tiles, fused, mine, other)
@@ -328,7 +332,7 @@
     far_sample, inv0, proj0, sq0 = leaf_node(at, [sums[d] for d in range(4)])
     sib = crossed(sq0, "y", 1)
     leaf_basis, carried = carry(far_sample, inv0, proj0)
-    inv1, proj1, sq1 = pair_node(sq0, sib)
+    inv1, proj1, sq1 = pair_node(sq0, after(sib, carried))
     cousin = crossed(sq1, "y", 2)
     carried = carry2(carried, inv1, proj1)
     nested = last_node(sq1, cousin, carried)

time: 133 us -> 130 us (0.977)
  Pallas kernels: 87.3 us -> 82.9 us
  starting transfers between devices: 32.1 us -> 29.8 us
  waiting for transfers between devices: 4.81 us -> 6.55 us
    pallas_call x4, Pallas kernels: 30.6 us -> 26.3 us  [leaf_sums(): pl.pallas_call(functools.partial(sums_body, turn, stored, fused), out_sha...]
    ppermute x12, waiting for transfers between devices: 0.03 us -> 3.71 us  [moved(): return lax.ppermute(x, axis, [(i, (i + by) % size) for i in range(size)])]
    ppermute x12, starting transfers between devices: 26.6 us -> 24.5 us  [moved(): return lax.ppermute(x, axis, [(i, (i + by) % size) for i in range(size)])]
    ppermute x8, waiting for transfers between devices: 4.78 us -> 2.84 us  [crossed(): lax.ppermute(x, axis, [(i, i ^ bit) for i in range(lax.axis_size(axis))])]
  transfers between devices with their start and end apart: 21 -> 21, of which waited for: 2 -> 3; matrix products, arithmetic and copies ran while one was open for 2% -> 2% of each run, Pallas kernels for 42% -> 40%
where the time goes in v4:
time: 130 us; the launch traced here: 128 us
  Pallas kernels  82.9 us (64%)
  starting transfers between devices  29.8 us (23%)
  local copies, waits for them, and re-layouts  7.56 us (6%)
  waiting for transfers between devices  6.55 us (5%)
    pallas_call x3, Pallas kernels, kernel_tiles(): pl.pallas_call(functools.partial(tiles_body, q), out_shape=jax.ShapeDtype...  26.5 us
    pallas_call x4, Pallas kernels, leaf_sums(): pl.pallas_call(functools.partial(sums_body, turn, stored, fused), out_sha...  26.3 us
    ppermute x12, starting transfers between devices, moved(): return lax.ppermute(x, axis, [(i, (i + by) % size) for i in range(size)])  24.5 us
    pallas_call x1, Pallas kernels, leaf_node(): pl.pallas_call(leaf_body, out_shape=(sds(128, LEAF),) + (sds(128, 128),)...  8.68 us
    pallas_call x1, Pallas kernels, last_node(): pl.pallas_call(last_body, out_shape=sds(512, 128), scratch_shapes=SCR, na...  8.13 us
    pallas_call x1, Pallas kernels, pair_node(): pl.pallas_call(node_body, out_shape=(sds(128, 128),) * 3, scratch_shapes=...  7.82 us
    unnamed x35, local copies, waits for them, and re-layouts  6.82 us
    ppermute x8, starting transfers between devices, crossed(): lax.ppermute(x, axis, [(i, i ^ bit) for i in range(lax.axis_size(axis))])  3.97 us
  transfers between devices with their start and end apart: 21, of which 3 were waited for; matrix products, arithmetic and copies ran while one was open for 2% of the time, Pallas kernels for 40%

profile of v4, /device:TPU:8, one launch (start us, length us, event | category | flops | bytes accessed | tf_op | source)
XLA Modules:
  0.0 128.4 jit_solution(199628884061216638)
XLA Ops:
  0.6 0.7 dynamic-slice_bitcast_fusion.1
  1.4 1.4 %collective-permute-start.5 = (bf16[8,1024]{1,0:T(8,128)(2,1)S(1)}, bf16[8,1024]{1,0:T(8,128)(2,1)S(1)}, u32[]{:S(2)}, u32[]{:S(2)}) collective-permute-start(bf16[8,1024]{1,0:T(8,128)(2,1)S(1)} %get-tuple-element.33), channel_id=1, source_target_pairs={{0,48},{16,32},{32,16},{48,0},{64,112},{80,96},{96,80},{112,64},{1... | collective-permute-start | bytes 49160 | tf_op jit(solution)/shard_map/ppermute | solution.py:296
  3.4 1.5 %collective-permute-start = (f32[3,2048]{1,0:T(4,128)}, f32[3,2048]{1,0:T(4,128)S(1)}, u32[]{:S(2)}, u32[]{:S(2)}) collective-permute-start(f32[3,2048]{1,0:T(4,128)} %src_ref.1), channel_id=1, source_target_pairs={{0,4},{4,8},{8,12},{12,0},{1,5},{5,9},{9,13},{13,1},{2,6},{6,10},{... | collective-permute-start | bytes 73736 | tf_op jit(solution)/shard_map/ppermute | solution.py:288
  4.9 1.7 %collective-permute-start.1 = (f32[3,2048]{1,0:T(4,128)}, f32[3,2048]{1,0:T(4,128)S(1)}, u32[]{:S(2)}, u32[]{:S(2)}) collective-permute-start(f32[3,2048]{1,0:T(4,128)} %src_ref.1), channel_id=1, source_target_pairs={{0,12},{4,0},{8,4},{12,8},{1,13},{5,1},{9,5},{13,9},{2,14},{6,2},{... | collective-permute-start | bytes 73736 | tf_op jit(solution)/shard_map/ppermute | solution.py:288
  6.8 1.4 %copy.9.near_ref = s32[16,8]{1,0:T(8,128)} copy(s32[16,8]{0,1:T(8,128)} %param.7) | data formatting | bytes 1024 | tf_op args[3]
  8.8 8.8 %kernel_tiles.3.refs_0_ = bf16[2048,2048]{1,0:T(8,128)(2,1)} custom-call(s32[4]{0:T(128)} %pad_add_fusion.at_ref, s32[16,8]{1,0:T(8,128)} %copy.9.near_ref, f32[3,8192]{1,0:T(4,128)} %tgt_ref.13, f32[3,2048]{1,0:T(4,128)} %src_ref.1), custom_call_target="tpu_custom_call" | custom-call | flops 8000000000 | bytes 8400000 | tf_op jit(solution)/shard_map/kernel_tiles/pallas_call | solution.py:75
  17.7 6.4 %collective-permute-start.8 = (bf16[32,1024]{1,0:T(8,128)(2,1)S(1)}, bf16[32,1024]{1,0:T(8,128)(2,1)S(1)}, u32[]{:S(2)}, u32[]{:S(2)}) collective-permute-start(bf16[32,1024]{1,0:T(8,128)(2,1)S(1)} %pad_maximum_fusion.1), channel_id=1, source_target_pairs={{0,192},{32,224},{64,0},{96,32},{128,64},{160,96},{192,128},{224,1... | collective-permute-start | bytes 196616 | tf_op jit(solution)/shard_map/ppermute | solution.py:288
  24.0 1.0 collective-permute-start.7
  25.0 2.8 %collective-permute-start.6 = (bf16[32,1024]{1,0:T(8,128)(2,1)S(1)}, bf16[32,1024]{1,0:T(8,128)(2,1)S(1)}, u32[]{:S(2)}, u32[]{:S(2)}) collective-permute-start(bf16[32,1024]{1,0:T(8,128)(2,1)S(1)} %pad_maximum_fusion.1), channel_id=1, source_target_pairs={{0,64},{32,96},{64,128},{96,160},{128,192},{160,224},{192,0},{224,... | collective-permute-start | bytes 196616 | tf_op jit(solution)/shard_map/ppermute | solution.py:288
  28.5 8.8 %kernel_tiles.4.refs_1_ = bf16[2048,2048]{1,0:T(8,128)(2,1)} custom-call(s32[4]{0:T(128)} %pad_add_fusion.at_ref, s32[16,8]{1,0:T(8,128)} %copy.9.near_ref, f32[3,8192]{1,0:T(4,128)} %tgt_ref.13, f32[3,2048]{1,0:T(4,128)} %copy-done.16), custom_call_target="tpu_custom_call" | custom-call | flops 8000000000 | bytes 8400000 | tf_op jit(solution)/shard_map/kernel_tiles/pallas_call | solution.py:75
  37.4 1.9 %collective-permute-start.11 = (bf16[4,32,1024]{2,1,0:T(8,128)(2,1)S(1)}, bf16[4,32,1024]{2,1,0:T(8,128)(2,1)S(1)}, u32[]{:S(2)}, u32[]{:S(2)}) collective-permute-start(bf16[4,32,1024]{2,1,0:T(8,128)(2,1)S(1)} %pad_maximum_fusion.refs_4_), channel_id=1, source_target_pairs={{0,8},{4,12},{8,0},{12,4},{1,9},{5,13},{9,1},{13,5},{2,10},{6,14},... | collective-permute-start | bytes 786440 | tf_op jit(solution)/shard_map/ppermute | solution.py:288
  39.2 1.1 collective-permute-start.10
  40.4 0.9 collective-permute-start.9
  41.9 8.9 %kernel_tiles.5.refs_2_ = bf16[2048,2048]{1,0:T(8,128)(2,1)} custom-call(s32[4]{0:T(128)} %pad_add_fusion.at_ref, s32[16,8]{1,0:T(8,128)} %copy.9.near_ref, f32[3,8192]{1,0:T(4,128)} %tgt_ref.13, f32[3,2048]{1,0:T(4,128)} %copy-done.15), custom_call_target="tpu_custom_call" | custom-call | flops 8000000000 | bytes 8400000 | tf_op jit(solution)/shard_map/kernel_tiles/pallas_call | solution.py:75
  51.8 1.7 %collective-permute-start.2 = (f32[3,2048]{1,0:T(4,128)S(1)}, f32[3,2048]{1,0:T(4,128)S(1)}, u32[]{:S(2)}, u32[]{:S(2)}) collective-permute-start(f32[3,2048]{1,0:T(4,128)S(1)} %copy-done.14), channel_id=1, source_target_pairs={{0,8},{4,12},{8,0},{12,4},{1,9},{5,13},{9,1},{13,5},{2,10},{6,14},... | collective-permute-start | bytes 73736 | tf_op jit(solution)/shard_map/ppermute | solution.py:288
  53.6 3.7 %collective-permute-done.2.refs_3_ = f32[3,2048]{1,0:T(4,128)S(1)} collective-permute-done((f32[3,2048]{1,0:T(4,128)S(1)}, f32[3,2048]{1,0:T(4,128)S(1)}, u32[]{:S(2)}, u32[]{:S(2)}) %collective-permute-start.2) | collective-permute-done | bytes 24608 | tf_op jit(solution)/shard_map/ppermute | solution.py:288
  58.8 6.6 %leaf_sums.5 = f32[128,512]{1,0:T(8,128)} custom-call(s32[4]{0:T(128)} %pad_add_fusion.at_ref, s32[16,8]{1,0:T(8,128)} %copy.9.near_ref, f32[3,8192]{1,0:T(4,128)} %tgt_ref.13, bf16[2048,2048]{1,0:T(8,128)(2,1)} %kernel_tiles.3.refs_0_, bf16[2048,2048]{1,0:T(8,128)(2,1)} %kernel_tiles.4.refs_1_, bf16[2048,2048]{1,0:T(8,128)(2,1)} %kernel_tiles.5.refs_2_, ...), custom_call_target="tpu_custom_call" | custom-call | flops 4000000000 | bytes 9000000 | tf_op jit(solution)/shard_map/leaf_sums/pallas_call | solution.py:126
  65.4 1.7 %collective-permute-start.16 = (f32[128,512]{1,0:T(8,128)}, f32[128,512]{1,0:T(8,128)S(1)}, u32[]{:S(2)}, u32[]{:S(2)}) collective-permute-start(f32[128,512]{1,0:T(8,128)} %leaf_sums.5), channel_id=1, source_target_pairs={{0,1},{1,2},{2,3},{3,0},{4,5},{5,6},{6,7},{7,4},{8,9},{9,10},{10,1... | collective-permute-start | bytes 786440 | tf_op jit(solution)/shard_map/ppermute | solution.py:288
  67.1 6.6 %leaf_sums.6 = f32[128,512]{1,0:T(8,128)} custom-call(s32[4]{0:T(128)} %pad_add_fusion.at_ref, s32[16,8]{1,0:T(8,128)} %copy.9.near_ref, f32[3,8192]{1,0:T(4,128)} %tgt_ref.13, bf16[2048,2048]{1,0:T(8,128)(2,1)} %kernel_tiles.3.refs_0_, bf16[2048,2048]{1,0:T(8,128)(2,1)} %kernel_tiles.4.refs_1_, bf16[2048,2048]{1,0:T(8,128)(2,1)} %kernel_tiles.5.refs_2_, ...), custom_call_target="tpu_custom_call" | custom-call | flops 4000000000 | bytes 9000000 | tf_op jit(solution)/shard_map/leaf_sums/pallas_call | solution.py:126
  73.7 1.0 collective-permute-start.17
  74.7 6.6 %leaf_sums.7 = f32[128,512]{1,0:T(8,128)} custom-call(s32[4]{0:T(128)} %pad_add_fusion.at_ref, s32[16,8]{1,0:T(8,128)} %copy.9.near_ref, f32[3,8192]{1,0:T(4,128)} %tgt_ref.13, bf16[2048,2048]{1,0:T(8,128)(2,1)} %kernel_tiles.3.refs_0_, bf16[2048,2048]{1,0:T(8,128)(2,1)} %kernel_tiles.4.refs_1_, bf16[2048,2048]{1,0:T(8,128)(2,1)} %kernel_tiles.5.refs_2_, ...), custom_call_target="tpu_custom_call" | custom-call | flops 4000000000 | bytes 9000000 | tf_op jit(solution)/shard_map/leaf_sums/pallas_call | solution.py:126
  81.3 2.7 %collective-permute-start.18 = (f32[128,512]{1,0:T(8,128)}, f32[128,512]{1,0:T(8,128)S(1)}, u32[]{:S(2)}, u32[]{:S(2)}) collective-permute-start(f32[128,512]{1,0:T(8,128)} %leaf_sums.7), channel_id=1, source_target_pairs={{0,3},{1,0},{2,1},{3,2},{4,7},{5,4},{6,5},{7,6},{8,11},{9,8},{10,9... | collective-permute-start | bytes 786440 | tf_op jit(solution)/shard_map/ppermute | solution.py:288
  84.0 6.6 %leaf_sums.4.a_ref = f32[128,512]{1,0:T(8,128)} custom-call(s32[4]{0:T(128)} %pad_add_fusion.at_ref, s32[16,8]{1,0:T(8,128)} %copy.9.near_ref, f32[3,8192]{1,0:T(4,128)} %tgt_ref.13, bf16[2048,2048]{1,0:T(8,128)(2,1)} %kernel_tiles.3.refs_0_, bf16[2048,2048]{1,0:T(8,128)(2,1)} %kernel_tiles.4.refs_1_, bf16[2048,2048]{1,0:T(8,128)(2,1)} %kernel_tiles.5.refs_2_, ...), custom_call_target="tpu_custom_call" | custom-call | flops 4000000000 | bytes 9000000 | tf_op jit(solution)/shard_map/leaf_sums/pallas_call | solution.py:126
  91.4 0.7 copy-done.11
  92.1 8.7 %leaf_node.1 = (f32[128,512]{1,0:T(8,128)}, f32[128,128]{1,0:T(8,128)}, f32[128,128]{1,0:T(8,128)}, f32[128,128]{1,0:T(8,128)}) custom-call(s32[4]{0:T(128)} %pad_add_fusion.at_ref, f32[128,512]{1,0:T(8,128)} %leaf_sums.4.a_ref, f32[128,512]{1,0:T(8,128)} %copy-done.9, f32[128,512]{1,0:T(8,128)} %copy-done.10, f32[128,512]{1,0:T(8,128)} %copy-done.11), custom_call_target="tpu_custom_call" | custom-call | tf_op jit(solution)/shard_map/leaf_node/pallas_call | solution.py:257
  100.8 1.3 %collective-permute-start.19 = (f32[128,128]{1,0:T(8,128)}, f32[128,128]{1,0:T(8,128)S(1)}, u32[]{:S(2)}, u32[]{:S(2)}) collective-permute-start(f32[128,128]{1,0:T(8,128)} %get-tuple-element.26.a_ref), channel_id=1, source_target_pairs={{0,1},{1,0},{2,3},{3,2},{4,5},{5,4},{6,7},{7,6},{8,9},{9,8},{10,11... | collective-permute-start | bytes 196616 | tf_op jit(solution)/shard_map/ppermute | solution.py:292
  102.1 2.8 %carry.1 = (f32[512,128]{1,0:T(8,128)}, f32[512,128]{1,0:T(8,128)}) custom-call(f32[128,512]{1,0:T(8,128)} %get-tuple-element.22.z_ref, f32[128,128]{1,0:T(8,128)} %get-tuple-element.23.inv_ref, f32[128,128]{1,0:T(8,128)} %get-tuple-element.24.proj_ref), custom_call_target="tpu_custom_call" | custom-call | tf_op jit(solution)/shard_map/carry/pallas_call | solution.py:271
  105.9 7.8 %pair_node.1 = (f32[128,128]{1,0:T(8,128)}, f32[128,128]{1,0:T(8,128)}, f32[128,128]{1,0:T(8,128)}) custom-call(f32[128,128]{1,0:T(8,128)} %get-tuple-element.26.a_ref, f32[128,128]{1,0:T(8,128)} %copy-done.13), custom_call_target="tpu_custom_call" | custom-call | tf_op jit(solution)/shard_map/pair_node/pallas_call | solution.py:267
  113.7 0.8 collective-permute-start.20
  114.5 2.7 %carry2.1.z_ref = f32[512,128]{1,0:T(8,128)} custom-call(f32[512,128]{1,0:T(8,128)} %get-tuple-element.27.z_ref, f32[128,128]{1,0:T(8,128)} %get-tuple-element.30.inv_ref, f32[128,128]{1,0:T(8,128)} %get-tuple-element.31.proj_ref), custom_call_target="tpu_custom_call" | custom-call | tf_op jit(solution)/shard_map/carry2/pallas_call | solution.py:275
  117.2 2.5 %collective-permute-done.20.b_ref = f32[128,128]{1,0:T(8,128)S(1)} collective-permute-done((f32[128,128]{1,0:T(8,128)}, f32[128,128]{1,0:T(8,128)S(1)}, u32[]{:S(2)}, u32[]{:S(2)}) %collective-permute-start.20) | collective-permute-done | bytes 65568 | tf_op jit(solution)/shard_map/ppermute | solution.py:292
  120.3 8.1 %last_node.1 = f32[512,128]{1,0:T(8,128)} custom-call(f32[128,128]{1,0:T(8,128)} %get-tuple-element.29.a_ref, f32[128,128]{1,0:T(8,128)} %copy-done.12, f32[512,128]{1,0:T(8,128)} %carry2.1.z_ref), custom_call_target="tpu_custom_call" | custom-call | tf_op jit(solution)/shard_map/last_node/pallas_call | solution.py:279
  (63 shorter events, 7.7 us)
Async XLA Ops:
  1.4 16.2 %collective-permute-start.5 = (bf16[8,1024]{1,0:T(8,128)(2,1)S(1)}, bf16[8,1024]{1,0:T(8,128)(2,1)S(1)}, u32[]{:S(2)}, u32[]{:S(2)}) collective-permute-start(bf16[8,1024]{1,0:T(8,128)(2,1)S(1)} %get-tuple-element.33), channel_id=1, source_target_pairs={{0,48},{16,32},{32,16},{48,0},{64,112},{80,96},{96,80},{112,64},{1... | collective-permute-start | bytes 49160 | tf_op jit(solution)/shard_map/ppermute | solution.py:296
  2.7 14.9 %collective-permute-start.3 = (bf16[8,1024]{1,0:T(8,128)(2,1)S(1)}, bf16[8,1024]{1,0:T(8,128)(2,1)S(1)}, u32[]{:S(2)}, u32[]{:S(2)}) collective-permute-start(bf16[8,1024]{1,0:T(8,128)(2,1)S(1)} %get-tuple-element.33), channel_id=1, source_target_pairs={{0,16},{16,0},{1,17},{17,1},{2,18},{18,2},{3,19},{19,3},{4,20},{20... | collective-permute-start | bytes 49160 | tf_op jit(solution)/shard_map/ppermute | solution.py:292
  3.4 24.4 %collective-permute-start = (f32[3,2048]{1,0:T(4,128)}, f32[3,2048]{1,0:T(4,128)S(1)}, u32[]{:S(2)}, u32[]{:S(2)}) collective-permute-start(f32[3,2048]{1,0:T(4,128)} %src_ref.1), channel_id=1, source_target_pairs={{0,4},{4,8},{8,12},{12,0},{1,5},{5,9},{9,13},{13,1},{2,6},{6,10},{... | collective-permute-start | bytes 73736 | tf_op jit(solution)/shard_map/ppermute | solution.py:288
  4.9 36.4 %collective-permute-start.1 = (f32[3,2048]{1,0:T(4,128)}, f32[3,2048]{1,0:T(4,128)S(1)}, u32[]{:S(2)}, u32[]{:S(2)}) collective-permute-start(f32[3,2048]{1,0:T(4,128)} %src_ref.1), channel_id=1, source_target_pairs={{0,12},{4,0},{8,4},{12,8},{1,13},{5,1},{9,5},{13,9},{2,14},{6,2},{... | collective-permute-start | bytes 73736 | tf_op jit(solution)/shard_map/ppermute | solution.py:288
  6.7 11.0 %collective-permute-start.4 = (bf16[8,1024]{1,0:T(8,128)(2,1)S(1)}, bf16[8,1024]{1,0:T(8,128)(2,1)S(1)}, u32[]{:S(2)}, u32[]{:S(2)}) collective-permute-start(bf16[8,1024]{1,0:T(8,128)(2,1)S(1)} %get-tuple-element.32), channel_id=1, source_target_pairs={{0,32},{32,0},{64,96},{96,64},{128,160},{160,128},{192,224},{224,1... | collective-permute-start | bytes 49160 | tf_op jit(solution)/shard_map/ppermute | solution.py:292
  17.7 19.6 %collective-permute-start.8 = (bf16[32,1024]{1,0:T(8,128)(2,1)S(1)}, bf16[32,1024]{1,0:T(8,128)(2,1)S(1)}, u32[]{:S(2)}, u32[]{:S(2)}) collective-permute-start(bf16[32,1024]{1,0:T(8,128)(2,1)S(1)} %pad_maximum_fusion.1), channel_id=1, source_target_pairs={{0,192},{32,224},{64,0},{96,32},{128,64},{160,96},{192,128},{224,1... | collective-permute-start | bytes 196616 | tf_op jit(solution)/shard_map/ppermute | solution.py:288
  24.0 13.2 %collective-permute-start.7 = (bf16[32,1024]{1,0:T(8,128)(2,1)S(1)}, bf16[32,1024]{1,0:T(8,128)(2,1)S(1)}, u32[]{:S(2)}, u32[]{:S(2)}) collective-permute-start(bf16[32,1024]{1,0:T(8,128)(2,1)S(1)} %pad_maximum_fusion.1), channel_id=1, source_target_pairs={{0,128},{32,160},{64,192},{96,224},{128,0},{160,32},{192,64},{224,... | collective-permute-start | bytes 196616 | tf_op jit(solution)/shard_map/ppermute | solution.py:288
  25.0 12.3 %collective-permute-start.6 = (bf16[32,1024]{1,0:T(8,128)(2,1)S(1)}, bf16[32,1024]{1,0:T(8,128)(2,1)S(1)}, u32[]{:S(2)}, u32[]{:S(2)}) collective-permute-start(bf16[32,1024]{1,0:T(8,128)(2,1)S(1)} %pad_maximum_fusion.1), channel_id=1, source_target_pairs={{0,64},{32,96},{64,128},{96,160},{128,192},{160,224},{192,0},{224,... | collective-permute-start | bytes 196616 | tf_op jit(solution)/shard_map/ppermute | solution.py:288
  37.3 13.4 %copy-start = (bf16[4,32,1024]{2,1,0:T(8,128)(2,1)}, bf16[4,32,1024]{2,1,0:T(8,128)(2,1)S(1)}, u32[]{:S(2)}) copy-start(bf16[4,32,1024]{2,1,0:T(8,128)(2,1)S(1)} %pad_maximum_fusion.refs_4_) | copy-start | bytes 786436
  37.3 14.5 %copy-start.14 = (f32[3,2048]{1,0:T(4,128)S(1)}, f32[3,2048]{1,0:T(4,128)}, u32[]{:S(2)}) copy-start(f32[3,2048]{1,0:T(4,128)} %src_ref.1) | copy-start | bytes 73732
  37.4 13.4 %collective-permute-start.11 = (bf16[4,32,1024]{2,1,0:T(8,128)(2,1)S(1)}, bf16[4,32,1024]{2,1,0:T(8,128)(2,1)S(1)}, u32[]{:S(2)}, u32[]{:S(2)}) collective-permute-start(bf16[4,32,1024]{2,1,0:T(8,128)(2,1)S(1)} %pad_maximum_fusion.refs_4_), channel_id=1, source_target_pairs={{0,8},{4,12},{8,0},{12,4},{1,9},{5,13},{9,1},{13,5},{2,10},{6,14},... | collective-permute-start | bytes 786440 | tf_op jit(solution)/shard_map/ppermute | solution.py:288
  39.2 12.0 %collective-permute-start.10 = (bf16[4,32,1024]{2,1,0:T(8,128)(2,1)S(1)}, bf16[4,32,1024]{2,1,0:T(8,128)(2,1)S(1)}, u32[]{:S(2)}, u32[]{:S(2)}) collective-permute-start(bf16[4,32,1024]{2,1,0:T(8,128)(2,1)S(1)} %pad_maximum_fusion.refs_4_), channel_id=1, source_target_pairs={{0,12},{4,0},{8,4},{12,8},{1,13},{5,1},{9,5},{13,9},{2,14},{6,2},{... | collective-permute-start | bytes 786440 | tf_op jit(solution)/shard_map/ppermute | solution.py:288
  40.4 11.0 %collective-permute-start.9 = (bf16[4,32,1024]{2,1,0:T(8,128)(2,1)S(1)}, bf16[4,32,1024]{2,1,0:T(8,128)(2,1)S(1)}, u32[]{:S(2)}, u32[]{:S(2)}) collective-permute-start(bf16[4,32,1024]{2,1,0:T(8,128)(2,1)S(1)} %pad_maximum_fusion.refs_4_), channel_id=1, source_target_pairs={{0,4},{4,8},{8,12},{12,0},{1,5},{5,9},{9,13},{13,1},{2,6},{6,10},{... | collective-permute-start | bytes 786440 | tf_op jit(solution)/shard_map/ppermute | solution.py:288
  50.8 6.5 %collective-permute-start.12 = (bf16[4,32,1024]{2,1,0:T(8,128)(2,1)S(1)}, bf16[4,32,1024]{2,1,0:T(8,128)(2,1)S(1)}, u32[]{:S(2)}, u32[]{:S(2)}) collective-permute-start(bf16[4,32,1024]{2,1,0:T(8,128)(2,1)S(1)} %pad_maximum_fusion.refs_4_), channel_id=1, source_target_pairs={{0,16},{16,0},{1,17},{17,1},{2,18},{18,2},{3,19},{19,3},{4,20},{20... | collective-permute-start | bytes 786440 | tf_op jit(solution)/shard_map/ppermute | solution.py:292
  50.8 6.5 %copy-start.1 = (bf16[4,32,1024]{2,1,0:T(8,128)(2,1)}, bf16[4,32,1024]{2,1,0:T(8,128)(2,1)S(1)}, u32[]{:S(2)}) copy-start(bf16[4,32,1024]{2,1,0:T(8,128)(2,1)S(1)} %collective-permute-done.11.refs_7_) | copy-start | bytes 786436
  50.8 6.5 %collective-permute-start.15 = (bf16[4,32,1024]{2,1,0:T(8,128)(2,1)S(1)}, bf16[4,32,1024]{2,1,0:T(8,128)(2,1)S(1)}, u32[]{:S(2)}, u32[]{:S(2)}) collective-permute-start(bf16[4,32,1024]{2,1,0:T(8,128)(2,1)S(1)} %collective-permute-done.11.refs_7_), channel_id=1, source_target_pairs={{0,16},{16,0},{1,17},{17,1},{2,18},{18,2},{3,19},{19,3},{4,20},{20... | collective-permute-start | bytes 786440 | tf_op jit(solution)/shard_map/ppermute | solution.py:292
  51.3 6.0 %copy-start.2 = (bf16[4,32,1024]{2,1,0:T(8,128)(2,1)}, bf16[4,32,1024]{2,1,0:T(8,128)(2,1)S(1)}, u32[]{:S(2)}) copy-start(bf16[4,32,1024]{2,1,0:T(8,128)(2,1)S(1)} %collective-permute-done.10.refs_6_) | copy-start | bytes 786436
  51.3 6.0 %collective-permute-start.14 = (bf16[4,32,1024]{2,1,0:T(8,128)(2,1)S(1)}, bf16[4,32,1024]{2,1,0:T(8,128)(2,1)S(1)}, u32[]{:S(2)}, u32[]{:S(2)}) collective-permute-start(bf16[4,32,1024]{2,1,0:T(8,128)(2,1)S(1)} %collective-permute-done.10.refs_6_), channel_id=1, source_target_pairs={{0,16},{16,0},{1,17},{17,1},{2,18},{18,2},{3,19},{19,3},{4,20},{20... | collective-permute-start | bytes 786440 | tf_op jit(solution)/shard_map/ppermute | solution.py:292
  51.4 5.9 %copy-start.3 = (bf16[4,32,1024]{2,1,0:T(8,128)(2,1)}, bf16[4,32,1024]{2,1,0:T(8,128)(2,1)S(1)}, u32[]{:S(2)}) copy-start(bf16[4,32,1024]{2,1,0:T(8,128)(2,1)S(1)} %collective-permute-done.9.refs_5_) | copy-start | bytes 786436
  51.4 5.9 %collective-permute-start.13 = (bf16[4,32,1024]{2,1,0:T(8,128)(2,1)S(1)}, bf16[4,32,1024]{2,1,0:T(8,128)(2,1)S(1)}, u32[]{:S(2)}, u32[]{:S(2)}) collective-permute-start(bf16[4,32,1024]{2,1,0:T(8,128)(2,1)S(1)} %collective-permute-done.9.refs_5_), channel_id=1, source_target_pairs={{0,16},{16,0},{1,17},{17,1},{2,18},{18,2},{3,19},{19,3},{4,20},{20... | collective-permute-start | bytes 786440 | tf_op jit(solution)/shard_map/ppermute | solution.py:292
  51.8 5.4 %collective-permute-start.2 = (f32[3,2048]{1,0:T(4,128)S(1)}, f32[3,2048]{1,0:T(4,128)S(1)}, u32[]{:S(2)}, u32[]{:S(2)}) collective-permute-start(f32[3,2048]{1,0:T(4,128)S(1)} %copy-done.14), channel_id=1, source_target_pairs={{0,8},{4,12},{8,0},{12,4},{1,9},{5,13},{9,1},{13,5},{2,10},{6,14},... | collective-permute-start | bytes 73736 | tf_op jit(solution)/shard_map/ppermute | solution.py:288
  57.2 0.7 copy-start.4
  57.2 0.8 copy-start.5
  57.3 0.9 copy-start.6
  65.4 25.1 %collective-permute-start.16 = (f32[128,512]{1,0:T(8,128)}, f32[128,512]{1,0:T(8,128)S(1)}, u32[]{:S(2)}, u32[]{:S(2)}) collective-permute-start(f32[128,512]{1,0:T(8,128)} %leaf_sums.5), channel_id=1, source_target_pairs={{0,1},{1,2},{2,3},{3,0},{4,5},{5,6},{6,7},{7,4},{8,9},{9,10},{10,1... | collective-permute-start | bytes 786440 | tf_op jit(solution)/shard_map/ppermute | solution.py:288
  73.7 16.9 %collective-permute-start.17 = (f32[128,512]{1,0:T(8,128)}, f32[128,512]{1,0:T(8,128)S(1)}, u32[]{:S(2)}, u32[]{:S(2)}) collective-permute-start(f32[128,512]{1,0:T(8,128)} %leaf_sums.6), channel_id=1, source_target_pairs={{0,2},{1,3},{2,0},{3,1},{4,6},{5,7},{6,4},{7,5},{8,10},{9,11},{10,... | collective-permute-start | bytes 786440 | tf_op jit(solution)/shard_map/ppermute | solution.py:288
  81.3 9.4 %collective-permute-start.18 = (f32[128,512]{1,0:T(8,128)}, f32[128,512]{1,0:T(8,128)S(1)}, u32[]{:S(2)}, u32[]{:S(2)}) collective-permute-start(f32[128,512]{1,0:T(8,128)} %leaf_sums.7), channel_id=1, source_target_pairs={{0,3},{1,0},{2,1},{3,2},{4,7},{5,4},{6,5},{7,6},{8,11},{9,8},{10,9... | collective-permute-start | bytes 786440 | tf_op jit(solution)/shard_map/ppermute | solution.py:288
  90.6 0.7 copy-start.9
  90.6 0.8 copy-start.10
  91.4 0.7 copy-start.11
  100.8 4.5 %collective-permute-start.19 = (f32[128,128]{1,0:T(8,128)}, f32[128,128]{1,0:T(8,128)S(1)}, u32[]{:S(2)}, u32[]{:S(2)}) collective-permute-start(f32[128,128]{1,0:T(8,128)} %get-tuple-element.26.a_ref), channel_id=1, source_target_pairs={{0,1},{1,0},{2,3},{3,2},{4,5},{5,4},{6,7},{7,6},{8,9},{9,8},{10,11... | collective-permute-start | bytes 196616 | tf_op jit(solution)/shard_map/ppermute | solution.py:292
  113.7 6.0 %collective-permute-start.20 = (f32[128,128]{1,0:T(8,128)}, f32[128,128]{1,0:T(8,128)S(1)}, u32[]{:S(2)}, u32[]{:S(2)}) collective-permute-start(f32[128,128]{1,0:T(8,128)} %get-tuple-element.29.a_ref), channel_id=1, source_target_pairs={{0,2},{1,3},{2,0},{3,1},{4,6},{5,7},{6,4},{7,5},{8,10},{9,11},{10,... | collective-permute-start | bytes 196616 | tf_op jit(solution)/shard_map/ppermute | solution.py:292
  (6 other events, 3.8 us)

commit v5 on v4

--- a/solution.py
+++ b/solution.py
@@ -51,74 +51,81 @@
     return features(pts_ref, centre, False), centre
 
 
-def tile_of(q, i, leaf, at_ref, near_ref, src_ref, pts_ref, cols, centre):
-    c, x, y = at_ref[1], at_ref[2], at_ref[3]
+def place():
+    return [lax.axis_index(a) for a in ("z", "c", "x", "y")]
+
+
+def tile_of(q, i, leaf, near_ref, src_ref, pts_ref, cols, centre):
+    _, c, x, y = place()
     chunk = jnp.bitwise_and(2 * c + i, 3)
     leaf_id = (jnp.bitwise_and(x - q, 3) * 4 + y) * 4 + chunk
-    hit = near_ref[x * 4 + leaf, 0] == leaf_id
+    hit = near_ref[0, x * 4 + leaf] == leaf_id
     for k in range(1, 8):
-        hit = jnp.logical_or(hit, near_ref[x * 4 + leaf, k] == leaf_id)
+        hit = jnp.logical_or(hit, near_ref[k, x * 4 + leaf] == leaf_id)
     pts_ref[0:3, :] = src_ref[:, pl.ds(pl.multiple_of(chunk * LEAF, LEAF), LEAF)]
     return kernel_tile(features(pts_ref, centre, True, jnp.where(hit, 1e9, 0.0)), cols)
 
 
-def tiles_body(q, at_ref, near_ref, tgt_ref, src_ref, out_ref, tpts_ref, spts_ref):
-    leaf = pl.program_id(0)
-    cols, centre = target_features(tgt_ref, tpts_ref, at_ref[2] * 4 + leaf)
+def tiles_body(q, near_ref, tgt_ref, src_ref, out_ref, tpts_ref, spts_ref):
+    _, _, x, y = place()
     spts_ref[...] = jnp.zeros_like(spts_ref)
-    for i in range(4):
-        out_ref[i * LEAF:(i + 1) * LEAF, :] = tile_of(
-            q, i, leaf, at_ref, near_ref, src_ref, spts_ref.at[i], cols, centre)
-
-
-def kernel_tiles(q, at, near, targets, sources):
+
+    def one_leaf(turn, carry):
+        leaf = jnp.bitwise_and(y + turn, 3)
+        cols, centre = target_features(tgt_ref, tpts_ref, x * 4 + leaf)
+        for i in range(4):
+            out_ref[turn, i * LEAF:(i + 1) * LEAF, :] = tile_of(
+                q, i, leaf, near_ref, src_ref, spts_ref.at[i], cols, centre)
+        return carry
+
+    lax.fori_loop(0, 4, one_leaf, 0)
+
+
+def params():
+    return pltpu.CompilerParams(vmem_limit_bytes=16 * 2**20)
+
+
+def kernel_tiles(q, near, targets, sources):
+    vm = pl.BlockSpec(memory_space=pltpu.VMEM)
     return pl.pallas_call(
         functools.partial(tiles_body, q),
-        out_shape=jax.ShapeDtypeStruct((2048, 2048), BF),
-        grid_spec=pltpu.PrefetchScalarGridSpec(
-            num_scalar_prefetch=2,
-            grid=(4,),
-            in_specs=[
-                pl.BlockSpec((3, targets.shape[1]), lambda i, a, n: (0, 0)),
-                pl.BlockSpec((3, 2048), lambda i, a, n: (0, 0)),
-            ],
-            out_specs=pl.BlockSpec((2048, LEAF), lambda i, a, n: (0, i)),
-            scratch_shapes=[pltpu.VMEM((8, LEAF), F32), pltpu.VMEM((4, 8, LEAF), F32)],
-        ),
+        out_shape=jax.ShapeDtypeStruct((4, 2048, LEAF), BF),
+        in_specs=[pl.BlockSpec(memory_space=pltpu.SMEM), vm, vm],
+        out_specs=vm,
+        scratch_shapes=[pltpu.VMEM((8, LEAF), F32), pltpu.VMEM((4, 8, LEAF), F32)],
         cost_estimate=pl.CostEstimate(flops=8_000_000_000, bytes_accessed=8_400_000, transcendentals=8_400_000),
+        compiler_params=params(),
         name="kernel_tiles",
-    )(at, near, targets, sources)
-
-
-def sums_body(turn, stored, fused, at_ref, near_ref, tgt_ref, *refs):
+    )(near, targets, sources)
+
+
+def sums_body(turn, stored, fused, near_ref, tgt_ref, *refs):
     ns, nf = len(stored), len(fused)
     tiles, refs = refs[:ns], refs[ns:]
     srcs, refs = refs[:nf], refs[nf:]
     mine, refs = refs[:ns + nf], refs[ns + nf:]
     other, refs = refs[:ns + nf], refs[ns + nf:]
-    out_ref, held_ref, tpts_ref, spts_ref, sems = refs
-    leaf = jnp.bitwise_and(at_ref[3] + turn, 3)
-    lanes = pl.ds(pl.multiple_of(leaf * LEAF, LEAF), LEAF)
-    copies = [pltpu.make_async_copy(tiles[n].at[:, lanes], held_ref.at[n], sems.at[n]) for n in range(ns)]
-    for copy in copies:
-        copy.start()
-    cols, centre = target_features(tgt_ref, tpts_ref, at_ref[2] * 4 + leaf)
+    out_ref, held_ref, tpts_ref, spts_ref = refs
+    _, _, x, y = place()
+    leaf = jnp.bitwise_and(y + turn, 3)
+    cols, centre = target_features(tgt_ref, tpts_ref, x * 4 + leaf)
     spts_ref[...] = jnp.zeros_like(spts_ref)
-    for n in range(nf):
-        for i in range(4):
-            held_ref[ns + n, i * LEAF:(i + 1) * LEAF, :] = tile_of(
-                fused[n], i, leaf, at_ref, near_ref, srcs[n], spts_ref.at[4 * n + i], cols, centre)
-    for copy in copies:
-        copy.wait()
     total = None
     for n in range(ns + nf):
         rows = jnp.concatenate([mine[n][...].reshape(128, 1024), other[n][...].reshape(128, 1024)], axis=1)
-        term = jnp.dot(rows, held_ref[n], preferred_element_type=F32)
+        if n >= ns:
+            for i in range(4):
+                held_ref[n - ns, i * LEAF:(i + 1) * LEAF, :] = tile_of(
+                    fused[n - ns], i, leaf, near_ref, srcs[n - ns], spts_ref.at[4 * (n - ns) + i], cols, centre)
+            tile = held_ref[n - ns]
+        else:
+            tile = tiles[n][turn]
+        term = jnp.dot(rows, tile, preferred_element_type=F32)
         total = term if total is None else total + term
     out_ref[...] = total
 
 
-def leaf_sums(turn, at, near, targets, tiles, sources, mine, other):
+def leaf_sums(turn, near, targets, tiles, sources, mine, other):
     stored, fused = sorted(tiles), sorted(sources)
     order = stored + fused
     vm = pl.BlockSpec(memory_space=pltpu.VMEM)
@@ -126,16 +133,16 @@
     return pl.pallas_call(
         functools.partial(sums_body, turn, stored, fused),
         out_shape=jax.ShapeDtypeStruct((128, LEAF), F32),
-        in_specs=[sm, sm, vm] + [pl.BlockSpec(memory_space=pl.ANY)] * len(stored) + [vm] * (len(fused) + 8),
+        in_specs=[sm, vm] + [vm] * (len(stored) + len(fused) + 8),
         scratch_shapes=[
-            pltpu.VMEM((4, 2048, LEAF), BF),
+            pltpu.VMEM((len(fused), 2048, LEAF), BF),
             pltpu.VMEM((8, LEAF), F32),
             pltpu.VMEM((4 * len(fused), 8, LEAF), F32),
-            pltpu.SemaphoreType.DMA((len(stored),)),
         ],
         cost_estimate=pl.CostEstimate(flops=4_000_000_000, bytes_accessed=9_000_000, transcendentals=1_000_000),
+        compiler_params=params(),
         name="leaf_sums",
-    )(at, near, targets, *[tiles[q] for q in stored], *[sources[q] for q in fused],
+    )(near, targets, *[tiles[q] for q in stored], *[sources[q] for q in fused],
       *[mine[q] for q in order], *[other[q] for q in order])
 
 
@@ -198,10 +205,10 @@
     return lax.dot_general(a, b, (((1,), (0,)), ((), ())), precision=HI, preferred_element_type=F32)
 
 
-def leaf_body(at_ref, a_ref, b_ref, c_ref, d_ref, z_ref, inv_ref, proj_ref, sq_ref, aug_ref, top_ref):
+def leaf_body(a_ref, b_ref, c_ref, d_ref, z_ref, inv_ref, proj_ref, sq_ref, aug_ref, top_ref):
     for k in range(4):
         for s in range(2):
-            plane = jnp.bitwise_xor(jnp.bitwise_and(at_ref[0] - 2 * k, 7), s)
+            plane = jnp.bitwise_xor(jnp.bitwise_and(place()[0] - 2 * k, 7), s)
             rows = slice(16 * (2 * k + s), 16 * (2 * k + s) + 16)
             both = (a_ref[rows, :] + b_ref[rows, :]) + (c_ref[rows, :] + d_ref[rows, :])
             z_ref[pl.ds(pl.multiple_of(plane * 16, 16), 16), :] = both
@@ -252,31 +259,32 @@
     return pl.CostEstimate(flops=f, bytes_accessed=400000, transcendentals=0)
 
 
-def leaf_node(at, parts):
+def leaf_node(parts):
     vm = pl.BlockSpec(memory_space=pltpu.VMEM)
     return pl.pallas_call(
         leaf_body,
         out_shape=(sds(128, LEAF),) + (sds(128, 128),) * 3,
-        in_specs=[pl.BlockSpec(memory_space=pltpu.SMEM)] + [vm] * 4,
+        in_specs=[vm] * 4,
         scratch_shapes=SCR,
         name="leaf_node",
-    )(at, *parts)
+        compiler_params=params(),
+    )(*parts)
 
 
 def pair_node(a, b):
-    return pl.pallas_call(node_body, out_shape=(sds(128, 128),) * 3, scratch_shapes=SCR, name="pair_node")(a, b)
+    return pl.pallas_call(node_body, out_shape=(sds(128, 128),) * 3, scratch_shapes=SCR, name="pair_node", compiler_params=params())(a, b)
 
 
 def carry(z, inv, proj):
-    return pl.pallas_call(carry_body, out_shape=(sds(512, 128),) * 2, name="carry")(z, inv, proj)
+    return pl.pallas_call(carry_body, out_shape=(sds(512, 128),) * 2, name="carry", compiler_params=params())(z, inv, proj)
 
 
 def carry2(z, inv, proj):
-    return pl.pallas_call(carry2_body, out_shape=sds(512, 128), name="carry2")(z, inv, proj)
+    return pl.pallas_call(carry2_body, out_shape=sds(512, 128), name="carry2", compiler_params=params())(z, inv, proj)
 
 
 def last_node(a, b, z):
-    return pl.pallas_call(last_body, out_shape=sds(512, 128), scratch_shapes=SCR, name="last_node")(a, b, z)
+    return pl.pallas_call(last_body, out_shape=sds(512, 128), scratch_shapes=SCR, name="last_node", compiler_params=params())(a, b, z)
 
 
 ROW = ("z", "c")
@@ -312,24 +320,25 @@
 
 
 def per_device(targets, sources, samples, near):
-    at = jnp.stack([lax.axis_index(a) for a in ("z", "c", "x", "y")]).astype(jnp.int32)
+    core = lax.axis_index("c")
+    near = near.T
     srcs = [sources] + [moved(sources, "x", q) for q in (1, 2, 3)]
-    pair = own_pair(samples, at[1])
-    tiles = {0: kernel_tiles(0, at, near, targets, sources)}
+    pair = own_pair(samples, core)
+    tiles = {0: kernel_tiles(0, near, targets, sources)}
     pair = after(pair, tiles[0])
     block = jnp.stack([pair] + [moved(pair, "z", 2 * k) for k in (1, 2, 3)])
-    tiles[1] = kernel_tiles(1, at, near, targets, srcs[1])
+    tiles[1] = kernel_tiles(1, near, targets, after(srcs[1], srcs[2], srcs[3]))
     block = after(block, tiles[1])
     mine = [block] + [moved(block, "x", q) for q in (1, 2, 3)]
-    tiles[3] = kernel_tiles(3, at, near, targets, srcs[3])
+    tiles[3] = kernel_tiles(3, near, targets, srcs[3])
     mine = [block] + [after(b, tiles[3]) for b in mine[1:]]
     other = [crossed(b, "c", 1) for b in mine]
     fused = {2: srcs[2]}
     sums = {}
     for d in (2, 1, 3, 0):
-        part = leaf_sums(d, at, near, targets, tiles, fused, mine, other)
+        part = leaf_sums(d, near, targets, tiles, fused, mine, other)
         sums[d] = moved(part, "y", d) if d else part
-    far_sample, inv0, proj0, sq0 = leaf_node(at, [sums[d] for d in range(4)])
+    far_sample, inv0, proj0, sq0 = leaf_node([sums[d] for d in range(4)])
     sib = crossed(sq0, "y", 1)
     leaf_basis, carried = carry(far_sample, inv0, proj0)
     inv1, proj1, sq1 = pair_node(sq0, after(sib, carried))

time: 130 us -> 108 us (0.83)
  Pallas kernels: 82.9 us -> 53.3 us
  waiting for transfers between devices: 6.55 us -> 19.3 us
  starting transfers between devices: 29.8 us -> 27.5 us
    pallas_call x4, Pallas kernels: 26.3 us -> 12 us  [leaf_sums(): pl.pallas_call(functools.partial(sums_body, turn, stored, fused), out_sha...]
    ppermute x8, waiting for transfers between devices: 2.84 us -> 11.8 us  [crossed(): lax.ppermute(x, axis, [(i, i ^ bit) for i in range(lax.axis_size(axis))])]
    pallas_call x3, Pallas kernels: 26.5 us -> 18.7 us  [kernel_tiles(): pl.pallas_call(functools.partial(tiles_body, q), out_shape=jax.ShapeDtype...]
    ppermute x12, waiting for transfers between devices: 3.71 us -> 7.45 us  [moved(): return lax.ppermute(x, axis, [(i, (i + by) % size) for i in range(size)])]
    pallas_call x2, Pallas kernels: 5.46 us -> 2.31 us  [the longest x1 1.31 us: carry(): pl.pallas_call(carry_body, out_shape=(sds(512, 128),) * 2, name='carry',...]
    pallas_call x1, Pallas kernels: 8.68 us -> 6.86 us  [leaf_node(): pl.pallas_call(leaf_body, out_shape=(sds(128, LEAF),) + (sds(128, 128),)...]
    pallas_call x1, Pallas kernels: 7.82 us -> 6.32 us  [pair_node(): pl.pallas_call(node_body, out_shape=(sds(128, 128),) * 3, scratch_shapes=...]
    ppermute x8, starting transfers between devices: 3.97 us -> 2.58 us  [crossed(): lax.ppermute(x, axis, [(i, i ^ bit) for i in range(lax.axis_size(axis))])]
  transfers between devices with their start and end apart: 21 -> 21, of which waited for: 3 -> 8; matrix products, arithmetic and copies ran while one was open for 2% -> 0% of each run, Pallas kernels for 40% -> 28%
where the time goes in v5:
time: 108 us; the launch traced here: 107 us
  Pallas kernels  53.3 us (49%)
  starting transfers between devices  27.5 us (25%)
  waiting for transfers between devices  19.3 us (18%)
  local copies, waits for them, and re-layouts  6.37 us (6%)
    ppermute x12, starting transfers between devices, moved(): return lax.ppermute(x, axis, [(i, (i + by) % size) for i in range(size)])  23.6 us
    pallas_call x3, Pallas kernels, kernel_tiles(): pl.pallas_call(functools.partial(tiles_body, q), out_shape=jax.ShapeDtype...  18.7 us
    pallas_call x4, Pallas kernels, leaf_sums(): pl.pallas_call(functools.partial(sums_body, turn, stored, fused), out_sha...  12 us
    ppermute x8, waiting for transfers between devices, crossed(): lax.ppermute(x, axis, [(i, i ^ bit) for i in range(lax.axis_size(axis))])  11.8 us
    ppermute x12, waiting for transfers between devices, moved(): return lax.ppermute(x, axis, [(i, (i + by) % size) for i in range(size)])  7.45 us
    pallas_call x1, Pallas kernels, last_node(): pl.pallas_call(last_body, out_shape=sds(512, 128), scratch_shapes=SCR, na...  7.12 us
    pallas_call x1, Pallas kernels, leaf_node(): pl.pallas_call(leaf_body, out_shape=(sds(128, LEAF),) + (sds(128, 128),)...  6.86 us
    pallas_call x1, Pallas kernels, pair_node(): pl.pallas_call(node_body, out_shape=(sds(128, 128),) * 3, scratch_shapes=...  6.32 us
  transfers between devices with their start and end apart: 21, of which 8 were waited for; matrix products, arithmetic and copies ran while one was open for 0% of the time, Pallas kernels for 28%

profile of v5, /device:TPU:8, one launch (start us, length us, event | category | flops | bytes accessed | tf_op | source)
XLA Modules:
  0.0 107.4 jit_solution(1443428295394495162)
XLA Ops:
  1.4 1.4 %collective-permute-start.5 = (bf16[8,1024]{1,0:T(8,128)(2,1)S(1)}, bf16[8,1024]{1,0:T(8,128)(2,1)S(1)}, u32[]{:S(2)}, u32[]{:S(2)}) collective-permute-start(bf16[8,1024]{1,0:T(8,128)(2,1)S(1)} %get-tuple-element.35), channel_id=1, source_target_pairs={{0,48},{16,32},{32,16},{48,0},{64,112},{80,96},{96,80},{112,64},{1... | collective-permute-start | bytes 49160 | tf_op jit(solution)/shard_map/ppermute | solution.py:304
  3.4 1.5 %collective-permute-start = (f32[3,2048]{1,0:T(4,128)}, f32[3,2048]{1,0:T(4,128)S(1)}, u32[]{:S(2)}, u32[]{:S(2)}) collective-permute-start(f32[3,2048]{1,0:T(4,128)} %src_ref.1), channel_id=1, source_target_pairs={{0,4},{4,8},{8,12},{12,0},{1,5},{5,9},{9,13},{13,1},{2,6},{6,10},{... | collective-permute-start | bytes 73736 | tf_op jit(solution)/shard_map/ppermute | solution.py:296
  4.9 1.7 %collective-permute-start.2 = (f32[3,2048]{1,0:T(4,128)}, f32[3,2048]{1,0:T(4,128)S(1)}, u32[]{:S(2)}, u32[]{:S(2)}) collective-permute-start(f32[3,2048]{1,0:T(4,128)} %src_ref.1), channel_id=1, source_target_pairs={{0,12},{4,0},{8,4},{12,8},{1,13},{5,1},{9,5},{13,9},{2,14},{6,2},{... | collective-permute-start | bytes 73736 | tf_op jit(solution)/shard_map/ppermute | solution.py:296
  6.7 1.8 %collective-permute-start.1 = (f32[3,2048]{1,0:T(4,128)}, f32[3,2048]{1,0:T(4,128)S(1)}, u32[]{:S(2)}, u32[]{:S(2)}) collective-permute-start(f32[3,2048]{1,0:T(4,128)} %src_ref.1), channel_id=1, source_target_pairs={{0,8},{4,12},{8,0},{12,4},{1,9},{5,13},{9,1},{13,5},{2,10},{6,14},... | collective-permute-start | bytes 73736 | tf_op jit(solution)/shard_map/ppermute | solution.py:296
  10.8 6.2 %kernel_tiles.3.refs_0_ = bf16[4,2048,512]{2,1,0:T(8,128)(2,1)S(1)} custom-call(s32[8,16]{1,0:T(8,128)S(1)} %bitcast.11, f32[3,8192]{1,0:T(4,128)S(1)} %copy-done.1, f32[3,2048]{1,0:T(4,128)S(1)} %copy-done.5), custom_call_target="tpu_custom_call" | custom-call | flops 8000000000 | bytes 8400000 | tf_op jit(solution)/shard_map/kernel_tiles/pallas_call | solution.py:90
  17.1 3.3 %copy-done = bf16[4,2048,512]{2,1,0:T(8,128)(2,1)} copy-done((bf16[4,2048,512]{2,1,0:T(8,128)(2,1)}, bf16[4,2048,512]{2,1,0:T(8,128)(2,1)S(1)}, u32[]{:S(2)}) %copy-start) | copy-done | bytes 8388632
  20.5 3.6 %collective-permute-done.4 = bf16[8,1024]{1,0:T(8,128)(2,1)S(1)} collective-permute-done((bf16[8,1024]{1,0:T(8,128)(2,1)S(1)}, bf16[8,1024]{1,0:T(8,128)(2,1)S(1)}, u32[]{:S(2)}, u32[]{:S(2)}) %collective-permute-start.4) | collective-permute-done | bytes 16416 | tf_op jit(solution)/shard_map/ppermute | solution.py:300
  24.1 5.5 %collective-permute-start.8 = (bf16[32,1024]{1,0:T(8,128)(2,1)S(1)}, bf16[32,1024]{1,0:T(8,128)(2,1)S(1)}, u32[]{:S(2)}, u32[]{:S(2)}) collective-permute-start(bf16[32,1024]{1,0:T(8,128)(2,1)S(1)} %pad_maximum_fusion.1), channel_id=1, source_target_pairs={{0,192},{32,224},{64,0},{96,32},{128,64},{160,96},{192,128},{224,1... | collective-permute-start | bytes 196616 | tf_op jit(solution)/shard_map/ppermute | solution.py:296
  29.6 1.6 %collective-permute-start.7 = (bf16[32,1024]{1,0:T(8,128)(2,1)S(1)}, bf16[32,1024]{1,0:T(8,128)(2,1)S(1)}, u32[]{:S(2)}, u32[]{:S(2)}) collective-permute-start(bf16[32,1024]{1,0:T(8,128)(2,1)S(1)} %pad_maximum_fusion.1), channel_id=1, source_target_pairs={{0,128},{32,160},{64,192},{96,224},{128,0},{160,32},{192,64},{224,... | collective-permute-start | bytes 196616 | tf_op jit(solution)/shard_map/ppermute | solution.py:296
  31.2 2.2 %collective-permute-start.6 = (bf16[32,1024]{1,0:T(8,128)(2,1)S(1)}, bf16[32,1024]{1,0:T(8,128)(2,1)S(1)}, u32[]{:S(2)}, u32[]{:S(2)}) collective-permute-start(bf16[32,1024]{1,0:T(8,128)(2,1)S(1)} %pad_maximum_fusion.1), channel_id=1, source_target_pairs={{0,64},{32,96},{64,128},{96,160},{128,192},{160,224},{192,0},{224,... | collective-permute-start | bytes 196616 | tf_op jit(solution)/shard_map/ppermute | solution.py:296
  33.4 6.2 %kernel_tiles.4.refs_1_ = bf16[4,2048,512]{2,1,0:T(8,128)(2,1)S(1)} custom-call(s32[8,16]{1,0:T(8,128)S(1)} %bitcast.12, f32[3,8192]{1,0:T(4,128)S(1)} %copy-done.2, f32[3,2048]{1,0:T(4,128)S(1)} %collective-permute-done.src_ref), custom_call_target="tpu_custom_call" | custom-call | flops 8000000000 | bytes 8400000 | tf_op jit(solution)/shard_map/kernel_tiles/pallas_call | solution.py:90
  39.8 1.8 %collective-permute-start.11 = (bf16[4,32,1024]{2,1,0:T(8,128)(2,1)S(1)}, bf16[4,32,1024]{2,1,0:T(8,128)(2,1)S(1)}, u32[]{:S(2)}, u32[]{:S(2)}) collective-permute-start(bf16[4,32,1024]{2,1,0:T(8,128)(2,1)S(1)} %pad_maximum_fusion.refs_4_), channel_id=1, source_target_pairs={{0,8},{4,12},{8,0},{12,4},{1,9},{5,13},{9,1},{13,5},{2,10},{6,14},... | collective-permute-start | bytes 786440 | tf_op jit(solution)/shard_map/ppermute | solution.py:296
  41.6 1.6 %collective-permute-start.10 = (bf16[4,32,1024]{2,1,0:T(8,128)(2,1)S(1)}, bf16[4,32,1024]{2,1,0:T(8,128)(2,1)S(1)}, u32[]{:S(2)}, u32[]{:S(2)}) collective-permute-start(bf16[4,32,1024]{2,1,0:T(8,128)(2,1)S(1)} %pad_maximum_fusion.refs_4_), channel_id=1, source_target_pairs={{0,12},{4,0},{8,4},{12,8},{1,13},{5,1},{9,5},{13,9},{2,14},{6,2},{... | collective-permute-start | bytes 786440 | tf_op jit(solution)/shard_map/ppermute | solution.py:296
  43.6 6.2 %kernel_tiles.5.refs_2_ = bf16[4,2048,512]{2,1,0:T(8,128)(2,1)S(1)} custom-call(s32[8,16]{1,0:T(8,128)S(1)} %bitcast.13, f32[3,8192]{1,0:T(4,128)S(1)} %copy-done.2, f32[3,2048]{1,0:T(4,128)S(1)} %collective-permute-done.2.src_ref), custom_call_target="tpu_custom_call" | custom-call | flops 8000000000 | bytes 8400000 | tf_op jit(solution)/shard_map/kernel_tiles/pallas_call | solution.py:90
  50.8 1.5 %collective-permute-done.9.refs_5_ = bf16[4,32,1024]{2,1,0:T(8,128)(2,1)S(1)} collective-permute-done((bf16[4,32,1024]{2,1,0:T(8,128)(2,1)S(1)}, bf16[4,32,1024]{2,1,0:T(8,128)(2,1)S(1)}, u32[]{:S(2)}, u32[]{:S(2)}) %collective-permute-start.9) | collective-permute-done | bytes 262176 | tf_op jit(solution)/shard_map/ppermute | solution.py:296
  52.4 1.5 %collective-permute-done.13.refs_9_ = bf16[4,32,1024]{2,1,0:T(8,128)(2,1)S(1)} collective-permute-done((bf16[4,32,1024]{2,1,0:T(8,128)(2,1)S(1)}, bf16[4,32,1024]{2,1,0:T(8,128)(2,1)S(1)}, u32[]{:S(2)}, u32[]{:S(2)}) %collective-permute-start.13) | collective-permute-done | bytes 262176 | tf_op jit(solution)/shard_map/ppermute | solution.py:300
  53.9 3.0 %leaf_sums.5 = f32[128,512]{1,0:T(8,128)S(1)} custom-call(s32[8,16]{1,0:T(8,128)S(1)} %bitcast.14, f32[3,8192]{1,0:T(4,128)S(1)} %copy-done.2, bf16[4,2048,512]{2,1,0:T(8,128)(2,1)S(1)} %bitcast.10, bf16[4,2048,512]{2,1,0:T(8,128)(2,1)S(1)} %kernel_tiles.4.refs_1_, bf16[4,2048,512]{2,1,0:T(8,128)(2,1)S(1)} %kernel_tiles.5.refs_2_, ...), custom_call_target="tpu_custom_call" | custom-call | flops 4000000000 | bytes 9000000 | tf_op jit(solution)/shard_map/leaf_sums/pallas_call | solution.py:133
  56.9 1.7 %collective-permute-start.16 = (f32[128,512]{1,0:T(8,128)S(1)}, f32[128,512]{1,0:T(8,128)S(1)}, u32[]{:S(2)}, u32[]{:S(2)}) collective-permute-start(f32[128,512]{1,0:T(8,128)S(1)} %leaf_sums.5), channel_id=1, source_target_pairs={{0,1},{1,2},{2,3},{3,0},{4,5},{5,6},{6,7},{7,4},{8,9},{9,10},{10,1... | collective-permute-start | bytes 786440 | tf_op jit(solution)/shard_map/ppermute | solution.py:296
  58.6 3.0 %leaf_sums.6 = f32[128,512]{1,0:T(8,128)S(1)} custom-call(s32[8,16]{1,0:T(8,128)S(1)} %bitcast.15, f32[3,8192]{1,0:T(4,128)S(1)} %copy-done.2, bf16[4,2048,512]{2,1,0:T(8,128)(2,1)S(1)} %bitcast.10, bf16[4,2048,512]{2,1,0:T(8,128)(2,1)S(1)} %kernel_tiles.4.refs_1_, bf16[4,2048,512]{2,1,0:T(8,128)(2,1)S(1)} %kernel_tiles.5.refs_2_, ...), custom_call_target="tpu_custom_call" | custom-call | flops 4000000000 | bytes 9000000 | tf_op jit(solution)/shard_map/leaf_sums/pallas_call | solution.py:133
  61.6 1.0 collective-permute-start.17
  62.6 3.0 %leaf_sums.7 = f32[128,512]{1,0:T(8,128)S(1)} custom-call(s32[8,16]{1,0:T(8,128)S(1)} %bitcast.16, f32[3,8192]{1,0:T(4,128)S(1)} %copy-done.2, bf16[4,2048,512]{2,1,0:T(8,128)(2,1)S(1)} %bitcast.10, bf16[4,2048,512]{2,1,0:T(8,128)(2,1)S(1)} %kernel_tiles.4.refs_1_, bf16[4,2048,512]{2,1,0:T(8,128)(2,1)S(1)} %kernel_tiles.5.refs_2_, ...), custom_call_target="tpu_custom_call" | custom-call | flops 4000000000 | bytes 9000000 | tf_op jit(solution)/shard_map/leaf_sums/pallas_call | solution.py:133
  65.6 2.7 %collective-permute-start.18 = (f32[128,512]{1,0:T(8,128)S(1)}, f32[128,512]{1,0:T(8,128)S(1)}, u32[]{:S(2)}, u32[]{:S(2)}) collective-permute-start(f32[128,512]{1,0:T(8,128)S(1)} %leaf_sums.7), channel_id=1, source_target_pairs={{0,3},{1,0},{2,1},{3,2},{4,7},{5,4},{6,5},{7,6},{8,11},{9,8},{10,9... | collective-permute-start | bytes 786440 | tf_op jit(solution)/shard_map/ppermute | solution.py:296
  68.3 3.0 %leaf_sums.4.a_ref = f32[128,512]{1,0:T(8,128)S(1)} custom-call(s32[8,16]{1,0:T(8,128)S(1)} %bitcast.17, f32[3,8192]{1,0:T(4,128)S(1)} %copy-done.2, bf16[4,2048,512]{2,1,0:T(8,128)(2,1)S(1)} %bitcast.10, bf16[4,2048,512]{2,1,0:T(8,128)(2,1)S(1)} %kernel_tiles.4.refs_1_, bf16[4,2048,512]{2,1,0:T(8,128)(2,1)S(1)} %kernel_tiles.5.refs_2_, ...), custom_call_target="tpu_custom_call" | custom-call | flops 4000000000 | bytes 9000000 | tf_op jit(solution)/shard_map/leaf_sums/pallas_call | solution.py:133
  71.3 1.1 collective-permute-done.17.c_ref
  72.4 4.5 %collective-permute-done.18.d_ref = f32[128,512]{1,0:T(8,128)S(1)} collective-permute-done((f32[128,512]{1,0:T(8,128)S(1)}, f32[128,512]{1,0:T(8,128)S(1)}, u32[]{:S(2)}, u32[]{:S(2)}) %collective-permute-start.18) | collective-permute-done | bytes 262176 | tf_op jit(solution)/shard_map/ppermute | solution.py:296
  76.8 6.9 %leaf_node.1 = (f32[128,512]{1,0:T(8,128)S(1)}, f32[128,128]{1,0:T(8,128)S(1)}, f32[128,128]{1,0:T(8,128)S(1)}, f32[128,128]{1,0:T(8,128)S(1)}) custom-call(f32[128,512]{1,0:T(8,128)S(1)} %leaf_sums.4.a_ref, f32[128,512]{1,0:T(8,128)S(1)} %collective-permute-done.16.b_ref, f32[128,512]{1,0:T(8,128)S(1)} %collective-permute-done.17.c_ref, ...), custom_call_target="tpu_custom_call" | custom-call | tf_op jit(solution)/shard_map/leaf_node/pallas_call | solution.py:264
  83.8 1.3 %carry.1 = (f32[512,128]{1,0:T(8,128)}, f32[512,128]{1,0:T(8,128)S(1)}) custom-call(f32[128,512]{1,0:T(8,128)S(1)} %get-tuple-element.24.z_ref, f32[128,128]{1,0:T(8,128)S(1)} %get-tuple-element.25.inv_ref, f32[128,128]{1,0:T(8,128)S(1)} %get-tuple-element.26.proj_ref), custom_call_target="tpu_custom_call" | custom-call | tf_op jit(solution)/shard_map/carry/pallas_call | solution.py:279
  85.1 2.9 %collective-permute-done.19.b_ref = f32[128,128]{1,0:T(8,128)S(1)} collective-permute-done((f32[128,128]{1,0:T(8,128)S(1)}, f32[128,128]{1,0:T(8,128)S(1)}, u32[]{:S(2)}, u32[]{:S(2)}) %collective-permute-start.19) | collective-permute-done | bytes 65568 | tf_op jit(solution)/shard_map/ppermute | solution.py:300
  88.1 6.3 %pair_node.1 = (f32[128,128]{1,0:T(8,128)S(1)}, f32[128,128]{1,0:T(8,128)S(1)}, f32[128,128]{1,0:T(8,128)S(1)}) custom-call(f32[128,128]{1,0:T(8,128)S(1)} %get-tuple-element.28.a_ref, f32[128,128]{1,0:T(8,128)S(1)} %collective-permute-done.19.b_ref), custom_call_target="tpu_custom_call" | custom-call | tf_op jit(solution)/shard_map/pair_node/pallas_call | solution.py:275
  94.4 1.1 %collective-permute-start.20 = (f32[128,128]{1,0:T(8,128)S(1)}, f32[128,128]{1,0:T(8,128)S(1)}, u32[]{:S(2)}, u32[]{:S(2)}) collective-permute-start(f32[128,128]{1,0:T(8,128)S(1)} %get-tuple-element.31.a_ref), channel_id=1, source_target_pairs={{0,2},{1,3},{2,0},{3,1},{4,6},{5,7},{6,4},{7,5},{8,10},{9,11},{10,... | collective-permute-start | bytes 196616 | tf_op jit(solution)/shard_map/ppermute | solution.py:300
  96.5 3.7 %collective-permute-done.20.b_ref = f32[128,128]{1,0:T(8,128)S(1)} collective-permute-done((f32[128,128]{1,0:T(8,128)S(1)}, f32[128,128]{1,0:T(8,128)S(1)}, u32[]{:S(2)}, u32[]{:S(2)}) %collective-permute-start.20) | collective-permute-done | bytes 65568 | tf_op jit(solution)/shard_map/ppermute | solution.py:300
  100.2 7.1 %last_node.1 = f32[512,128]{1,0:T(8,128)} custom-call(f32[128,128]{1,0:T(8,128)S(1)} %get-tuple-element.31.a_ref, f32[128,128]{1,0:T(8,128)S(1)} %collective-permute-done.20.b_ref, f32[512,128]{1,0:T(8,128)S(1)} %carry2.1.z_ref), custom_call_target="tpu_custom_call" | custom-call | tf_op jit(solution)/shard_map/last_node/pallas_call | solution.py:287
  (44 shorter events, 6.5 us)
Async XLA Ops:
  1.4 22.7 %collective-permute-start.5 = (bf16[8,1024]{1,0:T(8,128)(2,1)S(1)}, bf16[8,1024]{1,0:T(8,128)(2,1)S(1)}, u32[]{:S(2)}, u32[]{:S(2)}) collective-permute-start(bf16[8,1024]{1,0:T(8,128)(2,1)S(1)} %get-tuple-element.35), channel_id=1, source_target_pairs={{0,48},{16,32},{32,16},{48,0},{64,112},{80,96},{96,80},{112,64},{1... | collective-permute-start | bytes 49160 | tf_op jit(solution)/shard_map/ppermute | solution.py:304
  2.7 17.6 %collective-permute-start.3 = (bf16[8,1024]{1,0:T(8,128)(2,1)S(1)}, bf16[8,1024]{1,0:T(8,128)(2,1)S(1)}, u32[]{:S(2)}, u32[]{:S(2)}) collective-permute-start(bf16[8,1024]{1,0:T(8,128)(2,1)S(1)} %get-tuple-element.35), channel_id=1, source_target_pairs={{0,16},{16,0},{1,17},{17,1},{2,18},{18,2},{3,19},{19,3},{4,20},{20... | collective-permute-start | bytes 49160 | tf_op jit(solution)/shard_map/ppermute | solution.py:300
  3.4 27.8 %collective-permute-start = (f32[3,2048]{1,0:T(4,128)}, f32[3,2048]{1,0:T(4,128)S(1)}, u32[]{:S(2)}, u32[]{:S(2)}) collective-permute-start(f32[3,2048]{1,0:T(4,128)} %src_ref.1), channel_id=1, source_target_pairs={{0,4},{4,8},{8,12},{12,0},{1,5},{5,9},{9,13},{13,1},{2,6},{6,10},{... | collective-permute-start | bytes 73736 | tf_op jit(solution)/shard_map/ppermute | solution.py:296
  4.9 28.5 %collective-permute-start.2 = (f32[3,2048]{1,0:T(4,128)}, f32[3,2048]{1,0:T(4,128)S(1)}, u32[]{:S(2)}, u32[]{:S(2)}) collective-permute-start(f32[3,2048]{1,0:T(4,128)} %src_ref.1), channel_id=1, source_target_pairs={{0,12},{4,0},{8,4},{12,8},{1,13},{5,1},{9,5},{13,9},{2,14},{6,2},{... | collective-permute-start | bytes 73736 | tf_op jit(solution)/shard_map/ppermute | solution.py:296
  6.7 26.8 %collective-permute-start.1 = (f32[3,2048]{1,0:T(4,128)}, f32[3,2048]{1,0:T(4,128)S(1)}, u32[]{:S(2)}, u32[]{:S(2)}) collective-permute-start(f32[3,2048]{1,0:T(4,128)} %src_ref.1), channel_id=1, source_target_pairs={{0,8},{4,12},{8,0},{12,4},{1,9},{5,13},{9,1},{13,5},{2,10},{6,14},... | collective-permute-start | bytes 73736 | tf_op jit(solution)/shard_map/ppermute | solution.py:296
  8.5 0.9 copy-start.1
  9.4 0.7 copy-start.3
  10.1 0.8 copy-start.5
  10.8 22.6 %copy-start.2 = (f32[3,8192]{1,0:T(4,128)S(1)}, f32[3,8192]{1,0:T(4,128)}, u32[]{:S(2)}) copy-start(f32[3,8192]{1,0:T(4,128)} %tgt_ref.13) | copy-start | bytes 294916
  10.8 22.6 %copy-start.4 = (s32[16,8]{0,1:T(8,128)S(1)}, s32[16,8]{0,1:T(8,128)}, u32[]{:S(2)}) copy-start(s32[16,8]{0,1:T(8,128)} %param.7) | copy-start | bytes 1540
  17.1 3.3 %copy-start = (bf16[4,2048,512]{2,1,0:T(8,128)(2,1)}, bf16[4,2048,512]{2,1,0:T(8,128)(2,1)S(1)}, u32[]{:S(2)}) copy-start(bf16[4,2048,512]{2,1,0:T(8,128)(2,1)S(1)} %kernel_tiles.3.refs_0_) | copy-start | bytes 25165828
  20.3 3.7 %collective-permute-start.4 = (bf16[8,1024]{1,0:T(8,128)(2,1)S(1)}, bf16[8,1024]{1,0:T(8,128)(2,1)S(1)}, u32[]{:S(2)}, u32[]{:S(2)}) collective-permute-start(bf16[8,1024]{1,0:T(8,128)(2,1)S(1)} %get-tuple-element.34), channel_id=1, source_target_pairs={{0,32},{32,0},{64,96},{96,64},{128,160},{160,128},{192,224},{224,1... | collective-permute-start | bytes 49160 | tf_op jit(solution)/shard_map/ppermute | solution.py:300
  24.1 15.6 %collective-permute-start.8 = (bf16[32,1024]{1,0:T(8,128)(2,1)S(1)}, bf16[32,1024]{1,0:T(8,128)(2,1)S(1)}, u32[]{:S(2)}, u32[]{:S(2)}) collective-permute-start(bf16[32,1024]{1,0:T(8,128)(2,1)S(1)} %pad_maximum_fusion.1), channel_id=1, source_target_pairs={{0,192},{32,224},{64,0},{96,32},{128,64},{160,96},{192,128},{224,1... | collective-permute-start | bytes 196616 | tf_op jit(solution)/shard_map/ppermute | solution.py:296
  29.6 10.1 %collective-permute-start.7 = (bf16[32,1024]{1,0:T(8,128)(2,1)S(1)}, bf16[32,1024]{1,0:T(8,128)(2,1)S(1)}, u32[]{:S(2)}, u32[]{:S(2)}) collective-permute-start(bf16[32,1024]{1,0:T(8,128)(2,1)S(1)} %pad_maximum_fusion.1), channel_id=1, source_target_pairs={{0,128},{32,160},{64,192},{96,224},{128,0},{160,32},{192,64},{224,... | collective-permute-start | bytes 196616 | tf_op jit(solution)/shard_map/ppermute | solution.py:296
  31.2 8.5 %collective-permute-start.6 = (bf16[32,1024]{1,0:T(8,128)(2,1)S(1)}, bf16[32,1024]{1,0:T(8,128)(2,1)S(1)}, u32[]{:S(2)}, u32[]{:S(2)}) collective-permute-start(bf16[32,1024]{1,0:T(8,128)(2,1)S(1)} %pad_maximum_fusion.1), channel_id=1, source_target_pairs={{0,64},{32,96},{64,128},{96,160},{128,192},{160,224},{192,0},{224,... | collective-permute-start | bytes 196616 | tf_op jit(solution)/shard_map/ppermute | solution.py:296
  39.7 14.2 %slice-start = ((s8[8388608]{0:T(1024)(128)(4,1)}), s8[4194304]{0:T(1024)(128)(4,1)S(1)}, s32[]{:S(2)}) async-start(s8[8388608]{0:T(1024)(128)(4,1)} %bitcast.9), calls=%async_computation | async-start | bytes 8388608
  39.8 14.1 %slice-start.1 = ((s8[8388608]{0:T(1024)(128)(4,1)}), s8[4194304]{0:T(1024)(128)(4,1)S(1)}, s32[]{:S(2)}) async-start(s8[8388608]{0:T(1024)(128)(4,1)} %bitcast.9), calls=%async_computation.1 | async-start | bytes 8388608
  39.8 10.2 %collective-permute-start.11 = (bf16[4,32,1024]{2,1,0:T(8,128)(2,1)S(1)}, bf16[4,32,1024]{2,1,0:T(8,128)(2,1)S(1)}, u32[]{:S(2)}, u32[]{:S(2)}) collective-permute-start(bf16[4,32,1024]{2,1,0:T(8,128)(2,1)S(1)} %pad_maximum_fusion.refs_4_), channel_id=1, source_target_pairs={{0,8},{4,12},{8,0},{12,4},{1,9},{5,13},{9,1},{13,5},{2,10},{6,14},... | collective-permute-start | bytes 786440 | tf_op jit(solution)/shard_map/ppermute | solution.py:296
  41.6 9.3 %collective-permute-start.10 = (bf16[4,32,1024]{2,1,0:T(8,128)(2,1)S(1)}, bf16[4,32,1024]{2,1,0:T(8,128)(2,1)S(1)}, u32[]{:S(2)}, u32[]{:S(2)}) collective-permute-start(bf16[4,32,1024]{2,1,0:T(8,128)(2,1)S(1)} %pad_maximum_fusion.refs_4_), channel_id=1, source_target_pairs={{0,12},{4,0},{8,4},{12,8},{1,13},{5,1},{9,5},{13,9},{2,14},{6,2},{... | collective-permute-start | bytes 786440 | tf_op jit(solution)/shard_map/ppermute | solution.py:296
  43.2 9.2 %collective-permute-start.9 = (bf16[4,32,1024]{2,1,0:T(8,128)(2,1)S(1)}, bf16[4,32,1024]{2,1,0:T(8,128)(2,1)S(1)}, u32[]{:S(2)}, u32[]{:S(2)}) collective-permute-start(bf16[4,32,1024]{2,1,0:T(8,128)(2,1)S(1)} %pad_maximum_fusion.refs_4_), channel_id=1, source_target_pairs={{0,4},{4,8},{8,12},{12,0},{1,5},{5,9},{9,13},{13,1},{2,6},{6,10},{... | collective-permute-start | bytes 786440 | tf_op jit(solution)/shard_map/ppermute | solution.py:296
  49.8 2.5 %collective-permute-start.12 = (bf16[4,32,1024]{2,1,0:T(8,128)(2,1)S(1)}, bf16[4,32,1024]{2,1,0:T(8,128)(2,1)S(1)}, u32[]{:S(2)}, u32[]{:S(2)}) collective-permute-start(bf16[4,32,1024]{2,1,0:T(8,128)(2,1)S(1)} %pad_maximum_fusion.refs_4_), channel_id=1, source_target_pairs={{0,16},{16,0},{1,17},{17,1},{2,18},{18,2},{3,19},{19,3},{4,20},{20... | collective-permute-start | bytes 786440 | tf_op jit(solution)/shard_map/ppermute | solution.py:300
  50.0 2.4 %collective-permute-start.15 = (bf16[4,32,1024]{2,1,0:T(8,128)(2,1)S(1)}, bf16[4,32,1024]{2,1,0:T(8,128)(2,1)S(1)}, u32[]{:S(2)}, u32[]{:S(2)}) collective-permute-start(bf16[4,32,1024]{2,1,0:T(8,128)(2,1)S(1)} %collective-permute-done.11.refs_7_), channel_id=1, source_target_pairs={{0,16},{16,0},{1,17},{17,1},{2,18},{18,2},{3,19},{19,3},{4,20},{20... | collective-permute-start | bytes 786440 | tf_op jit(solution)/shard_map/ppermute | solution.py:300
  50.8 1.5 %collective-permute-start.14 = (bf16[4,32,1024]{2,1,0:T(8,128)(2,1)S(1)}, bf16[4,32,1024]{2,1,0:T(8,128)(2,1)S(1)}, u32[]{:S(2)}, u32[]{:S(2)}) collective-permute-start(bf16[4,32,1024]{2,1,0:T(8,128)(2,1)S(1)} %collective-permute-done.10.refs_6_), channel_id=1, source_target_pairs={{0,16},{16,0},{1,17},{17,1},{2,18},{18,2},{3,19},{19,3},{4,20},{20... | collective-permute-start | bytes 786440 | tf_op jit(solution)/shard_map/ppermute | solution.py:300
  52.4 1.5 %collective-permute-start.13 = (bf16[4,32,1024]{2,1,0:T(8,128)(2,1)S(1)}, bf16[4,32,1024]{2,1,0:T(8,128)(2,1)S(1)}, u32[]{:S(2)}, u32[]{:S(2)}) collective-permute-start(bf16[4,32,1024]{2,1,0:T(8,128)(2,1)S(1)} %collective-permute-done.9.refs_5_), channel_id=1, source_target_pairs={{0,16},{16,0},{1,17},{17,1},{2,18},{18,2},{3,19},{19,3},{4,20},{20... | collective-permute-start | bytes 786440 | tf_op jit(solution)/shard_map/ppermute | solution.py:300
  56.9 14.4 %collective-permute-start.16 = (f32[128,512]{1,0:T(8,128)S(1)}, f32[128,512]{1,0:T(8,128)S(1)}, u32[]{:S(2)}, u32[]{:S(2)}) collective-permute-start(f32[128,512]{1,0:T(8,128)S(1)} %leaf_sums.5), channel_id=1, source_target_pairs={{0,1},{1,2},{2,3},{3,0},{4,5},{5,6},{6,7},{7,4},{8,9},{9,10},{10,1... | collective-permute-start | bytes 786440 | tf_op jit(solution)/shard_map/ppermute | solution.py:296
  61.6 10.8 %collective-permute-start.17 = (f32[128,512]{1,0:T(8,128)S(1)}, f32[128,512]{1,0:T(8,128)S(1)}, u32[]{:S(2)}, u32[]{:S(2)}) collective-permute-start(f32[128,512]{1,0:T(8,128)S(1)} %leaf_sums.6), channel_id=1, source_target_pairs={{0,2},{1,3},{2,0},{3,1},{4,6},{5,7},{6,4},{7,5},{8,10},{9,11},{10,... | collective-permute-start | bytes 786440 | tf_op jit(solution)/shard_map/ppermute | solution.py:296
  65.6 11.2 %collective-permute-start.18 = (f32[128,512]{1,0:T(8,128)S(1)}, f32[128,512]{1,0:T(8,128)S(1)}, u32[]{:S(2)}, u32[]{:S(2)}) collective-permute-start(f32[128,512]{1,0:T(8,128)S(1)} %leaf_sums.7), channel_id=1, source_target_pairs={{0,3},{1,0},{2,1},{3,2},{4,7},{5,4},{6,5},{7,6},{8,11},{9,8},{10,9... | collective-permute-start | bytes 786440 | tf_op jit(solution)/shard_map/ppermute | solution.py:296
  83.7 4.4 %collective-permute-start.19 = (f32[128,128]{1,0:T(8,128)S(1)}, f32[128,128]{1,0:T(8,128)S(1)}, u32[]{:S(2)}, u32[]{:S(2)}) collective-permute-start(f32[128,128]{1,0:T(8,128)S(1)} %get-tuple-element.28.a_ref), channel_id=1, source_target_pairs={{0,1},{1,0},{2,3},{3,2},{4,5},{5,4},{6,7},{7,6},{8,9},{9,8},{10,11... | collective-permute-start | bytes 196616 | tf_op jit(solution)/shard_map/ppermute | solution.py:300
  94.4 5.9 %collective-permute-start.20 = (f32[128,128]{1,0:T(8,128)S(1)}, f32[128,128]{1,0:T(8,128)S(1)}, u32[]{:S(2)}, u32[]{:S(2)}) collective-permute-start(f32[128,128]{1,0:T(8,128)S(1)} %get-tuple-element.31.a_ref), channel_id=1, source_target_pairs={{0,2},{1,3},{2,0},{3,1},{4,6},{5,7},{6,4},{7,5},{8,10},{9,11},{10,... | collective-permute-start | bytes 196616 | tf_op jit(solution)/shard_map/ppermute | solution.py:300
